TPU v7x, 1024 devices: a whole 8x8x8 slice. The times are simulated.
1024 devices in a mesh: face: 32 (over z_lo, y, core), tile: 32 (over x, z_hi).
Axes of the slice: x: 8, y: 8, z: 8 (z_hi: 4, z_lo: 2; z = z_hi * 2 + z_lo), core: 2. Of those that a mesh axis runs over, the one named last changes fastest.
Arguments:
- adjoint_end: float32 [2, 36, 512, 4096], P(None, None, 'face', 'tile'), may hold values from -6 to 6
- stored_rows: bfloat16 [32, 3072, 2, 36, 128], P('face', 'tile'), may hold values from -2.5 to 2.5
- stored_owner: int32 [32, 3072], P('face', 'tile'), may hold values from 0 to 31, as said below
- stored_unit: int32 [32, 3072], P('face', 'tile'), may hold values from 0 to 47
- stored_valid: int32 [32, 3072], P('face', 'tile'), may hold values from 0 to 1
- edge_match: int32 [32, 32], P('face', 'tile'), may hold values from 0 to 31, as said below
- edge_turn: int32 [32, 32], P('face', 'tile'), may hold values from 0 to 1
Outputs:
- adjoint_start: float32 [2, 36, 512, 4096], P(None, None, 'face', 'tile')
Inputs may be any that keep to these rules, and one draw needn't show every extreme that they name: `stored_owner`: in each face row the valid slots of all holders name every unit of every owner exactly once; one holder has at most 3 valid slots for one owner, and every owner's own holder has exactly 3 for it. For each tile index, edge_match over the face rows is a permutation.
All inputs are finite; a program needn't handle non-finite values.
Results may differ from a plain program's by a relative error of at most 0.0003.
Values may be sent and summed in bfloat16 or wider, within the bound.
No kernel may reach another device: no remote copies, remote signals or barrier semaphores. Data moves between devices by JAX's collectives and lax.ppermute only.
A program may use at most 32 MiB of HBM per device.

v0:
```python
import jax
import jax.numpy as jnp
from jax import lax
from jax.sharding import PartitionSpec as P

STEPS = 3


courant = 0.2


def from_behind(block, axis, distance):
    devices = range(lax.axis_size(axis))
    route = [((i - distance) % len(devices), i) for i in devices]
    return lax.ppermute(block, axis, route)


def padded_2(cells, sides, width):
    for axis, dim in sides:
        count = lax.axis_size(axis)
        head = lax.slice_in_dim(cells, 0, width, axis=dim)
        tail = lax.slice_in_dim(cells, cells.shape[dim] - width, cells.shape[dim], axis=dim)
        cells = jnp.concatenate(
            [
                lax.ppermute(tail, axis, [(i, (i + 1) % count) for i in range(count)]),
                cells,
                lax.ppermute(head, axis, [((i + 1) % count, i) for i in range(count)]),
            ],
            axis=dim,
        )
    return cells


def flipped(values, turned):
    return jnp.where(turned == 1, jnp.flip(values, -1), values)


def adjoint_update(
    adjoint,
    north_values,
    south_values,
    western,
    eastern,
    wind_west,
    wind_east,
    wind_north,
    wind_south,
):
    result = adjoint + courant * jnp.minimum(wind_west, 0.0) * (adjoint - western)
    result = result + courant * jnp.maximum(wind_east, 0.0) * (eastern - adjoint)
    result = result + courant * jnp.minimum(wind_north, 0.0) * (adjoint - north_values)
    result = result + courant * jnp.maximum(wind_south, 0.0) * (south_values - adjoint)
    return result


def shards(
    adjoint_end, stored_rows, stored_owner, stored_unit, stored_valid, edge_match, edge_turn
):
    tile_count = lax.axis_size("tile")
    face_count = lax.axis_size("face")
    held_rows = stored_rows[0]
    slot_count = held_rows.shape[0]
    capacity = slot_count // tile_count
    levels = adjoint_end.shape[1]
    row_count = adjoint_end.shape[2]
    columns = adjoint_end.shape[3]
    unit_count = STEPS * row_count
    owner_tile = stored_owner[0]
    live_slot = stored_valid[0]
    unit_index = stored_unit[0]
    member = (
        (owner_tile[:, None] == jnp.arange(tile_count, dtype=jnp.int32)[None, :])
        & (live_slot[:, None] == 1)
    ).astype(jnp.int32)
    earlier = jnp.cumsum(member, axis=0) - member
    within = jnp.sum(earlier * member, axis=1)
    target = jnp.where(live_slot == 1, owner_tile * capacity + within, -1)
    placing = jnp.arange(slot_count, dtype=jnp.int32)[:, None] == target[None, :]
    outgoing = jnp.dot(
        placing.astype(jnp.bfloat16),
        held_rows.reshape(slot_count, -1),
        preferred_element_type=jnp.float32,
    )
    outgoing = outgoing.astype(jnp.bfloat16).reshape(held_rows.shape)
    labels = jnp.sum(placing.astype(jnp.int32) * (unit_index + 1)[None, :], axis=1) - 1
    arrived, arrived_unit = (
        lax.all_to_all(outgoing, "tile", split_axis=0, concat_axis=0, tiled=True),
        lax.all_to_all(labels, "tile", split_axis=0, concat_axis=0, tiled=True),
    )
    choose = (jnp.arange(unit_count, dtype=jnp.int32)[:, None] == arrived_unit[None, :]).astype(
        jnp.bfloat16
    )
    face_winds = jnp.dot(
        choose, arrived.reshape(arrived.shape[0], -1), preferred_element_type=jnp.float32
    )
    face_winds = face_winds.astype(jnp.bfloat16).reshape(STEPS, row_count, 2, levels, columns)
    face_winds = jnp.transpose(face_winds, (0, 2, 3, 1, 4))
    east_column = from_behind(face_winds[:, 0, :, :, 0], "tile", -1)
    face_here = lax.axis_index("face")
    partner = edge_match[0, 0]
    turn_here = edge_turn[0, 0]
    face_ids = jnp.arange(face_count, dtype=jnp.int32)
    adjoint = adjoint_end
    for time_step in reversed(range(STEPS)):
        wind_west = face_winds[time_step, 0].astype(jnp.float32)
        wind_north = face_winds[time_step, 1].astype(jnp.float32)
        padded = padded_2(adjoint, (("tile", 3),), 1)
        western = padded[..., :-2]
        eastern = padded[..., 2:]
        wind_east = jnp.concatenate(
            [wind_west[:, :, 1:], east_column[time_step][:, :, None].astype(jnp.float32)], axis=2
        )
        edge_rows = jnp.concatenate(
            [adjoint[:, :, 0], adjoint[:, :, row_count - 1]], axis=0
        ).astype(jnp.bfloat16)
        package = jnp.concatenate([edge_rows, face_winds[time_step, 1, :, 0][None]], axis=0)
        strips, all_match, all_turn = (
            lax.all_gather(package[None], "face", axis=0, tiled=True),
            lax.all_gather(edge_match, "face", axis=0, tiled=True),
            lax.all_gather(edge_turn, "face", axis=0, tiled=True),
        )
        lower_face = jnp.sum(jnp.where(all_match[:, 0] == face_here, face_ids, 0))
        lower_turn = all_turn[lower_face, 0]
        south_edge = flipped(strips[lower_face, 4], lower_turn)
        upper_edge = flipped(strips[partner, 2:4], turn_here).astype(jnp.float32)
        lower_edge = flipped(strips[lower_face, 0:2], lower_turn).astype(jnp.float32)
        north_values = jnp.concatenate([upper_edge[:, :, None], adjoint[:, :, :-1]], axis=2)
        south_values = jnp.concatenate([adjoint[:, :, 1:], lower_edge[:, :, None]], axis=2)
        wind_south = jnp.concatenate(
            [wind_north[:, 1:], south_edge[:, None].astype(jnp.float32)], axis=1
        )
        adjoint = adjoint_update(
            adjoint,
            north_values,
            south_values,
            western,
            eastern,
            wind_west,
            wind_east,
            wind_north,
            wind_south,
        )
    return adjoint


def solution(mesh):
    placed = (
        P(None, None, "face", "tile"),
        P("face", "tile", None, None, None),
        P("face", "tile"),
        P("face", "tile"),
        P("face", "tile"),
        P("face", "tile"),
        P("face", "tile"),
    )
    return jax.shard_map(
        shards, mesh=mesh, in_specs=placed, out_specs=P(None, None, "face", "tile"), check_vma=False
    )
```

profile of v0, /device:TPU:1, one launch (start us, length us, event | category | flops | bytes accessed | tf_op | source)
XLA Modules:
  0.0 359.1 jit_solution(1106031793165310526)
XLA Ops:
  10.5 21.6 %all-to-all-start = ((s32[32,3,1]{1,2,0:T(1,128)}), s32[32,3,1]{1,2,0:T(1,128)S(1)}, u32[]{:S(2)}, u32[]{:S(2)}) async-start(s32[32,3,1]{1,2,0:T(1,128)} %bitcast.5), calls=%async_computation | async-start | bytes 32768 | tf_op jit(solution)/shard_map/all_to_all | solution.py:88
  32.1 1.8 copy.207
  33.9 2.3 reshape_squeeze.3
  36.2 3.3 convolution_convert_fusion
  39.5 2.8 reshape.243
  42.3 2.6 copy.208
  44.9 11.9 %all-to-all-start.1 = ((bf16[96,2,36,128]{3,1,2,0:T(2,128)(2,1)}), bf16[96,2,36,128]{3,1,2,0:T(2,128)(2,1)}, u32[]{:S(2)}, u32[]{:S(2)}) async-start(bf16[96,2,36,128]{3,1,2,0:T(2,128)(2,1)} %copy.208), calls=%async_computation.1 | async-start | bytes 3538944 | tf_op jit(solution)/shard_map/all_to_all | solution.py:87
  59.2 38.8 %all-to-all-done.1 = bf16[96,2,36,128]{3,1,2,0:T(2,128)(2,1)} async-done(((bf16[96,2,36,128]{3,1,2,0:T(2,128)(2,1)}), bf16[96,2,36,128]{3,1,2,0:T(2,128)(2,1)}, u32[]{:S(2)}, u32[]{:S(2)}) %all-to-all-start.1) | async-done | bytes 1769504 | tf_op jit(solution)/shard_map/all_to_all | solution.py:87
  99.9 2.3 reshape.244
  102.2 1.9 convolution_convert_fusion.1
  105.9 3.9 %collective-permute-start = (f32[2,36,16,1]{1,2,3,0:T(8,128)S(1)}, f32[2,36,16,1]{1,2,3,0:T(8,128)S(1)}, u32[]{:S(2)}, u32[]{:S(2)}) collective-permute-start(f32[2,36,16,1]{1,2,3,0:T(8,128)S(1)} %copy.254), channel_id=1, source_target_pairs={{0,1},{1,2},{2,3},{3,4},{4,5},{5,6},{6,7},{7,8},{8,9},{9,10},{10,1... | collective-permute-start | bytes 13832 | tf_op jit(solution)/shard_map/ppermute | solution.py:25
  110.1 5.7 %collective-permute-start.2 = (f32[2,36,16,1]{1,2,3,0:T(8,128)S(1)}, f32[2,36,16,1]{1,2,3,0:T(8,128)S(1)}, u32[]{:S(2)}, u32[]{:S(2)}) collective-permute-start(f32[2,36,16,1]{1,2,3,0:T(8,128)S(1)} %copy.255), channel_id=1, source_target_pairs={{1,0},{2,1},{3,2},{4,3},{5,4},{6,5},{7,6},{8,7},{9,8},{10,9},{11,1... | collective-permute-start | bytes 13832 | tf_op jit(solution)/shard_map/ppermute | solution.py:27
  120.3 21.2 %all-reduce.2 = (s32[32]{0:T(128)S(1)}, s32[32]{0:T(128)S(1)}) all-reduce(s32[32]{0:T(128)S(1)} %bitcast_dynamic-update-slice_fusion, s32[32]{0:T(128)S(1)} %bitcast_dynamic-update-slice_fusion.1), channel_id=1, replica_groups=mesh['face'=32,'tile'=32] {'face'}, use_global_device_ids=true, to_apply=%add.1 | all-reduce | flops 64 | bytes 512
  147.8 2.1 collective-permute-start.1
  154.4 25.4 %all-gather.7.cloned.1.call-done = bf16[160,36,128]{2,1,0:T(8,128)(2,1)} async-done(((bf16[5,36,128]{2,1,0:T(8,128)(2,1)}), bf16[160,36,128]{2,1,0:T(8,128)(2,1)}) %all-gather.7.cloned.1.call-update) | async-done | bytes 1474576 | tf_op jit(solution)/shard_map/all_gather | solution.py:118
  183.5 4.0 %fusion.65 = (bf16[2,36,16,128]{3,0,1,2:T(2,128)(2,1)S(1)}, f32[2,36,16,128]{3,0,1,2:T(2,128)S(1)}) fusion(f32[2,36,16,128]{3,0,1,2:T(2,128)S(1)} %copy.215, f32[2,36,1,128]{3,0,1,2:T(2,128)S(1)} %fusion.52, f32[2,36,15,128]{3,0,1,2:T(2,128)} %get-tuple-element.43, f32[36,16,128]{2,0,1:T(8,128)S(1)} %fusion.31, ...), kind=kLoop, calls=%fused_computation.150 | loop fusion | flops 2506752 | bytes 3843072 | tf_op jit(solution)/shard_map/convert.29
  193.3 4.8 %collective-permute-start.3 = (f32[2,36,16,1]{1,2,3,0:T(8,128)S(1)}, f32[2,36,16,1]{1,2,3,0:T(8,128)S(1)}, u32[]{:S(2)}, u32[]{:S(2)}) collective-permute-start(f32[2,36,16,1]{1,2,3,0:T(8,128)S(1)} %copy.232), channel_id=1, source_target_pairs={{0,1},{1,2},{2,3},{3,4},{4,5},{5,6},{6,7},{7,8},{8,9},{9,10},{10,1... | collective-permute-start | bytes 13832 | tf_op jit(solution)/shard_map/ppermute | solution.py:25
  198.4 5.9 %collective-permute-start.4 = (f32[2,36,16,1]{1,2,3,0:T(8,128)S(1)}, f32[2,36,16,1]{1,2,3,0:T(8,128)S(1)}, u32[]{:S(2)}, u32[]{:S(2)}) collective-permute-start(f32[2,36,16,1]{1,2,3,0:T(8,128)S(1)} %copy.235), channel_id=1, source_target_pairs={{1,0},{2,1},{3,2},{4,3},{5,4},{6,5},{7,6},{8,7},{9,8},{10,9},{11,1... | collective-permute-start | bytes 13832 | tf_op jit(solution)/shard_map/ppermute | solution.py:27
  205.5 52.7 %all-gather.9.cloned.1.call-done = bf16[160,36,128]{2,1,0:T(8,128)(2,1)} async-done(((bf16[5,36,128]{2,1,0:T(8,128)(2,1)}), bf16[160,36,128]{2,1,0:T(8,128)(2,1)}) %all-gather.9.cloned.1.call-update) | async-done | bytes 1474576 | tf_op jit(solution)/shard_map/all_gather | solution.py:118
  261.0 3.8 %fusion.63 = (bf16[2,36,16,128]{3,0,1,2:T(2,128)(2,1)S(1)}, f32[2,36,16,128]{3,0,1,2:T(2,128)S(1)}) fusion(f32[2,36,16,128]{3,0,1,2:T(2,128)S(1)} %get-tuple-element.10, f32[2,36,1,128]{3,0,1,2:T(2,128)S(1)} %fusion.54, f32[2,36,15,128]{3,0,1,2:T(2,128)S(1)} %get-tuple-element.39, f32[36,16,128]{2,0,1:T(8,128)S(1)} %fusion.33, ...), kind=kLoop, calls=%fused_computation.149 | loop fusion | flops 2506752 | bytes 3843072 | tf_op jit(solution)/shard_map/convert.23
  269.7 4.7 %collective-permute-start.5 = (f32[2,36,16,1]{1,2,3,0:T(8,128)S(1)}, f32[2,36,16,1]{1,2,3,0:T(8,128)S(1)}, u32[]{:S(2)}, u32[]{:S(2)}) collective-permute-start(f32[2,36,16,1]{1,2,3,0:T(8,128)S(1)} %copy.243), channel_id=1, source_target_pairs={{0,1},{1,2},{2,3},{3,4},{4,5},{5,6},{6,7},{7,8},{8,9},{9,10},{10,1... | collective-permute-start | bytes 13832 | tf_op jit(solution)/shard_map/ppermute | solution.py:25
  274.8 6.0 %collective-permute-start.6 = (f32[2,36,16,1]{1,2,3,0:T(8,128)S(1)}, f32[2,36,16,1]{1,2,3,0:T(8,128)}, u32[]{:S(2)}, u32[]{:S(2)}) collective-permute-start(f32[2,36,16,1]{1,2,3,0:T(8,128)S(1)} %copy.246), channel_id=1, source_target_pairs={{1,0},{2,1},{3,2},{4,3},{5,4},{6,5},{7,6},{8,7},{9,8},{10,9},{11,1... | collective-permute-start | bytes 13832 | tf_op jit(solution)/shard_map/ppermute | solution.py:27
  282.7 52.9 %all-gather.11.cloned.1.call-done = bf16[160,36,128]{2,1,0:T(8,128)(2,1)} async-done(((bf16[5,36,128]{2,1,0:T(8,128)(2,1)}), bf16[160,36,128]{2,1,0:T(8,128)(2,1)}) %all-gather.11.cloned.1.call-update) | async-done | bytes 1474576 | tf_op jit(solution)/shard_map/all_gather | solution.py:118
  348.3 3.4 fusion.4
  (127 shorter events, 55.6 us)
Async XLA Ops:
  10.5 34.4 %all-to-all-start = ((s32[32,3,1]{1,2,0:T(1,128)}), s32[32,3,1]{1,2,0:T(1,128)S(1)}, u32[]{:S(2)}, u32[]{:S(2)}) async-start(s32[32,3,1]{1,2,0:T(1,128)} %bitcast.5), calls=%async_computation | async-start | bytes 32768 | tf_op jit(solution)/shard_map/all_to_all | solution.py:88
  44.9 11.9 %copy-start = (f32[2,36,16,128]{3,2,1,0:T(8,128)S(1)}, f32[2,36,16,128]{3,2,1,0:T(8,128)}, u32[]{:S(2)}) copy-start(f32[2,36,16,128]{3,2,1,0:T(8,128)} %param.7) | copy-start | bytes 1769476
  44.9 53.2 %all-to-all-start.1 = ((bf16[96,2,36,128]{3,1,2,0:T(2,128)(2,1)}), bf16[96,2,36,128]{3,1,2,0:T(2,128)(2,1)}, u32[]{:S(2)}, u32[]{:S(2)}) async-start(bf16[96,2,36,128]{3,1,2,0:T(2,128)(2,1)} %copy.208), calls=%async_computation.1 | async-start | bytes 3538944 | tf_op jit(solution)/shard_map/all_to_all | solution.py:87
  56.8 123.1 %all-gather.7.cloned.1.call-start = ((), (), s32[]{:S(2)}) async-start(), calls=%async_computation.2 | async-start | bytes 1689600 | tf_op jit(solution)/shard_map/all_gather | solution.py:118
  102.2 2.4 copy-start.3
  102.2 2.4 copy-start.4
  105.3 153.0 %all-gather.9.cloned.1.call-start = ((), (), s32[]{:S(2)}) async-start(), calls=%async_computation.3 | async-start | bytes 1689600 | tf_op jit(solution)/shard_map/all_gather | solution.py:118
  105.9 40.8 %collective-permute-start = (f32[2,36,16,1]{1,2,3,0:T(8,128)S(1)}, f32[2,36,16,1]{1,2,3,0:T(8,128)S(1)}, u32[]{:S(2)}, u32[]{:S(2)}) collective-permute-start(f32[2,36,16,1]{1,2,3,0:T(8,128)S(1)} %copy.254), channel_id=1, source_target_pairs={{0,1},{1,2},{2,3},{3,4},{4,5},{5,6},{6,7},{7,8},{8,9},{9,10},{10,1... | collective-permute-start | bytes 13832 | tf_op jit(solution)/shard_map/ppermute | solution.py:25
  110.1 37.0 %collective-permute-start.2 = (f32[2,36,16,1]{1,2,3,0:T(8,128)S(1)}, f32[2,36,16,1]{1,2,3,0:T(8,128)S(1)}, u32[]{:S(2)}, u32[]{:S(2)}) collective-permute-start(f32[2,36,16,1]{1,2,3,0:T(8,128)S(1)} %copy.255), channel_id=1, source_target_pairs={{1,0},{2,1},{3,2},{4,3},{5,4},{6,5},{7,6},{8,7},{9,8},{10,9},{11,1... | collective-permute-start | bytes 13832 | tf_op jit(solution)/shard_map/ppermute | solution.py:27
  147.8 5.5 %collective-permute-start.1 = (bf16[3,36,16]{1,2,0:T(8,128)(2,1)S(1)}, bf16[3,36,16]{1,2,0:T(8,128)(2,1)S(1)}, u32[]{:S(2)}, u32[]{:S(2)}) collective-permute-start(bf16[3,36,16]{1,2,0:T(8,128)(2,1)S(1)} %slice_reduce_fusion), channel_id=1, source_target_pairs={{1,0},{2,1},{3,2},{4,3},{5,4},{6,5},{7,6},{8,7},{9,8},{10,9},{11,1... | collective-permute-start | bytes 10376 | tf_op jit(solution)/shard_map/ppermute | solution.py:15
  188.2 147.4 %all-gather.11.cloned.1.call-start = ((), (), s32[]{:S(2)}) async-start(), calls=%async_computation.4 | async-start | bytes 1689600 | tf_op jit(solution)/shard_map/all_gather | solution.py:118
  193.3 11.4 %collective-permute-start.3 = (f32[2,36,16,1]{1,2,3,0:T(8,128)S(1)}, f32[2,36,16,1]{1,2,3,0:T(8,128)S(1)}, u32[]{:S(2)}, u32[]{:S(2)}) collective-permute-start(f32[2,36,16,1]{1,2,3,0:T(8,128)S(1)} %copy.232), channel_id=1, source_target_pairs={{0,1},{1,2},{2,3},{3,4},{4,5},{5,6},{6,7},{7,8},{8,9},{9,10},{10,1... | collective-permute-start | bytes 13832 | tf_op jit(solution)/shard_map/ppermute | solution.py:25
  198.4 62.5 %copy-start.2 = (f32[36,15,128]{2,0,1:T(8,128)S(1)}, f32[36,15,128]{2,0,1:T(8,128)}, u32[]{:S(2)}) copy-start(f32[36,15,128]{2,0,1:T(8,128)} %slice.205) | copy-start | bytes 829444
  198.4 6.8 %collective-permute-start.4 = (f32[2,36,16,1]{1,2,3,0:T(8,128)S(1)}, f32[2,36,16,1]{1,2,3,0:T(8,128)S(1)}, u32[]{:S(2)}, u32[]{:S(2)}) collective-permute-start(f32[2,36,16,1]{1,2,3,0:T(8,128)S(1)} %copy.235), channel_id=1, source_target_pairs={{1,0},{2,1},{3,2},{4,3},{5,4},{6,5},{7,6},{8,7},{9,8},{10,9},{11,1... | collective-permute-start | bytes 13832 | tf_op jit(solution)/shard_map/ppermute | solution.py:27
  269.7 11.4 %collective-permute-start.5 = (f32[2,36,16,1]{1,2,3,0:T(8,128)S(1)}, f32[2,36,16,1]{1,2,3,0:T(8,128)S(1)}, u32[]{:S(2)}, u32[]{:S(2)}) collective-permute-start(f32[2,36,16,1]{1,2,3,0:T(8,128)S(1)} %copy.243), channel_id=1, source_target_pairs={{0,1},{1,2},{2,3},{3,4},{4,5},{5,6},{6,7},{7,8},{8,9},{9,10},{10,1... | collective-permute-start | bytes 13832 | tf_op jit(solution)/shard_map/ppermute | solution.py:25
  274.8 73.5 %copy-start.1 = (f32[36,16,128]{2,0,1:T(8,128)S(1)}, f32[36,16,128]{2,0,1:T(8,128)}, u32[]{:S(2)}) copy-start(f32[36,16,128]{2,0,1:T(8,128)} %get-tuple-element.17) | copy-start | bytes 884740
  274.8 6.9 %collective-permute-start.6 = (f32[2,36,16,1]{1,2,3,0:T(8,128)S(1)}, f32[2,36,16,1]{1,2,3,0:T(8,128)}, u32[]{:S(2)}, u32[]{:S(2)}) collective-permute-start(f32[2,36,16,1]{1,2,3,0:T(8,128)S(1)} %copy.246), channel_id=1, source_target_pairs={{1,0},{2,1},{3,2},{4,3},{5,4},{6,5},{7,6},{8,7},{9,8},{10,9},{11,1... | collective-permute-start | bytes 13832 | tf_op jit(solution)/shard_map/ppermute | solution.py:27
Sparse Core Ops, SparseCore 0:
  105.4 74.3 all-gather.6
  188.4 69.8 all-gather.8
  265.6 70.0 all-gather.10
where the time goes:
time: 361 us; the launch traced here: 359 us
  waiting for transfers between devices  170 us (47%)
  starting transfers between devices  66.8 us (19%)
  local copies, waits for them, and re-layouts  51.3 us (14%)
  other arithmetic  26.6 us (7%)
  blocking collectives  21.2 us (6%)
  between operations  17.7 us (5%)
  matrix products  5.17 us (1%)
    all_gather x3, waiting for transfers between devices, shards(): lax.all_gather(package[None], 'face', axis=0, tiled=True)  131 us
    all_to_all x1, waiting for transfers between devices, shards(): lax.all_to_all(outgoing, 'tile', split_axis=0, concat_axis=0, tiled=True)  38.8 us
    all_to_all x1, starting transfers between devices, shards(): lax.all_to_all(labels, 'tile', split_axis=0, concat_axis=0, tiled=True)  21.6 us
    unnamed x1, blocking collectives  21.2 us
    ppermute x3, starting transfers between devices, padded_2(): lax.ppermute(head, axis, [((i + 1) % count, i) for i in range(count)])  17.7 us
    ppermute x3, starting transfers between devices, padded_2(): lax.ppermute(tail, axis, [(i, (i + 1) % count) for i in range(count)])  13.4 us
    all_to_all x1, starting transfers between devices, shards(): lax.all_to_all(outgoing, 'tile', split_axis=0, concat_axis=0, tiled=True)  11.9 us
    another operation x2, other arithmetic  7.72 us
  transfers between devices with their start and end apart: 12, of which 6 were waited for; matrix products, arithmetic and copies ran while one was open for 11% of the time, Pallas kernels for 0%

commit v1 on v0

v1 whole, which is shorter than its diff:
```python
import functools

import jax
import jax.numpy as jnp
from jax import lax
from jax.experimental import pallas as pl
from jax.experimental.pallas import tpu as pltpu
from jax.sharding import Mesh
from jax.sharding import PartitionSpec as P

STEPS = 3
COURANT = 0.2
PAD = 40
LABEL, LABEL_EAST = 64, 65
INTERPRET = False

VM = pl.BlockSpec(memory_space=pltpu.VMEM)
SM = pl.BlockSpec(memory_space=pltpu.SMEM)
F32, BF16 = jnp.float32, jnp.bfloat16


def call(kernel, out_shape, in_specs, out_specs, scratch=(), flops=1 << 20, moved=1 << 20):
    return pl.pallas_call(
        kernel,
        out_shape=out_shape,
        in_specs=in_specs,
        out_specs=out_specs,
        scratch_shapes=list(scratch),
        compiler_params=pltpu.CompilerParams(vmem_limit_bytes=40 << 20),
        cost_estimate=pl.CostEstimate(flops=flops, bytes_accessed=moved, transcendentals=0),
        interpret=INTERPRET,
    )


def lanes(rows, width):
    return lax.broadcasted_iota(jnp.int32, (rows, width), 1)


def spread(values, lane, shape):
    return jnp.broadcast_to(values[:, lane : lane + 1], shape)


def pack_kernel(levels, step_unit, owner, unit, valid, rows, out, mini, count, source, label, first, flat):
    slots, width = rows.shape[0], rows.shape[3]
    tiles = mini.shape[0]
    capacity = slots // tiles

    def clear(i, c):
        count[i] = 0
        first[i] = -1
        return c

    lax.fori_loop(0, tiles, clear, 0)

    def blank(i, c):
        source[i] = 0
        label[i] = -1
        return c

    lax.fori_loop(0, slots, blank, 0)

    def place(s, c):
        @pl.when(valid[0, s] == 1)
        def _():
            o, u = owner[0, s], unit[0, s]
            p = o * capacity + count[o]
            source[p] = s
            label[p] = u
            count[o] = count[o] + 1

            @pl.when(u == step_unit)
            def _():
                first[o] = s

        return c

    lax.fori_loop(0, slots, place, 0)

    lane = lanes(levels, width)

    def column(s, held):
        v = rows[s, 0].astype(F32)
        return jnp.where(lane == s, spread(v, 0, v.shape), held)

    held = lax.fori_loop(0, slots, column, jnp.zeros((levels, width), F32), unroll=8)
    flat[...] = jnp.zeros_like(flat)
    flat[0:levels, :] = held
    flat[...] = flat[...].T

    extra_lane = lanes(1, width)
    zeros = jnp.zeros((PAD - levels, width), BF16)

    def fill(p, c):
        s = source[p]
        q = jnp.where(p + capacity >= slots, p + capacity - slots, p + capacity)
        out[p, 0, 0:levels, :] = rows[s, 0]
        out[p, 1, 0:levels, :] = rows[s, 1]
        extra = flat[pl.ds(source[q], 1), :]
        extra = jnp.where(extra_lane == LABEL, label[p].astype(F32), extra)
        extra = jnp.where(extra_lane == LABEL_EAST, label[q].astype(F32), extra)
        out[p, 0, levels:PAD, :] = jnp.broadcast_to(extra, zeros.shape).astype(BF16)
        out[p, 1, levels:PAD, :] = zeros
        return c

    lax.fori_loop(0, slots, fill, 0, unroll=2)

    def fill_mini(o, c):
        s = first[o]
        mini[o, 0:levels, :] = rows[jnp.maximum(s, 0), 1]
        flag = jnp.where(s >= 0, 1.0, 0.0)
        mini[o, levels:PAD, :] = jnp.full(zeros.shape, flag, F32).astype(BF16)
        return c

    lax.fori_loop(0, tiles, fill_mini, 0, unroll=2)


def edges_kernel(levels, row_count, field_stride, adj, turned, item, sides):
    width = adj.shape[1]
    lane = lanes(PAD, width)
    last = jnp.zeros((PAD, width), F32)
    head = jnp.zeros((PAD, width), F32)
    for r in range(row_count):
        for f in range(2):
            for l0 in range(0, levels, 8):
                n = min(8, levels - l0)
                turned[r, f, l0 : l0 + n, :] = adj[pl.ds((f * levels + l0) * row_count + r, n, stride=row_count), :]
            turned[r, f, levels:PAD, :] = jnp.zeros((PAD - levels, width), F32)
            v = turned[r, f]
            q = r * 2 + f
            last = jnp.where(lane == q, spread(v, width - 1, v.shape), last)
            head = jnp.where(lane == q, spread(v, 0, v.shape), head)
            if r == 0:
                item[f] = v.astype(BF16)
            if r == row_count - 1:
                item[2 + f] = v.astype(BF16)
    sides[0] = last
    sides[1] = head


def join_kernel(levels, mini, edge, item):
    holders = mini.shape[0]

    def pick(h, total):
        v = mini[h].astype(F32)
        flag = jnp.broadcast_to(v[levels : levels + 1, :], v.shape)
        return jnp.where(flag > 0.5, v, total)

    wind = lax.fori_loop(0, holders, pick, jnp.zeros(mini.shape[1:], F32), unroll=4)
    item[0] = edge[0]
    item[1] = edge[1]
    item[2] = wind.astype(BF16)
    item[3] = edge[2]
    item[4] = edge[3]


def invert(code, inverse):
    def one(f, c):
        inverse[lax.shift_right_logical(code[0, f], 1)] = f
        return c

    lax.fori_loop(0, code.shape[1], one, 0)


def choose_kernel(sizes, code, where, gathered, out, inverse):
    _, ny, nc = sizes
    invert(code, inverse)
    zl, c = where[0, 0], where[0, 2]
    for y in range(ny):
        dest = (zl * ny + y) * nc + c
        for source, a, b in (
            (inverse[dest], 0, 3),
            (lax.shift_right_logical(code[0, dest], 1), 3, 5),
        ):
            group = (source // (ny * nc)) * nc + source % nc
            for i in range(a, b):
                out[y, i] = gathered[group, i]


def neighbours(sizes, code, where, inverse):
    _, ny, nc = sizes
    invert(code, inverse)
    me = (where[0, 0] * ny + where[0, 1]) * nc + where[0, 2]
    north, south = lax.shift_right_logical(code[0, me], 1), inverse[me]
    return (north // nc) % ny, code[0, me] & 1, (south // nc) % ny, code[0, south] & 1


def oriented(block, turn):
    n, rows, width = block.shape
    i = lax.broadcasted_iota(jnp.int32, (width, width), 0)
    j = lax.broadcasted_iota(jnp.int32, (width, width), 1)
    source = jnp.where(turn == 1, width - 1 - j, j)
    matrix = jnp.where(i == source, 1.0, 0.0).astype(BF16)
    out = jnp.dot(block.reshape(n * rows, width), matrix, preferred_element_type=F32)
    return out.reshape(n, rows, width)


def step_kernel(step, levels, row_count, sizes, *refs):
    opening, closing = step == STEPS - 1, step == 0
    refs = list(refs)
    code, where = refs.pop(0), refs.pop(0)
    if not opening:
        found = refs.pop(0)
    winds, adj, edge, from_west, from_east = (refs.pop(0) for _ in range(5))
    if not opening:
        east_wind = refs.pop(0)
    out = refs.pop(0)
    if not closing:
        item, sides = refs.pop(0), refs.pop(0)
    if opening:
        found_out, east_wind = refs.pop(0), refs.pop(0)
    inverse = refs.pop(0)
    if opening:
        found, sem = refs.pop(0), refs.pop(0)
    width = adj.shape[3]
    slots = winds.shape[0]

    if opening:
        extra = winds[:, 0, PAD - 8 : PAD, :].astype(F32).reshape(slots * 8, width)
        row = lax.broadcasted_iota(jnp.int32, extra.shape, 0)
        ours = (row & 7) == levels - (PAD - 8)
        lane = lanes(slots * 8, width).astype(F32)
        here = ours & (spread(extra, LABEL, extra.shape) == lane)
        there = ours & (spread(extra, LABEL_EAST, extra.shape) == lane)
        slot = lax.shift_right_logical(row, 3).astype(F32)
        index = jnp.sum(jnp.where(here, slot, 0.0), axis=0, keepdims=True)
        found_out[...] = index.astype(jnp.int32)
        copy = pltpu.make_async_copy(found_out, found, sem)
        copy.start()
        columns = lax.dot_general(
            jnp.where(ours, extra, 0.0).astype(BF16),
            jnp.where(there, 1.0, 0.0).astype(BF16),
            (((0,), (0,)), ((), ())),
            preferred_element_type=F32,
        )
        east_wind[...] = columns[0:PAD, :]
        copy.wait()

    y_north, turn_north, y_south, turn_south = neighbours(sizes, code, where, inverse)
    upper = oriented(edge[y_north, 3:5], turn_north)
    lower = oriented(edge[y_south, 0:3], turn_south)

    lane = lanes(PAD, width)
    last = jnp.zeros((PAD, width), F32)
    head = jnp.zeros((PAD, width), F32)
    base = step * row_count
    north_wind = winds[found[0, base], 1].astype(F32)
    for r in range(row_count):
        west_wind = winds[found[0, base + r], 0].astype(F32)
        if r + 1 < row_count:
            south_wind = winds[found[0, base + r + 1], 1].astype(F32)
        else:
            south_wind = lower[2]
        u = base + r
        eastern_wind = jnp.where(
            lane == width - 1, spread(east_wind, u, lane.shape), pltpu.roll(west_wind, width - 1, 1)
        )
        cw = COURANT * jnp.minimum(west_wind, 0.0)
        ce = COURANT * jnp.maximum(eastern_wind, 0.0)
        cn = COURANT * jnp.minimum(north_wind, 0.0)
        cs = COURANT * jnp.maximum(south_wind, 0.0)
        for f in range(2):
            q = r * 2 + f
            a = adj[r, f]
            west = jnp.where(lane == 0, spread(from_west, q, a.shape), pltpu.roll(a, 1, 1))
            east = jnp.where(lane == width - 1, spread(from_east, q, a.shape), pltpu.roll(a, width - 1, 1))
            north = adj[r - 1, f] if r > 0 else upper[f]
            south = adj[r + 1, f] if r + 1 < row_count else lower[f]
            v = a + cw * (a - west)
            v = v + ce * (east - a)
            v = v + cn * (a - north)
            v = v + cs * (south - a)
            if closing:
                for l0 in range(0, levels, 8):
                    n = min(8, levels - l0)
                    out[pl.ds((f * levels + l0) * row_count + r, n, stride=row_count), :] = v[l0 : l0 + n]
            else:
                out[r, f] = v
                last = jnp.where(lane == q, spread(v, width - 1, v.shape), last)
                head = jnp.where(lane == q, spread(v, 0, v.shape), head)
                if r == 0:
                    item[f] = v.astype(BF16)
                if r == row_count - 1:
                    item[3 + f] = v.astype(BF16)
        north_wind = south_wind
    if not closing:
        item[2] = winds[found[0, base - row_count], 1]
        sides[0] = last
        sides[1] = head


def shards(sizes, tile_sizes, adjoint_end, stored_rows, stored_owner, stored_unit, stored_valid, edge_match, edge_turn):
    face, tile, group = ("zl", "y", "c"), ("x", "zh"), ("zl", "c")
    faces = sizes[0] * sizes[1] * sizes[2]
    tiles = tile_sizes[0] * tile_sizes[1]
    levels, row_count, width = adjoint_end.shape[1:]
    slots = stored_rows.shape[1]
    sds = jax.ShapeDtypeStruct

    where = jnp.stack([lax.axis_index(a) for a in face]).astype(jnp.int32).reshape(1, 3)
    code = edge_match * 2 + edge_turn
    code = lax.all_to_all(jnp.broadcast_to(code, (faces, 1)), face, 0, 0, tiled=True).reshape(1, faces)

    payload, mini = call(
        functools.partial(pack_kernel, levels, (STEPS - 1) * row_count),
        (sds((slots, 2, PAD, width), BF16), sds((tiles, PAD, width), BF16)),
        [SM, SM, SM, VM],
        (VM, VM),
        [
            pltpu.SMEM((tiles,), jnp.int32),
            pltpu.SMEM((slots,), jnp.int32),
            pltpu.SMEM((slots,), jnp.int32),
            pltpu.SMEM((tiles,), jnp.int32),
            pltpu.VMEM((width, width), F32),
        ],
    )(stored_owner, stored_unit, stored_valid, stored_rows[0])
    mini = lax.all_to_all(mini, tile, 0, 0, tiled=True)
    winds = lax.all_to_all(payload, tile, 0, 0, tiled=True)

    turned, edge, sides = call(
        functools.partial(edges_kernel, levels, row_count, levels),
        (sds((row_count, 2, PAD, width), F32), sds((4, PAD, width), BF16), sds((2, PAD, width), F32)),
        [VM],
        (VM, VM, VM),
    )(adjoint_end.reshape(2 * levels * row_count, width))
    item = call(
        functools.partial(join_kernel, levels), sds((5, PAD, width), BF16), [VM, VM], VM
    )(mini, edge)

    def to_sides(sides):
        ahead = [(i, (i + 1) % tiles) for i in range(tiles)]
        back = [((i + 1) % tiles, i) for i in range(tiles)]
        return lax.ppermute(sides[0], tile, ahead), lax.ppermute(sides[1], tile, back)

    def exchange(item):
        gathered = lax.all_gather(item, group, axis=0, tiled=False)
        chosen = call(
            functools.partial(choose_kernel, sizes),
            sds((sizes[1],) + item.shape, BF16),
            [SM, SM, VM],
            VM,
            [pltpu.SMEM((faces,), jnp.int32)],
        )(code, where, gathered)
        return lax.all_to_all(chosen, "y", 0, 0, tiled=True)

    found = east_wind = None
    adj = turned
    for step in reversed(range(STEPS)):
        opening, closing = step == STEPS - 1, step == 0
        from_west, from_east = to_sides(sides)
        edge = exchange(item)
        if closing:
            shape, spec = [sds((2 * levels * row_count, width), F32)], [VM]
        else:
            shape = [sds(turned.shape, F32), sds((5, PAD, width), BF16), sds((2, PAD, width), F32)]
            spec = [VM] * 3
        scratch = [pltpu.SMEM((faces,), jnp.int32)]
        if opening:
            shape += [sds((1, width), jnp.int32), sds((PAD, width), F32)]
            spec += [VM, VM]
            scratch += [pltpu.SMEM((1, width), jnp.int32), pltpu.SemaphoreType.DMA]
            ins, args = [SM, SM] + [VM] * 5, [code, where, winds, adj, edge, from_west, from_east]
        else:
            ins = [SM, SM, SM] + [VM] * 6
            args = [code, where, found, winds, adj, edge, from_west, from_east, east_wind]
        got = call(
            functools.partial(step_kernel, step, levels, row_count, sizes),
            tuple(shape),
            ins,
            tuple(spec),
            scratch,
        )(*args)
        if closing:
            return got[0].reshape(adjoint_end.shape)
        adj, item, sides = got[:3]
        if opening:
            found, east_wind = got[3:]


def solution(mesh, sizes=(2, 8, 2), tile_sizes=(8, 4)):
    fine = Mesh(mesh.devices.reshape(sizes + tile_sizes), ("zl", "y", "c", "x", "zh"))
    face, tile = ("zl", "y", "c"), ("x", "zh")
    placed = (
        P(None, None, face, tile),
        P(face, tile, None, None, None),
        P(face, tile),
        P(face, tile),
        P(face, tile),
        P(face, tile),
        P(face, tile),
    )
    return jax.shard_map(
        functools.partial(shards, sizes, tile_sizes),
        mesh=fine,
        in_specs=placed,
        out_specs=P(None, None, face, tile),
        check_vma=False,
    )
```

time: 361 us -> 220 us (0.61)
  the two profiles are of different devices: /device:TPU:1 before, /device:TPU:9 now
where the time goes in v1:
time: 220 us; the launch traced here: 219 us
  starting transfers between devices  73.4 us (33%)
  waiting for transfers between devices  72.8 us (33%)
  blocking collectives  41.2 us (19%)
  Pallas kernels  23.6 us (11%)
  local copies, waits for them, and re-layouts  5.66 us (3%)
    ppermute x3, waiting for transfers between devices, to_sides(): lax.ppermute(sides[0], tile, ahead)  42.1 us
    all_to_all x1, blocking collectives, exchange(): return lax.all_to_all(chosen, 'y', 0, 0, tiled=True)  21.7 us
    ppermute x3, starting transfers between devices, to_sides(): lax.ppermute(sides[1], tile, back)  20.7 us
    all_to_all x1, starting transfers between devices, shards(): mini = lax.all_to_all(mini, tile, 0, 0, tiled=True)  19.8 us
    all_gather x3, blocking collectives, exchange(): gathered = lax.all_gather(item, group, axis=0, tiled=False)  19.5 us
    pallas_call x3, Pallas kernels, shards(): call(functools.partial(step_kernel, step, levels, row_count, sizes), tupl...  12.4 us
    all_to_all x1, starting transfers between devices, shards(): lax.all_to_all(jnp.broadcast_to(code, (faces, 1)), face, 0, 0, tiled=True)  11.1 us
    all_to_all x1, waiting for transfers between devices, shards(): mini = lax.all_to_all(mini, tile, 0, 0, tiled=True)  10.5 us
  transfers between devices with their start and end apart: 11, of which 7 were waited for; matrix products, arithmetic and copies ran while one was open for 1% of the time, Pallas kernels for 3%

profile of v1, /device:TPU:9, one launch (start us, length us, event | category | flops | bytes accessed | tf_op | source)
XLA Modules:
  0.0 219.0 jit_solution(6428012775573323445)
XLA Ops:
  2.0 11.1 %all-to-all-start = ((s32[32,1,1]{2,1,0:T(1,128)}), s32[32,1,1]{2,1,0:T(1,128)S(1)}, u32[]{:S(2)}, u32[]{:S(2)}) async-start(s32[32,1,1]{2,1,0:T(1,128)} %broadcast_in_dim.8), calls=%async_computation | async-start | bytes 32768 | tf_op jit(solution)/shard_map/all_to_all | solution.py:301
  14.9 6.2 %shard_map.73 = (bf16[96,2,40,128]{3,2,1,0:T(8,128)(2,1)S(1)}, bf16[32,40,128]{2,1,0:T(8,128)(2,1)}) custom-call(s32[1,96]{1,0:T(1,128)S(1)} %copy-done.4, s32[1,96]{1,0:T(1,128)S(1)} %copy-done.5, s32[1,96]{1,0:T(1,128)S(1)} %copy-done.6, bf16[96,2,36,128]{3,2,1,0:T(8,128)(2,1)S(1)} %bitcast.27), custom_call_target="tpu_custom_call" | custom-call | flops 1048576 | bytes 1048576 | tf_op jit(solution)/shard_map/pallas_call | solution.py:303
  22.4 19.8 %all-to-all-start.2 = ((bf16[32,40,128]{2,1,0:T(8,128)(2,1)}), bf16[32,40,128]{2,1,0:T(8,128)(2,1)S(1)}, u32[]{:S(2)}, u32[]{:S(2)}) async-start(bf16[32,40,128]{2,1,0:T(8,128)(2,1)} %get-tuple-element.20), calls=%async_computation.2 | async-start | bytes 655360 | tf_op jit(solution)/shard_map/all_to_all | solution.py:316
  43.5 10.5 %all-to-all-done.2.mini = bf16[32,40,128]{2,1,0:T(8,128)(2,1)S(1)} async-done(((bf16[32,40,128]{2,1,0:T(8,128)(2,1)}), bf16[32,40,128]{2,1,0:T(8,128)(2,1)S(1)}, u32[]{:S(2)}, u32[]{:S(2)}) %all-to-all-start.2) | async-done | bytes 327712 | tf_op jit(solution)/shard_map/all_to_all | solution.py:316
  54.1 7.5 %all-gather = bf16[20,40,128]{2,1,0:T(8,128)(2,1)S(1)} all-gather(bf16[5,40,128]{2,1,0:T(8,128)(2,1)S(1)} %shard_map.75), channel_id=2, replica_groups=mesh['zl'=2,'y'=8,'c'=2,'x'=8,'zh'=4] {'zl','c'}, dimensions={0}, use_global_device_ids=true | all-gather | bytes 256000 | tf_op jit(solution)/shard_map/all_gather | solution.py:335
  62.6 21.7 %all_to_all.31.refs_4_ = bf16[8,5,40,128]{3,2,1,0:T(8,128)(2,1)S(1)} all-to-all(bf16[8,5,40,128]{3,2,1,0:T(8,128)(2,1)S(1)} %shard_map.76), channel_id=1, replica_groups=mesh['zl'=2,'y'=8,'c'=2,'x'=8,'zh'=4] {'y'}, dimensions={0} | all-to-all | bytes 819200 | tf_op jit(solution)/shard_map/all_to_all | solution.py:343
  84.3 7.1 %all-to-all-start.1 = ((bf16[96,2,40,128]{3,2,1,0:T(8,128)(2,1)}), bf16[96,2,40,128]{3,2,1,0:T(8,128)(2,1)S(1)}, u32[]{:S(2)}, u32[]{:S(2)}) async-start(bf16[96,2,40,128]{3,2,1,0:T(8,128)(2,1)} %copy-done), calls=%async_computation.1 | async-start | bytes 3932160 | tf_op jit(solution)/shard_map/all_to_all | solution.py:317
  91.4 4.0 %collective-permute-start = (f32[40,128]{1,0:T(8,128)S(1)}, f32[40,128]{1,0:T(8,128)S(1)}, u32[]{:S(2)}, u32[]{:S(2)}) collective-permute-start(f32[40,128]{1,0:T(8,128)S(1)} %get-tuple-element.36), channel_id=1, source_target_pairs={{0,1},{1,2},{2,3},{3,4},{4,5},{5,6},{6,7},{7,8},{8,9},{9,10},{10,1... | collective-permute-start | bytes 61448 | tf_op jit(solution)/shard_map/ppermute | solution.py:332
  95.4 5.5 %collective-permute-start.1 = (f32[40,128]{1,0:T(8,128)S(1)}, f32[40,128]{1,0:T(8,128)S(1)}, u32[]{:S(2)}, u32[]{:S(2)}) collective-permute-start(f32[40,128]{1,0:T(8,128)S(1)} %get-tuple-element.35), channel_id=1, source_target_pairs={{1,0},{2,1},{3,2},{4,3},{5,4},{6,5},{7,6},{8,7},{9,8},{10,9},{11,1... | collective-permute-start | bytes 61448 | tf_op jit(solution)/shard_map/ppermute | solution.py:332
  100.9 42.1 %collective-permute-done.refs_5_ = f32[40,128]{1,0:T(8,128)S(1)} collective-permute-done((f32[40,128]{1,0:T(8,128)S(1)}, f32[40,128]{1,0:T(8,128)S(1)}, u32[]{:S(2)}, u32[]{:S(2)}) %collective-permute-start) | collective-permute-done | bytes 20512 | tf_op jit(solution)/shard_map/ppermute | solution.py:332
  143.0 8.4 %all-to-all-done.1.refs_2_.refs_3_ = bf16[96,2,40,128]{3,2,1,0:T(8,128)(2,1)S(1)} async-done(((bf16[96,2,40,128]{3,2,1,0:T(8,128)(2,1)}), bf16[96,2,40,128]{3,2,1,0:T(8,128)(2,1)S(1)}, u32[]{:S(2)}, u32[]{:S(2)}) %all-to-all-start.1) | async-done | bytes 1966112 | tf_op jit(solution)/shard_map/all_to_all | solution.py:317
  151.4 5.2 %shard_map.77 = (f32[16,2,40,128]{3,2,1,0:T(8,128)S(1)}, bf16[5,40,128]{2,1,0:T(8,128)(2,1)S(1)}, f32[2,40,128]{2,1,0:T(8,128)S(1)}, s32[1,128]{1,0:T(1,128)S(1)}, f32[40,128]{1,0:T(8,128)S(1)}) custom-call(s32[1,32]{1,0:T(1,128)S(1)} %bitcast.33, s32[1,3]{1,0:T(1,128)S(1)} %add_bitcast_fusion.where.refs_1_, ...), custom_call_target="tpu_custom_call" | custom-call | flops 1048576 | bytes 1048576 | tf_op jit(solution)/shard_map/pallas_call | solution.py:365
  157.5 6.1 %all-gather.1 = bf16[20,40,128]{2,1,0:T(8,128)(2,1)S(1)} all-gather(bf16[5,40,128]{2,1,0:T(8,128)(2,1)S(1)} %get-tuple-element.25), channel_id=3, replica_groups=mesh['zl'=2,'y'=8,'c'=2,'x'=8,'zh'=4] {'zl','c'}, dimensions={0}, use_global_device_ids=true | all-gather | bytes 256000 | tf_op jit(solution)/shard_map/all_gather | solution.py:335
  165.3 3.5 %all-to-all-start.4 = ((bf16[8,5,40,128]{3,2,1,0:T(8,128)(2,1)}), bf16[8,5,40,128]{3,2,1,0:T(8,128)(2,1)S(1)}, u32[]{:S(2)}, u32[]{:S(2)}) async-start(bf16[8,5,40,128]{3,2,1,0:T(8,128)(2,1)} %shard_map.78), calls=%async_computation.4 | async-start | bytes 819200 | tf_op jit(solution)/shard_map/all_to_all | solution.py:343
  168.8 1.9 collective-permute-start.2
  170.7 7.6 %collective-permute-start.3 = (f32[40,128]{1,0:T(8,128)S(1)}, f32[40,128]{1,0:T(8,128)S(1)}, u32[]{:S(2)}, u32[]{:S(2)}) collective-permute-start(f32[40,128]{1,0:T(8,128)S(1)} %get-tuple-element.33), channel_id=1, source_target_pairs={{1,0},{2,1},{3,2},{4,3},{5,4},{6,5},{7,6},{8,7},{9,8},{10,9},{11,1... | collective-permute-start | bytes 61448 | tf_op jit(solution)/shard_map/ppermute | solution.py:332
  179.2 5.0 %all-to-all-done.4.refs_5_ = bf16[8,5,40,128]{3,2,1,0:T(8,128)(2,1)S(1)} async-done(((bf16[8,5,40,128]{3,2,1,0:T(8,128)(2,1)}), bf16[8,5,40,128]{3,2,1,0:T(8,128)(2,1)S(1)}, u32[]{:S(2)}, u32[]{:S(2)}) %all-to-all-start.4) | async-done | bytes 409632 | tf_op jit(solution)/shard_map/all_to_all | solution.py:343
  185.3 4.4 %shard_map.79 = (f32[16,2,40,128]{3,2,1,0:T(8,128)S(1)}, bf16[5,40,128]{2,1,0:T(8,128)(2,1)S(1)}, f32[2,40,128]{2,1,0:T(8,128)S(1)}) custom-call(s32[1,32]{1,0:T(1,128)S(1)} %bitcast.35, s32[1,3]{1,0:T(1,128)S(1)} %add_bitcast_fusion.where.refs_1_, s32[1,128]{1,0:T(1,128)S(1)} %get-tuple-element.23.refs_2_, ...), custom_call_target="tpu_custom_call" | custom-call | flops 1048576 | bytes 1048576 | tf_op jit(solution)/shard_map/pallas_call | solution.py:365
  189.7 5.9 %all-gather.2 = bf16[20,40,128]{2,1,0:T(8,128)(2,1)S(1)} all-gather(bf16[5,40,128]{2,1,0:T(8,128)(2,1)S(1)} %get-tuple-element.29), channel_id=4, replica_groups=mesh['zl'=2,'y'=8,'c'=2,'x'=8,'zh'=4] {'zl','c'}, dimensions={0}, use_global_device_ids=true | all-gather | bytes 256000 | tf_op jit(solution)/shard_map/all_gather | solution.py:335
  197.4 3.5 %all-to-all-start.5 = ((bf16[8,5,40,128]{3,2,1,0:T(8,128)(2,1)}), bf16[8,5,40,128]{3,2,1,0:T(8,128)(2,1)S(1)}, u32[]{:S(2)}, u32[]{:S(2)}) async-start(bf16[8,5,40,128]{3,2,1,0:T(8,128)(2,1)} %shard_map.80), calls=%async_computation.5 | async-start | bytes 819200 | tf_op jit(solution)/shard_map/all_to_all | solution.py:343
  200.8 1.9 collective-permute-start.4
  202.8 7.6 %collective-permute-start.5 = (f32[40,128]{1,0:T(8,128)S(1)}, f32[40,128]{1,0:T(8,128)S(1)}, u32[]{:S(2)}, u32[]{:S(2)}) collective-permute-start(f32[40,128]{1,0:T(8,128)S(1)} %get-tuple-element.31), channel_id=1, source_target_pairs={{1,0},{2,1},{3,2},{4,3},{5,4},{6,5},{7,6},{8,7},{9,8},{10,9},{11,1... | collective-permute-start | bytes 61448 | tf_op jit(solution)/shard_map/ppermute | solution.py:332
  211.2 5.0 %all-to-all-done.5.refs_5_ = bf16[8,5,40,128]{3,2,1,0:T(8,128)(2,1)S(1)} async-done(((bf16[8,5,40,128]{3,2,1,0:T(8,128)(2,1)}), bf16[8,5,40,128]{3,2,1,0:T(8,128)(2,1)S(1)}, u32[]{:S(2)}, u32[]{:S(2)}) %all-to-all-start.5) | async-done | bytes 409632 | tf_op jit(solution)/shard_map/all_to_all | solution.py:343
  216.3 2.8 %shard_map.81 = f32[1152,128]{1,0:T(8,128)} custom-call(s32[1,32]{1,0:T(1,128)S(1)} %bitcast.37, s32[1,3]{1,0:T(1,128)S(1)} %add_bitcast_fusion.where.refs_1_, s32[1,128]{1,0:T(1,128)S(1)} %get-tuple-element.23.refs_2_, bf16[96,2,40,128]{3,2,1,0:T(8,128)(2,1)S(1)} %all-to-all-done.1.refs_2_.refs_3_, f32[16,2,40,128]{3,2,1,0:T(8,128)S(1)} %get-tuple-element.28.refs_4_, ...), custom_call_target="tpu_custom_call" | custom-call | flops 1048576 | bytes 1048576 | tf_op jit(solution)/shard_map/pallas_call | solution.py:365
  (32 shorter events, 13.2 us)
Async XLA Ops:
  0.0 14.9 %copy-start.4 = (s32[1,96]{1,0:T(1,128)S(1)}, s32[1,96]{1,0:T(1,128)}, u32[]{:S(2)}) copy-start(s32[1,96]{1,0:T(1,128)} %owner.1) | copy-start | bytes 1156
  0.0 14.9 %copy-start.5 = (s32[1,96]{1,0:T(1,128)S(1)}, s32[1,96]{1,0:T(1,128)}, u32[]{:S(2)}) copy-start(s32[1,96]{1,0:T(1,128)} %unit.1) | copy-start | bytes 1156
  0.0 14.9 %copy-start.6 = (s32[1,96]{1,0:T(1,128)S(1)}, s32[1,96]{1,0:T(1,128)}, u32[]{:S(2)}) copy-start(s32[1,96]{1,0:T(1,128)} %valid.1) | copy-start | bytes 1156
  2.0 20.5 %all-to-all-start = ((s32[32,1,1]{2,1,0:T(1,128)}), s32[32,1,1]{2,1,0:T(1,128)S(1)}, u32[]{:S(2)}, u32[]{:S(2)}) async-start(s32[32,1,1]{2,1,0:T(1,128)} %broadcast_in_dim.8), calls=%async_computation | async-start | bytes 32768 | tf_op jit(solution)/shard_map/all_to_all | solution.py:301
  14.9 27.4 %copy-start.3 = (f32[2,36,16,128]{3,2,1,0:T(8,128)S(1)}, f32[2,36,16,128]{3,2,1,0:T(8,128)}, u32[]{:S(2)}) copy-start(f32[2,36,16,128]{3,2,1,0:T(8,128)} %param.7) | copy-start | bytes 1769476
  21.1 1.3 copy-start
  22.4 31.6 %all-to-all-start.2 = ((bf16[32,40,128]{2,1,0:T(8,128)(2,1)}), bf16[32,40,128]{2,1,0:T(8,128)(2,1)S(1)}, u32[]{:S(2)}, u32[]{:S(2)}) async-start(bf16[32,40,128]{2,1,0:T(8,128)(2,1)} %get-tuple-element.20), calls=%async_computation.2 | async-start | bytes 655360 | tf_op jit(solution)/shard_map/all_to_all | solution.py:316
  84.3 67.1 %all-to-all-start.1 = ((bf16[96,2,40,128]{3,2,1,0:T(8,128)(2,1)}), bf16[96,2,40,128]{3,2,1,0:T(8,128)(2,1)S(1)}, u32[]{:S(2)}, u32[]{:S(2)}) async-start(bf16[96,2,40,128]{3,2,1,0:T(8,128)(2,1)} %copy-done), calls=%async_computation.1 | async-start | bytes 3932160 | tf_op jit(solution)/shard_map/all_to_all | solution.py:317
  91.4 51.6 %collective-permute-start = (f32[40,128]{1,0:T(8,128)S(1)}, f32[40,128]{1,0:T(8,128)S(1)}, u32[]{:S(2)}, u32[]{:S(2)}) collective-permute-start(f32[40,128]{1,0:T(8,128)S(1)} %get-tuple-element.36), channel_id=1, source_target_pairs={{0,1},{1,2},{2,3},{3,4},{4,5},{5,6},{6,7},{7,8},{8,9},{9,10},{10,1... | collective-permute-start | bytes 61448 | tf_op jit(solution)/shard_map/ppermute | solution.py:332
  95.4 47.6 %collective-permute-start.1 = (f32[40,128]{1,0:T(8,128)S(1)}, f32[40,128]{1,0:T(8,128)S(1)}, u32[]{:S(2)}, u32[]{:S(2)}) collective-permute-start(f32[40,128]{1,0:T(8,128)S(1)} %get-tuple-element.35), channel_id=1, source_target_pairs={{1,0},{2,1},{3,2},{4,3},{5,4},{6,5},{7,6},{8,7},{9,8},{10,9},{11,1... | collective-permute-start | bytes 61448 | tf_op jit(solution)/shard_map/ppermute | solution.py:332
  156.7 0.8 copy-start.1
  165.3 18.9 %all-to-all-start.4 = ((bf16[8,5,40,128]{3,2,1,0:T(8,128)(2,1)}), bf16[8,5,40,128]{3,2,1,0:T(8,128)(2,1)S(1)}, u32[]{:S(2)}, u32[]{:S(2)}) async-start(bf16[8,5,40,128]{3,2,1,0:T(8,128)(2,1)} %shard_map.78), calls=%async_computation.4 | async-start | bytes 819200 | tf_op jit(solution)/shard_map/all_to_all | solution.py:343
  168.8 9.5 %collective-permute-start.2 = (f32[40,128]{1,0:T(8,128)S(1)}, f32[40,128]{1,0:T(8,128)S(1)}, u32[]{:S(2)}, u32[]{:S(2)}) collective-permute-start(f32[40,128]{1,0:T(8,128)S(1)} %get-tuple-element.34), channel_id=1, source_target_pairs={{0,1},{1,2},{2,3},{3,4},{4,5},{5,6},{6,7},{7,8},{8,9},{9,10},{10,1... | collective-permute-start | bytes 61448 | tf_op jit(solution)/shard_map/ppermute | solution.py:332
  170.7 8.5 %collective-permute-start.3 = (f32[40,128]{1,0:T(8,128)S(1)}, f32[40,128]{1,0:T(8,128)S(1)}, u32[]{:S(2)}, u32[]{:S(2)}) collective-permute-start(f32[40,128]{1,0:T(8,128)S(1)} %get-tuple-element.33), channel_id=1, source_target_pairs={{1,0},{2,1},{3,2},{4,3},{5,4},{6,5},{7,6},{8,7},{9,8},{10,9},{11,1... | collective-permute-start | bytes 61448 | tf_op jit(solution)/shard_map/ppermute | solution.py:332
  184.2 1.1 copy-start.2
  197.4 18.9 %all-to-all-start.5 = ((bf16[8,5,40,128]{3,2,1,0:T(8,128)(2,1)}), bf16[8,5,40,128]{3,2,1,0:T(8,128)(2,1)S(1)}, u32[]{:S(2)}, u32[]{:S(2)}) async-start(bf16[8,5,40,128]{3,2,1,0:T(8,128)(2,1)} %shard_map.80), calls=%async_computation.5 | async-start | bytes 819200 | tf_op jit(solution)/shard_map/all_to_all | solution.py:343
  200.8 9.5 %collective-permute-start.4 = (f32[40,128]{1,0:T(8,128)S(1)}, f32[40,128]{1,0:T(8,128)S(1)}, u32[]{:S(2)}, u32[]{:S(2)}) collective-permute-start(f32[40,128]{1,0:T(8,128)S(1)} %get-tuple-element.32), channel_id=1, source_target_pairs={{0,1},{1,2},{2,3},{3,4},{4,5},{5,6},{6,7},{7,8},{8,9},{9,10},{10,1... | collective-permute-start | bytes 61448 | tf_op jit(solution)/shard_map/ppermute | solution.py:332
  202.8 8.5 %collective-permute-start.5 = (f32[40,128]{1,0:T(8,128)S(1)}, f32[40,128]{1,0:T(8,128)S(1)}, u32[]{:S(2)}, u32[]{:S(2)}) collective-permute-start(f32[40,128]{1,0:T(8,128)S(1)} %get-tuple-element.31), channel_id=1, source_target_pairs={{1,0},{2,1},{3,2},{4,3},{5,4},{6,5},{7,6},{8,7},{9,8},{10,9},{11,1... | collective-permute-start | bytes 61448 | tf_op jit(solution)/shard_map/ppermute | solution.py:332

commit v2 on v1

v2 whole, which is shorter than its diff:
```python
import functools

import jax
import jax.numpy as jnp
from jax import lax
from jax.experimental import pallas as pl
from jax.experimental.pallas import tpu as pltpu
from jax.sharding import Mesh
from jax.sharding import PartitionSpec as P

STEPS = 3
COURANT = 0.2
PAD = 40
LABEL, LABEL_EAST = 64, 65
INTERPRET = False

VM = pl.BlockSpec(memory_space=pltpu.VMEM)
SM = pl.BlockSpec(memory_space=pltpu.SMEM)
F32, BF16 = jnp.float32, jnp.bfloat16


def call(kernel, out_shape, in_specs, out_specs, scratch=(), flops=1 << 20, moved=1 << 20):
    return pl.pallas_call(
        kernel,
        out_shape=out_shape,
        in_specs=in_specs,
        out_specs=out_specs,
        scratch_shapes=list(scratch),
        compiler_params=pltpu.CompilerParams(vmem_limit_bytes=40 << 20),
        cost_estimate=pl.CostEstimate(flops=flops, bytes_accessed=moved, transcendentals=0),
        interpret=INTERPRET,
    )


def lanes(rows, width):
    return lax.broadcasted_iota(jnp.int32, (rows, width), 1)


def spread(values, lane, shape):
    return jnp.broadcast_to(values[:, lane : lane + 1], shape)


def pack_kernel(levels, tiles, owner, unit, valid, rows, out, count, source, label, flat):
    slots, width = rows.shape[0], rows.shape[3]
    capacity = slots // tiles

    def clear(i, c):
        count[i] = 0
        return c

    lax.fori_loop(0, tiles, clear, 0, unroll=8)

    def blank(i, c):
        source[i] = 0
        label[i] = -1
        return c

    lax.fori_loop(0, slots, blank, 0, unroll=8)

    def place(s, c):
        @pl.when(valid[0, s] == 1)
        def _():
            o = owner[0, s]
            p = o * capacity + count[o]
            source[p] = s
            label[p] = unit[0, s]
            count[o] = count[o] + 1

        return c

    lax.fori_loop(0, slots, place, 0)

    lane = lanes(levels, width)

    def column(s, held):
        v = rows[s, 0].astype(F32)
        return jnp.where(lane == s, spread(v, 0, v.shape), held)

    held = lax.fori_loop(0, slots, column, jnp.zeros((levels, width), F32), unroll=8)
    flat[...] = jnp.zeros_like(flat)
    flat[0:levels, :] = held
    flat[...] = flat[...].T

    extra_lane = lanes(1, width)
    zeros = jnp.zeros((PAD - levels, width), BF16)

    def fill(p, c):
        s = source[p]
        q = jnp.where(p + capacity >= slots, p + capacity - slots, p + capacity)
        out[p, 0, 0:levels, :] = rows[s, 0]
        out[p, 1, 0:levels, :] = rows[s, 1]
        extra = flat[pl.ds(source[q], 1), :]
        extra = jnp.where(extra_lane == LABEL, label[p].astype(F32), extra)
        extra = jnp.where(extra_lane == LABEL_EAST, label[q].astype(F32), extra)
        out[p, 0, levels:PAD, :] = jnp.broadcast_to(extra, zeros.shape).astype(BF16)
        out[p, 1, levels:PAD, :] = zeros
        return c

    lax.fori_loop(0, slots, fill, 0, unroll=4)


def edges_kernel(levels, row_count, adj, turned, item, last_out, head_out):
    width = adj.shape[1]
    lane = lanes(PAD, width)
    last = jnp.zeros((PAD, width), F32)
    head = jnp.zeros((PAD, width), F32)
    for r in range(row_count):
        for f in range(2):
            for l0 in range(0, levels, 8):
                n = min(8, levels - l0)
                turned[r, f, l0 : l0 + n, :] = adj[pl.ds((f * levels + l0) * row_count + r, n, stride=row_count), :]
            turned[r, f, levels:PAD, :] = jnp.zeros((PAD - levels, width), F32)
            v = turned[r, f]
            q = r * 2 + f
            last = jnp.where(lane == q, spread(v, width - 1, v.shape), last)
            head = jnp.where(lane == q, spread(v, 0, v.shape), head)
            if r == 0:
                item[f] = v.astype(BF16)
            if r == row_count - 1:
                item[2 + f] = v.astype(BF16)
    last_out[...] = last
    head_out[...] = head


def invert(code, inverse):
    def one(f, c):
        inverse[lax.shift_right_logical(code[0, f], 1)] = f
        return c

    lax.fori_loop(0, code.shape[1], one, 0)


def choose_kernel(sizes, north_from, shifted, code, where, gathered, *refs):
    _, ny, nc = sizes
    outs, inverse = refs[:-1], refs[-1]
    invert(code, inverse)
    zl, y, c = where[0, 0], where[0, 1], where[0, 2]
    for d in range(ny):
        plane = lax.rem(y + d, ny) if shifted else d
        dest = (zl * ny + plane) * nc + c
        for source, a, b in (
            (inverse[dest], 0, north_from),
            (lax.shift_right_logical(code[0, dest], 1), north_from, gathered.shape[1]),
        ):
            group = (source // (ny * nc)) * nc + source % nc
            for i in range(a, b):
                if shifted:
                    outs[d][i] = gathered[group, i]
                else:
                    outs[0][d, i] = gathered[group, i]


def neighbours(sizes, shifted, code, where, inverse):
    _, ny, nc = sizes
    invert(code, inverse)
    y = where[0, 1]
    me = (where[0, 0] * ny + y) * nc + where[0, 2]
    north, south = lax.shift_right_logical(code[0, me], 1), inverse[me]
    north_plane, south_plane = (north // nc) % ny, (south // nc) % ny
    if shifted:
        north_plane, south_plane = lax.rem(y - north_plane + ny, ny), lax.rem(y - south_plane + ny, ny)
    return north_plane, code[0, me] & 1, south_plane, code[0, south] & 1


def oriented(block, turn):
    n, rows, width = block.shape
    i = lax.broadcasted_iota(jnp.int32, (width, width), 0)
    j = lax.broadcasted_iota(jnp.int32, (width, width), 1)
    source = jnp.where(turn == 1, width - 1 - j, j)
    matrix = jnp.where(i == source, 1.0, 0.0).astype(BF16)
    out = jnp.dot(block.reshape(n * rows, width), matrix, preferred_element_type=F32)
    return out.reshape(n, rows, width)


def find_slots(levels, winds, found_out, found, sem, east_wind):
    slots, width = winds.shape[0], winds.shape[3]
    extra = winds[:, 0, PAD - 8 : PAD, :].astype(F32).reshape(slots * 8, width)
    row = lax.broadcasted_iota(jnp.int32, extra.shape, 0)
    ours = (row & 7) == levels - (PAD - 8)
    lane = lanes(slots * 8, width).astype(F32)
    here = ours & (spread(extra, LABEL, extra.shape) == lane)
    there = ours & (spread(extra, LABEL_EAST, extra.shape) == lane)
    slot = lax.shift_right_logical(row, 3).astype(F32)
    index = jnp.sum(jnp.where(here, slot, 0.0), axis=0, keepdims=True)
    found_out[...] = index.astype(jnp.int32)
    copy = pltpu.make_async_copy(found_out, found, sem)
    copy.start()
    columns = lax.dot_general(
        jnp.where(ours, extra, 0.0).astype(BF16),
        jnp.where(there, 1.0, 0.0).astype(BF16),
        (((0,), (0,)), ((), ())),
        preferred_element_type=F32,
    )
    east_wind[...] = columns[0:PAD, :]
    copy.wait()


def advance(step, winds, found, east_wind, adj, final, upper, lower, south_end, from_west, from_east, put, sides):
    row_count, width = adj.shape[0], adj.shape[3]
    lane = lanes(PAD, width)
    last = jnp.zeros((PAD, width), F32)
    head = jnp.zeros((PAD, width), F32)
    base = step * row_count

    def row(r, f):
        return final[f] if final is not None and r == row_count - 1 else adj[r, f]

    north_wind = winds[found[0, base], 1].astype(F32)
    for r in range(row_count):
        west_wind = winds[found[0, base + r], 0].astype(F32)
        if r + 1 < row_count:
            south_wind = winds[found[0, base + r + 1], 1].astype(F32)
        else:
            south_wind = south_end
        eastern_wind = jnp.where(
            lane == width - 1, spread(east_wind, base + r, lane.shape), pltpu.roll(west_wind, width - 1, 1)
        )
        cw = COURANT * jnp.minimum(west_wind, 0.0)
        ce = COURANT * jnp.maximum(eastern_wind, 0.0)
        cn = COURANT * jnp.minimum(north_wind, 0.0)
        if south_wind is not None:
            cs = COURANT * jnp.maximum(south_wind, 0.0)
        for f in range(2):
            q = r * 2 + f
            a = row(r, f)
            west = jnp.where(lane == 0, spread(from_west, q, a.shape), pltpu.roll(a, 1, 1))
            east = jnp.where(lane == width - 1, spread(from_east, q, a.shape), pltpu.roll(a, width - 1, 1))
            v = a + cw * (a - west)
            v = v + ce * (east - a)
            v = v + cn * (a - (row(r - 1, f) if r > 0 else upper[f]))
            if south_wind is not None:
                v = v + cs * ((row(r + 1, f) if r + 1 < row_count else lower[f]) - a)
            put(r, f, v)
            if sides is not None:
                last = jnp.where(lane == q, spread(v, width - 1, v.shape), last)
                head = jnp.where(lane == q, spread(v, 0, v.shape), head)
        north_wind = south_wind
    if sides is not None:
        sides[0][...] = last
        sides[1][...] = head


def first_kernel(
    step, levels, sizes,
    code, where, winds, adj, edge, from_west, from_east,
    out, item, kept, last_out, head_out, found_out, east_wind,
    inverse, found, sem,
):
    row_count = adj.shape[0]
    end = row_count - 1
    find_slots(levels, winds, found_out, found, sem, east_wind)
    north, turn_north, south, turn_south = neighbours(sizes, True, code, where, inverse)
    upper = oriented(edge[north, 2:4], turn_north)
    lower = oriented(edge[south, 0:2], turn_south)

    def put(r, f, v):
        out[r, f] = v
        if r == 0:
            item[f] = v.astype(BF16)
        if r == end:
            item[4 + f] = v.astype(BF16)
            kept[9 + f] = v

    advance(step, winds, found, east_wind, adj, None, upper, None, None, from_west, from_east, put, (last_out, head_out))
    item[2] = winds[found[0, step * row_count], 1]
    item[3] = winds[found[0, (step - 1) * row_count], 1]
    kept[0:2] = upper
    kept[2:4] = lower
    kept[4:6] = adj[end]
    kept[6:8] = adj[0]
    kept[8] = winds[found[0, step * row_count], 1].astype(F32)


def mend_kernel(sizes, row_count, code, where, edge, kept, last_in, head_in, ends, last_out, head_out, inverse):
    width = kept.shape[2]
    north, turn_north, south, turn_south = neighbours(sizes, False, code, where, inverse)
    lower = oriented(edge[south, 0:4], turn_south)
    cs = COURANT * jnp.maximum(lower[2], 0.0)
    lane = lanes(PAD, width)
    last, head = last_in[...], head_in[...]
    for f in range(2):
        v = kept[9 + f] + cs * (kept[2 + f] - kept[4 + f])
        ends[f] = v
        q = 2 * (row_count - 1) + f
        last = jnp.where(lane == q, spread(v, width - 1, v.shape), last)
        head = jnp.where(lane == q, spread(v, 0, v.shape), head)
    last_out[...] = last
    head_out[...] = head
    upper = oriented(edge[north, 4:6], turn_north)
    cs = COURANT * jnp.maximum(kept[8], 0.0)
    for f in range(2):
        mine = kept[6 + f].astype(BF16).astype(F32)
        v = upper[f] + cs * (mine - kept[f])
        ends[2 + f] = v.astype(BF16).astype(F32)
        ends[4 + f] = lower[f]
    ends[6] = lower[3]


def middle_kernel(step, found, winds, adj, ends, from_west, from_east, east_wind, out, item, last_out, head_out):
    row_count = adj.shape[0]

    def put(r, f, v):
        out[r, f] = v
        if r == 0:
            item[f] = v.astype(BF16)
        if r == row_count - 1:
            item[3 + f] = v.astype(BF16)

    advance(
        step, winds, found, east_wind, adj, (ends[0], ends[1]), (ends[2], ends[3]), (ends[4], ends[5]), ends[6],
        from_west, from_east, put, (last_out, head_out),
    )
    item[2] = winds[found[0, (step - 1) * row_count], 1]


def last_kernel(
    step, levels, sizes, code, where, found, winds, adj, edge, from_west, from_east, east_wind, out, inverse
):
    row_count = adj.shape[0]
    north, turn_north, south, turn_south = neighbours(sizes, False, code, where, inverse)
    upper = oriented(edge[north, 3:5], turn_north)
    lower = oriented(edge[south, 0:3], turn_south)

    def put(r, f, v):
        for l0 in range(0, levels, 8):
            n = min(8, levels - l0)
            out[pl.ds((f * levels + l0) * row_count + r, n, stride=row_count), :] = v[l0 : l0 + n]

    advance(step, winds, found, east_wind, adj, None, upper, lower, lower[2], from_west, from_east, put, None)


def shards(sizes, tile_sizes, adjoint_end, stored_rows, stored_owner, stored_unit, stored_valid, edge_match, edge_turn):
    face, tile, group = ("zl", "y", "c"), ("x", "zh"), ("zl", "c")
    faces = sizes[0] * sizes[1] * sizes[2]
    tiles = tile_sizes[0] * tile_sizes[1]
    levels, row_count, width = adjoint_end.shape[1:]
    slots = stored_rows.shape[1]
    sds = jax.ShapeDtypeStruct
    side = sds((PAD, width), F32)

    where = jnp.stack([lax.axis_index(a) for a in face]).astype(jnp.int32).reshape(1, 3)
    code = edge_match * 2 + edge_turn
    code = lax.all_to_all(jnp.broadcast_to(code, (faces, 1)), face, 0, 0, tiled=True).reshape(1, faces)

    payload = call(
        functools.partial(pack_kernel, levels, tiles),
        sds((slots, 2, PAD, width), BF16),
        [SM, SM, SM, VM],
        VM,
        [
            pltpu.SMEM((tiles,), jnp.int32),
            pltpu.SMEM((slots,), jnp.int32),
            pltpu.SMEM((slots,), jnp.int32),
            pltpu.VMEM((width, width), F32),
        ],
    )(stored_owner, stored_unit, stored_valid, stored_rows[0])
    winds = lax.all_to_all(payload, tile, 0, 0, tiled=True)

    turned, item, *sides = call(
        functools.partial(edges_kernel, levels, row_count),
        (sds((row_count, 2, PAD, width), F32), sds((4, PAD, width), BF16), side, side),
        [VM],
        (VM,) * 4,
    )(adjoint_end.reshape(2 * levels * row_count, width))

    inverse = pltpu.SMEM((faces,), jnp.int32)
    planes = sizes[1]

    def to_sides(sides):
        ahead = [(i, (i + 1) % tiles) for i in range(tiles)]
        back = [((i + 1) % tiles, i) for i in range(tiles)]
        return lax.ppermute(sides[0], tile, ahead), lax.ppermute(sides[1], tile, back)

    def gathered(item, north_from, shifted):
        mates = lax.all_gather(item, group, axis=0, tiled=False)
        if shifted:
            shape, spec = (sds(item.shape, BF16),) * planes, (VM,) * planes
        else:
            shape, spec = sds((planes,) + item.shape, BF16), VM
        kernel = functools.partial(choose_kernel, sizes, north_from, shifted)
        return call(kernel, shape, [SM, SM, VM], spec, [inverse])(code, where, mates)

    from_west, from_east = to_sides(sides)
    parts = gathered(item, 2, True)
    moved = [parts[0]]
    for d in range(1, planes):
        moved.append(lax.ppermute(parts[d], "y", [(i, (i + d) % planes) for i in range(planes)]))
    edge = jnp.stack(moved)

    adj, item, kept, *sides, found, east_wind = call(
        functools.partial(first_kernel, STEPS - 1, levels, sizes),
        (
            sds(turned.shape, F32),
            sds((6, PAD, width), BF16),
            sds((11, PAD, width), F32),
            side,
            side,
            sds((1, width), jnp.int32),
            side,
        ),
        [SM, SM] + [VM] * 5,
        (VM,) * 7,
        [inverse, pltpu.SMEM((1, width), jnp.int32), pltpu.SemaphoreType.DMA],
    )(code, where, winds, turned, edge, from_west, from_east)

    edge = lax.all_to_all(gathered(item, 4, False), "y", 0, 0, tiled=True)
    ends, *sides = call(
        functools.partial(mend_kernel, sizes, row_count),
        (sds((7, PAD, width), F32), side, side),
        [SM, SM] + [VM] * 4,
        (VM,) * 3,
        [inverse],
    )(code, where, edge, kept, *sides)

    from_west, from_east = to_sides(sides)
    adj, item, *sides = call(
        functools.partial(middle_kernel, STEPS - 2),
        (sds(turned.shape, F32), sds((5, PAD, width), BF16), side, side),
        [SM] + [VM] * 6,
        (VM,) * 4,
    )(found, winds, adj, ends, from_west, from_east, east_wind)

    from_west, from_east = to_sides(sides)
    edge = lax.all_to_all(gathered(item, 3, False), "y", 0, 0, tiled=True)
    out = call(
        functools.partial(last_kernel, STEPS - 3, levels, sizes),
        sds((2 * levels * row_count, width), F32),
        [SM, SM, SM] + [VM] * 6,
        VM,
        [inverse],
    )(code, where, found, winds, adj, edge, from_west, from_east, east_wind)
    return out.reshape(adjoint_end.shape)


def solution(mesh, sizes=(2, 8, 2), tile_sizes=(8, 4)):
    fine = Mesh(mesh.devices.reshape(sizes + tile_sizes), ("zl", "y", "c", "x", "zh"))
    face, tile = ("zl", "y", "c"), ("x", "zh")
    placed = (
        P(None, None, face, tile),
        P(face, tile, None, None, None),
        P(face, tile),
        P(face, tile),
        P(face, tile),
        P(face, tile),
        P(face, tile),
    )
    return jax.shard_map(
        functools.partial(shards, sizes, tile_sizes),
        mesh=fine,
        in_specs=placed,
        out_specs=P(None, None, face, tile),
        check_vma=False,
    )
```

time: 220 us -> 211 us (0.959)
  waiting for transfers between devices: 72.8 us -> 10.1 us
  blocking collectives: 41.2 us -> 79.8 us
  starting transfers between devices: 73.4 us -> 91.7 us
    ppermute x3, waiting for transfers between devices: 42.1 us -> 0.01 us  [to_sides(): lax.ppermute(sides[0], tile, ahead)]
    all_gather x3, blocking collectives: 19.5 us -> 59.4 us  [gathered(): mates = lax.all_gather(item, group, axis=0, tiled=False)]
    ppermute x0 -> x7, starting transfers between devices: none -> 28.8 us  [shards(): lax.ppermute(parts[d], 'y', [(i, (i + d) % planes) for i in range(planes)])]
    all_to_all x3 -> x1, starting transfers between devices: 26.8 us -> 3.46 us  [shards(): edge = lax.all_to_all(gathered(item, 3, False), 'y', 0, 0, tiled=True)]
    all_to_all x3 -> x1, waiting for transfers between devices: 20.5 us -> 4.46 us  [shards(): edge = lax.all_to_all(gathered(item, 3, False), 'y', 0, 0, tiled=True)]
    all_to_all x1, starting transfers between devices: 7.06 us -> 19.8 us  [shards(): winds = lax.all_to_all(payload, tile, 0, 0, tiled=True)]
    all_to_all x1, waiting for transfers between devices: 8.41 us -> 0.01 us  [shards(): winds = lax.all_to_all(payload, tile, 0, 0, tiled=True)]
    ppermute x3, starting transfers between devices: 7.83 us -> 11.5 us  [to_sides(): lax.ppermute(sides[0], tile, ahead)]
  transfers between devices with their start and end apart: 11 -> 16, of which waited for: 7 -> 5; matrix products, arithmetic and copies ran while one was open for 1% -> 1% of each run, Pallas kernels for 3% -> 3%
where the time goes in v2:
time: 211 us; the launch traced here: 210 us
  starting transfers between devices  91.7 us (43%)
  blocking collectives  79.8 us (38%)
  Pallas kernels  22 us (10%)
  waiting for transfers between devices  10.1 us (5%)
  local copies, waits for them, and re-layouts  3.8 us (2%)
    all_gather x3, blocking collectives, gathered(): mates = lax.all_gather(item, group, axis=0, tiled=False)  59.4 us
    ppermute x7, starting transfers between devices, shards(): lax.ppermute(parts[d], 'y', [(i, (i + d) % planes) for i in range(planes)])  28.8 us
    all_to_all x1, blocking collectives, shards(): edge = lax.all_to_all(gathered(item, 4, False), 'y', 0, 0, tiled=True)  20.4 us
    all_to_all x1, starting transfers between devices, shards(): winds = lax.all_to_all(payload, tile, 0, 0, tiled=True)  19.8 us
    ppermute x3, starting transfers between devices, to_sides(): lax.ppermute(sides[1], tile, back)  17 us
    ppermute x3, starting transfers between devices, to_sides(): lax.ppermute(sides[0], tile, ahead)  11.5 us
    all_to_all x1, starting transfers between devices, shards(): lax.all_to_all(jnp.broadcast_to(code, (faces, 1)), face, 0, 0, tiled=True)  11.1 us
    pallas_call x1, Pallas kernels, shards(): call(functools.partial(first_kernel, STEPS - 1, levels, sizes), (sds(turn...  5.26 us
  transfers between devices with their start and end apart: 16, of which 5 were waited for; matrix products, arithmetic and copies ran while one was open for 1% of the time, Pallas kernels for 3%

profile of v2, /device:TPU:9, one launch (start us, length us, event | category | flops | bytes accessed | tf_op | source)
XLA Modules:
  0.0 209.8 jit_solution(10714329427284859328)
XLA Ops:
  2.0 11.1 %all-to-all-start = ((s32[32,1,1]{2,1,0:T(1,128)}), s32[32,1,1]{2,1,0:T(1,128)S(1)}, u32[]{:S(2)}, u32[]{:S(2)}) async-start(s32[32,1,1]{2,1,0:T(1,128)} %broadcast_in_dim.8), calls=%async_computation | async-start | bytes 32768 | tf_op jit(solution)/shard_map/all_to_all | solution.py:343
  14.9 4.4 %shard_map.73 = bf16[96,2,40,128]{3,2,1,0:T(8,128)(2,1)S(1)} custom-call(s32[1,96]{1,0:T(1,128)S(1)} %copy-done.2, s32[1,96]{1,0:T(1,128)S(1)} %copy-done.3, s32[1,96]{1,0:T(1,128)S(1)} %copy-done.4, bf16[96,2,36,128]{3,2,1,0:T(8,128)(2,1)S(1)} %bitcast.31), custom_call_target="tpu_custom_call" | custom-call | flops 1048576 | bytes 1048576 | tf_op jit(solution)/shard_map/pallas_call | solution.py:345
  20.8 19.8 %all-to-all-start.1 = ((bf16[96,2,40,128]{3,2,1,0:T(8,128)(2,1)}), bf16[96,2,40,128]{3,2,1,0:T(8,128)(2,1)S(1)}, u32[]{:S(2)}, u32[]{:S(2)}) async-start(bf16[96,2,40,128]{3,2,1,0:T(8,128)(2,1)} %copy-done), calls=%async_computation.1 | async-start | bytes 3932160 | tf_op jit(solution)/shard_map/all_to_all | solution.py:357
  41.2 4.0 %collective-permute-start.7 = (f32[40,128]{1,0:T(8,128)S(1)}, f32[40,128]{1,0:T(8,128)S(1)}, u32[]{:S(2)}, u32[]{:S(2)}) collective-permute-start(f32[40,128]{1,0:T(8,128)S(1)} %get-tuple-element.41), channel_id=1, source_target_pairs={{0,1},{1,2},{2,3},{3,4},{4,5},{5,6},{6,7},{7,8},{8,9},{9,10},{10,1... | collective-permute-start | bytes 61448 | tf_op jit(solution)/shard_map/ppermute | solution.py:372
  45.2 5.5 %collective-permute-start.8 = (f32[40,128]{1,0:T(8,128)S(1)}, f32[40,128]{1,0:T(8,128)S(1)}, u32[]{:S(2)}, u32[]{:S(2)}) collective-permute-start(f32[40,128]{1,0:T(8,128)S(1)} %get-tuple-element.42), channel_id=1, source_target_pairs={{1,0},{2,1},{3,2},{4,3},{5,4},{6,5},{7,6},{8,7},{9,8},{10,9},{11,1... | collective-permute-start | bytes 61448 | tf_op jit(solution)/shard_map/ppermute | solution.py:372
  50.8 41.0 %all-gather = bf16[16,40,128]{2,1,0:T(8,128)(2,1)S(1)} all-gather(bf16[4,40,128]{2,1,0:T(8,128)(2,1)S(1)} %get-tuple-element.32), channel_id=2, replica_groups=mesh['zl'=2,'y'=8,'c'=2,'x'=8,'zh'=4] {'zl','c'}, dimensions={0}, use_global_device_ids=true | all-gather | bytes 204800 | tf_op jit(solution)/shard_map/all_gather | solution.py:375
  93.5 4.0 %collective-permute-start = (bf16[4,40,128]{2,1,0:T(8,128)(2,1)S(1)}, bf16[4,40,128]{2,1,0:T(8,128)(2,1)S(1)}, u32[]{:S(2)}, u32[]{:S(2)}) collective-permute-start(bf16[4,40,128]{2,1,0:T(8,128)(2,1)S(1)} %get-tuple-element.34), channel_id=1, source_target_pairs={{0,64},{64,128},{128,192},{192,256},{256,320},{320,384},{384,448},... | collective-permute-start | bytes 122888 | tf_op jit(solution)/shard_map/ppermute | solution.py:387
  97.6 4.0 %collective-permute-start.1 = (bf16[4,40,128]{2,1,0:T(8,128)(2,1)S(1)}, bf16[4,40,128]{2,1,0:T(8,128)(2,1)S(1)}, u32[]{:S(2)}, u32[]{:S(2)}) collective-permute-start(bf16[4,40,128]{2,1,0:T(8,128)(2,1)S(1)} %get-tuple-element.35), channel_id=1, source_target_pairs={{0,128},{64,192},{128,256},{192,320},{256,384},{320,448},{384,0},{... | collective-permute-start | bytes 122888 | tf_op jit(solution)/shard_map/ppermute | solution.py:387
  101.6 4.5 %collective-permute-start.2 = (bf16[4,40,128]{2,1,0:T(8,128)(2,1)S(1)}, bf16[4,40,128]{2,1,0:T(8,128)(2,1)S(1)}, u32[]{:S(2)}, u32[]{:S(2)}) collective-permute-start(bf16[4,40,128]{2,1,0:T(8,128)(2,1)S(1)} %get-tuple-element.36), channel_id=1, source_target_pairs={{0,192},{64,256},{128,320},{192,384},{256,448},{320,0},{384,64},{4... | collective-permute-start | bytes 122888 | tf_op jit(solution)/shard_map/ppermute | solution.py:387
  106.1 3.6 %collective-permute-start.3 = (bf16[4,40,128]{2,1,0:T(8,128)(2,1)S(1)}, bf16[4,40,128]{2,1,0:T(8,128)(2,1)S(1)}, u32[]{:S(2)}, u32[]{:S(2)}) collective-permute-start(bf16[4,40,128]{2,1,0:T(8,128)(2,1)S(1)} %get-tuple-element.37), channel_id=1, source_target_pairs={{0,256},{64,320},{128,384},{192,448},{256,0},{320,64},{384,128},{4... | collective-permute-start | bytes 122888 | tf_op jit(solution)/shard_map/ppermute | solution.py:387
  109.7 5.2 %collective-permute-start.4 = (bf16[4,40,128]{2,1,0:T(8,128)(2,1)S(1)}, bf16[4,40,128]{2,1,0:T(8,128)(2,1)S(1)}, u32[]{:S(2)}, u32[]{:S(2)}) collective-permute-start(bf16[4,40,128]{2,1,0:T(8,128)(2,1)S(1)} %get-tuple-element.38), channel_id=1, source_target_pairs={{0,320},{64,384},{128,448},{192,0},{256,64},{320,128},{384,192},{4... | collective-permute-start | bytes 122888 | tf_op jit(solution)/shard_map/ppermute | solution.py:387
  114.9 4.6 %collective-permute-start.5 = (bf16[4,40,128]{2,1,0:T(8,128)(2,1)S(1)}, bf16[4,40,128]{2,1,0:T(8,128)(2,1)S(1)}, u32[]{:S(2)}, u32[]{:S(2)}) collective-permute-start(bf16[4,40,128]{2,1,0:T(8,128)(2,1)S(1)} %get-tuple-element.39), channel_id=1, source_target_pairs={{0,384},{64,448},{128,0},{192,64},{256,128},{320,192},{384,256},{4... | collective-permute-start | bytes 122888 | tf_op jit(solution)/shard_map/ppermute | solution.py:387
  119.6 2.9 %collective-permute-start.6 = (bf16[4,40,128]{2,1,0:T(8,128)(2,1)S(1)}, bf16[4,40,128]{2,1,0:T(8,128)(2,1)S(1)}, u32[]{:S(2)}, u32[]{:S(2)}) collective-permute-start(bf16[4,40,128]{2,1,0:T(8,128)(2,1)S(1)} %get-tuple-element.40), channel_id=1, source_target_pairs={{0,448},{64,0},{128,64},{192,128},{256,192},{320,256},{384,320},{4... | collective-permute-start | bytes 122888 | tf_op jit(solution)/shard_map/ppermute | solution.py:387
  124.3 5.3 %shard_map.76 = (f32[16,2,40,128]{3,2,1,0:T(8,128)S(1)}, bf16[6,40,128]{2,1,0:T(8,128)(2,1)S(1)}, f32[11,40,128]{2,1,0:T(8,128)S(1)}, f32[40,128]{1,0:T(8,128)S(...) custom-call(s32[1,32]{1,0:T(1,128)S(1)} %bitcast.37, s32[1,3]{1,0:T(1,128)S(1)} %add_bitcast_fusion.where, ...), custom_call_target="tpu_custom_call" | custom-call | flops 1048576 | bytes 1048576 | tf_op jit(solution)/shard_map/pallas_call | solution.py:390
  129.6 11.0 %all-gather.1 = bf16[24,40,128]{2,1,0:T(8,128)(2,1)S(1)} all-gather(bf16[6,40,128]{2,1,0:T(8,128)(2,1)S(1)} %get-tuple-element.45), channel_id=3, replica_groups=mesh['zl'=2,'y'=8,'c'=2,'x'=8,'zh'=4] {'zl','c'}, dimensions={0}, use_global_device_ids=true | all-gather | bytes 307200 | tf_op jit(solution)/shard_map/all_gather | solution.py:375
  141.6 20.4 %all_to_all.21.edge = bf16[8,6,40,128]{3,2,1,0:T(8,128)(2,1)S(1)} all-to-all(bf16[8,6,40,128]{3,2,1,0:T(8,128)(2,1)S(1)} %shard_map.77), channel_id=1, replica_groups=mesh['zl'=2,'y'=8,'c'=2,'x'=8,'zh'=4] {'y'}, dimensions={0} | all-to-all | bytes 983040 | tf_op jit(solution)/shard_map/all_to_all | solution.py:406
  165.1 7.6 %collective-permute-start.10 = (f32[40,128]{1,0:T(8,128)S(1)}, f32[40,128]{1,0:T(8,128)S(1)}, u32[]{:S(2)}, u32[]{:S(2)}) collective-permute-start(f32[40,128]{1,0:T(8,128)S(1)} %get-tuple-element.51), channel_id=1, source_target_pairs={{1,0},{2,1},{3,2},{4,3},{5,4},{6,5},{7,6},{8,7},{9,8},{10,9},{11,1... | collective-permute-start | bytes 61448 | tf_op jit(solution)/shard_map/ppermute | solution.py:372
  174.8 4.1 %shard_map.79 = (f32[16,2,40,128]{3,2,1,0:T(8,128)S(1)}, bf16[5,40,128]{2,1,0:T(8,128)(2,1)S(1)}, f32[40,128]{1,0:T(8,128)S(1)}, f32[40,128]{1,0:T(8,128)S(1)}) custom-call(s32[1,128]{1,0:T(1,128)S(1)} %get-tuple-element.43.found, bf16[96,2,40,128]{3,2,1,0:T(8,128)(2,1)S(1)} %all-to-all-done.1.winds, f32[16,2,40,128]{3,2,1,0:T(8,128)S(1)} %get-tuple-element.44.adj, ...), custom_call_target="tpu_custom_call" | custom-call | flops 1048576 | bytes 1048576 | tf_op jit(solution)/shard_map/pallas_call | solution.py:416
  179.0 7.4 %all-gather.2 = bf16[20,40,128]{2,1,0:T(8,128)(2,1)S(1)} all-gather(bf16[5,40,128]{2,1,0:T(8,128)(2,1)S(1)} %get-tuple-element.54), channel_id=4, replica_groups=mesh['zl'=2,'y'=8,'c'=2,'x'=8,'zh'=4] {'zl','c'}, dimensions={0}, use_global_device_ids=true | all-gather | bytes 256000 | tf_op jit(solution)/shard_map/all_gather | solution.py:375
  188.1 3.5 %all-to-all-start.3 = ((bf16[8,5,40,128]{3,2,1,0:T(8,128)(2,1)}), bf16[8,5,40,128]{3,2,1,0:T(8,128)(2,1)S(1)}, u32[]{:S(2)}, u32[]{:S(2)}) async-start(bf16[8,5,40,128]{3,2,1,0:T(8,128)(2,1)} %shard_map.80), calls=%async_computation.3 | async-start | bytes 819200 | tf_op jit(solution)/shard_map/all_to_all | solution.py:424
  191.5 5.5 %collective-permute-start.11 = (f32[40,128]{1,0:T(8,128)S(1)}, f32[40,128]{1,0:T(8,128)S(1)}, u32[]{:S(2)}, u32[]{:S(2)}) collective-permute-start(f32[40,128]{1,0:T(8,128)S(1)} %get-tuple-element.55), channel_id=1, source_target_pairs={{0,1},{1,2},{2,3},{3,4},{4,5},{5,6},{6,7},{7,8},{8,9},{9,10},{10,1... | collective-permute-start | bytes 61448 | tf_op jit(solution)/shard_map/ppermute | solution.py:372
  197.1 4.0 %collective-permute-start.12 = (f32[40,128]{1,0:T(8,128)S(1)}, f32[40,128]{1,0:T(8,128)S(1)}, u32[]{:S(2)}, u32[]{:S(2)}) collective-permute-start(f32[40,128]{1,0:T(8,128)S(1)} %get-tuple-element.56), channel_id=1, source_target_pairs={{1,0},{2,1},{3,2},{4,3},{5,4},{6,5},{7,6},{8,7},{9,8},{10,9},{11,1... | collective-permute-start | bytes 61448 | tf_op jit(solution)/shard_map/ppermute | solution.py:372
  202.5 4.5 %all-to-all-done.3.edge = bf16[8,5,40,128]{3,2,1,0:T(8,128)(2,1)S(1)} async-done(((bf16[8,5,40,128]{3,2,1,0:T(8,128)(2,1)}), bf16[8,5,40,128]{3,2,1,0:T(8,128)(2,1)S(1)}, u32[]{:S(2)}, u32[]{:S(2)}) %all-to-all-start.3) | async-done | bytes 409632 | tf_op jit(solution)/shard_map/all_to_all | solution.py:424
  207.0 2.8 %shard_map.81 = f32[1152,128]{1,0:T(8,128)} custom-call(s32[1,32]{1,0:T(1,128)S(1)} %bitcast.41, s32[1,3]{1,0:T(1,128)S(1)} %add_bitcast_fusion.where, s32[1,128]{1,0:T(1,128)S(1)} %get-tuple-element.43.found, bf16[96,2,40,128]{3,2,1,0:T(8,128)(2,1)S(1)} %all-to-all-done.1.winds, f32[16,2,40,128]{3,2,1,0:T(8,128)S(1)} %get-tuple-element.53.adj, ...), custom_call_target="tpu_custom_call" | custom-call | flops 1048576 | bytes 1048576 | tf_op jit(solution)/shard_map/pallas_call | solution.py:425
  (43 shorter events, 17.4 us)
Async XLA Ops:
  0.0 14.9 %copy-start.2 = (s32[1,96]{1,0:T(1,128)S(1)}, s32[1,96]{1,0:T(1,128)}, u32[]{:S(2)}) copy-start(s32[1,96]{1,0:T(1,128)} %owner.1) | copy-start | bytes 1156
  0.0 14.9 %copy-start.3 = (s32[1,96]{1,0:T(1,128)S(1)}, s32[1,96]{1,0:T(1,128)}, u32[]{:S(2)}) copy-start(s32[1,96]{1,0:T(1,128)} %unit.1) | copy-start | bytes 1156
  0.0 14.9 %copy-start.4 = (s32[1,96]{1,0:T(1,128)S(1)}, s32[1,96]{1,0:T(1,128)}, u32[]{:S(2)}) copy-start(s32[1,96]{1,0:T(1,128)} %valid.1) | copy-start | bytes 1156
  2.0 18.9 %all-to-all-start = ((s32[32,1,1]{2,1,0:T(1,128)}), s32[32,1,1]{2,1,0:T(1,128)S(1)}, u32[]{:S(2)}, u32[]{:S(2)}) async-start(s32[32,1,1]{2,1,0:T(1,128)} %broadcast_in_dim.8), calls=%async_computation | async-start | bytes 32768 | tf_op jit(solution)/shard_map/all_to_all | solution.py:343
  19.4 1.3 copy-start
  20.7 20.0 %copy-start.1 = (f32[2,36,16,128]{3,2,1,0:T(8,128)S(1)}, f32[2,36,16,128]{3,2,1,0:T(8,128)}, u32[]{:S(2)}) copy-start(f32[2,36,16,128]{3,2,1,0:T(8,128)} %param.7) | copy-start | bytes 1769476
  20.8 103.5 %all-to-all-start.1 = ((bf16[96,2,40,128]{3,2,1,0:T(8,128)(2,1)}), bf16[96,2,40,128]{3,2,1,0:T(8,128)(2,1)S(1)}, u32[]{:S(2)}, u32[]{:S(2)}) async-start(bf16[96,2,40,128]{3,2,1,0:T(8,128)(2,1)} %copy-done), calls=%async_computation.1 | async-start | bytes 3932160 | tf_op jit(solution)/shard_map/all_to_all | solution.py:357
  41.2 83.1 %collective-permute-start.7 = (f32[40,128]{1,0:T(8,128)S(1)}, f32[40,128]{1,0:T(8,128)S(1)}, u32[]{:S(2)}, u32[]{:S(2)}) collective-permute-start(f32[40,128]{1,0:T(8,128)S(1)} %get-tuple-element.41), channel_id=1, source_target_pairs={{0,1},{1,2},{2,3},{3,4},{4,5},{5,6},{6,7},{7,8},{8,9},{9,10},{10,1... | collective-permute-start | bytes 61448 | tf_op jit(solution)/shard_map/ppermute | solution.py:372
  45.2 79.1 %collective-permute-start.8 = (f32[40,128]{1,0:T(8,128)S(1)}, f32[40,128]{1,0:T(8,128)S(1)}, u32[]{:S(2)}, u32[]{:S(2)}) collective-permute-start(f32[40,128]{1,0:T(8,128)S(1)} %get-tuple-element.42), channel_id=1, source_target_pairs={{1,0},{2,1},{3,2},{4,3},{5,4},{6,5},{7,6},{8,7},{9,8},{10,9},{11,1... | collective-permute-start | bytes 61448 | tf_op jit(solution)/shard_map/ppermute | solution.py:372
  93.5 12.5 %collective-permute-start = (bf16[4,40,128]{2,1,0:T(8,128)(2,1)S(1)}, bf16[4,40,128]{2,1,0:T(8,128)(2,1)S(1)}, u32[]{:S(2)}, u32[]{:S(2)}) collective-permute-start(bf16[4,40,128]{2,1,0:T(8,128)(2,1)S(1)} %get-tuple-element.34), channel_id=1, source_target_pairs={{0,64},{64,128},{128,192},{192,256},{256,320},{320,384},{384,448},... | collective-permute-start | bytes 122888 | tf_op jit(solution)/shard_map/ppermute | solution.py:387
  97.6 12.1 %collective-permute-start.1 = (bf16[4,40,128]{2,1,0:T(8,128)(2,1)S(1)}, bf16[4,40,128]{2,1,0:T(8,128)(2,1)S(1)}, u32[]{:S(2)}, u32[]{:S(2)}) collective-permute-start(bf16[4,40,128]{2,1,0:T(8,128)(2,1)S(1)} %get-tuple-element.35), channel_id=1, source_target_pairs={{0,128},{64,192},{128,256},{192,320},{256,384},{320,448},{384,0},{... | collective-permute-start | bytes 122888 | tf_op jit(solution)/shard_map/ppermute | solution.py:387
  101.6 13.3 %collective-permute-start.2 = (bf16[4,40,128]{2,1,0:T(8,128)(2,1)S(1)}, bf16[4,40,128]{2,1,0:T(8,128)(2,1)S(1)}, u32[]{:S(2)}, u32[]{:S(2)}) collective-permute-start(bf16[4,40,128]{2,1,0:T(8,128)(2,1)S(1)} %get-tuple-element.36), channel_id=1, source_target_pairs={{0,192},{64,256},{128,320},{192,384},{256,448},{320,0},{384,64},{4... | collective-permute-start | bytes 122888 | tf_op jit(solution)/shard_map/ppermute | solution.py:387
  106.1 13.5 %collective-permute-start.3 = (bf16[4,40,128]{2,1,0:T(8,128)(2,1)S(1)}, bf16[4,40,128]{2,1,0:T(8,128)(2,1)S(1)}, u32[]{:S(2)}, u32[]{:S(2)}) collective-permute-start(bf16[4,40,128]{2,1,0:T(8,128)(2,1)S(1)} %get-tuple-element.37), channel_id=1, source_target_pairs={{0,256},{64,320},{128,384},{192,448},{256,0},{320,64},{384,128},{4... | collective-permute-start | bytes 122888 | tf_op jit(solution)/shard_map/ppermute | solution.py:387
  109.7 12.8 %collective-permute-start.4 = (bf16[4,40,128]{2,1,0:T(8,128)(2,1)S(1)}, bf16[4,40,128]{2,1,0:T(8,128)(2,1)S(1)}, u32[]{:S(2)}, u32[]{:S(2)}) collective-permute-start(bf16[4,40,128]{2,1,0:T(8,128)(2,1)S(1)} %get-tuple-element.38), channel_id=1, source_target_pairs={{0,320},{64,384},{128,448},{192,0},{256,64},{320,128},{384,192},{4... | collective-permute-start | bytes 122888 | tf_op jit(solution)/shard_map/ppermute | solution.py:387
  114.9 7.6 %collective-permute-start.5 = (bf16[4,40,128]{2,1,0:T(8,128)(2,1)S(1)}, bf16[4,40,128]{2,1,0:T(8,128)(2,1)S(1)}, u32[]{:S(2)}, u32[]{:S(2)}) collective-permute-start(bf16[4,40,128]{2,1,0:T(8,128)(2,1)S(1)} %get-tuple-element.39), channel_id=1, source_target_pairs={{0,384},{64,448},{128,0},{192,64},{256,128},{320,192},{384,256},{4... | collective-permute-start | bytes 122888 | tf_op jit(solution)/shard_map/ppermute | solution.py:387
  119.6 4.7 %collective-permute-start.6 = (bf16[4,40,128]{2,1,0:T(8,128)(2,1)S(1)}, bf16[4,40,128]{2,1,0:T(8,128)(2,1)S(1)}, u32[]{:S(2)}, u32[]{:S(2)}) collective-permute-start(bf16[4,40,128]{2,1,0:T(8,128)(2,1)S(1)} %get-tuple-element.40), channel_id=1, source_target_pairs={{0,448},{64,0},{128,64},{192,128},{256,192},{320,256},{384,320},{4... | collective-permute-start | bytes 122888 | tf_op jit(solution)/shard_map/ppermute | solution.py:387
  163.1 9.5 %collective-permute-start.9 = (f32[40,128]{1,0:T(8,128)S(1)}, f32[40,128]{1,0:T(8,128)S(1)}, u32[]{:S(2)}, u32[]{:S(2)}) collective-permute-start(f32[40,128]{1,0:T(8,128)S(1)} %get-tuple-element.50), channel_id=1, source_target_pairs={{0,1},{1,2},{2,3},{3,4},{4,5},{5,6},{6,7},{7,8},{8,9},{9,10},{10,1... | collective-permute-start | bytes 61448 | tf_op jit(solution)/shard_map/ppermute | solution.py:372
  165.1 9.8 %collective-permute-start.10 = (f32[40,128]{1,0:T(8,128)S(1)}, f32[40,128]{1,0:T(8,128)S(1)}, u32[]{:S(2)}, u32[]{:S(2)}) collective-permute-start(f32[40,128]{1,0:T(8,128)S(1)} %get-tuple-element.51), channel_id=1, source_target_pairs={{1,0},{2,1},{3,2},{4,3},{5,4},{6,5},{7,6},{8,7},{9,8},{10,9},{11,1... | collective-permute-start | bytes 61448 | tf_op jit(solution)/shard_map/ppermute | solution.py:372
  188.1 18.9 %all-to-all-start.3 = ((bf16[8,5,40,128]{3,2,1,0:T(8,128)(2,1)}), bf16[8,5,40,128]{3,2,1,0:T(8,128)(2,1)S(1)}, u32[]{:S(2)}, u32[]{:S(2)}) async-start(bf16[8,5,40,128]{3,2,1,0:T(8,128)(2,1)} %shard_map.80), calls=%async_computation.3 | async-start | bytes 819200 | tf_op jit(solution)/shard_map/all_to_all | solution.py:424
  191.5 9.5 %collective-permute-start.11 = (f32[40,128]{1,0:T(8,128)S(1)}, f32[40,128]{1,0:T(8,128)S(1)}, u32[]{:S(2)}, u32[]{:S(2)}) collective-permute-start(f32[40,128]{1,0:T(8,128)S(1)} %get-tuple-element.55), channel_id=1, source_target_pairs={{0,1},{1,2},{2,3},{3,4},{4,5},{5,6},{6,7},{7,8},{8,9},{9,10},{10,1... | collective-permute-start | bytes 61448 | tf_op jit(solution)/shard_map/ppermute | solution.py:372
  197.1 5.4 %collective-permute-start.12 = (f32[40,128]{1,0:T(8,128)S(1)}, f32[40,128]{1,0:T(8,128)S(1)}, u32[]{:S(2)}, u32[]{:S(2)}) collective-permute-start(f32[40,128]{1,0:T(8,128)S(1)} %get-tuple-element.56), channel_id=1, source_target_pairs={{1,0},{2,1},{3,2},{4,3},{5,4},{6,5},{7,6},{8,7},{9,8},{10,9},{11,1... | collective-permute-start | bytes 61448 | tf_op jit(solution)/shard_map/ppermute | solution.py:372

commit v3 on v2

--- a/solution.py
+++ b/solution.py
@@ -12,22 +12,24 @@
 COURANT = 0.2
 PAD = 40
 LABEL, LABEL_EAST = 64, 65
+CHUNKS = 4
 INTERPRET = False
 
 VM = pl.BlockSpec(memory_space=pltpu.VMEM)
 SM = pl.BlockSpec(memory_space=pltpu.SMEM)
+HBM = pl.BlockSpec(memory_space=pltpu.HBM)
 F32, BF16 = jnp.float32, jnp.bfloat16
 
 
-def call(kernel, out_shape, in_specs, out_specs, scratch=(), flops=1 << 20, moved=1 << 20):
+def call(kernel, out_shape, in_specs, out_specs, scratch=(), vmem=40 << 20):
     return pl.pallas_call(
         kernel,
         out_shape=out_shape,
         in_specs=in_specs,
         out_specs=out_specs,
         scratch_shapes=list(scratch),
-        compiler_params=pltpu.CompilerParams(vmem_limit_bytes=40 << 20),
-        cost_estimate=pl.CostEstimate(flops=flops, bytes_accessed=moved, transcendentals=0),
+        compiler_params=pltpu.CompilerParams(vmem_limit_bytes=vmem),
+        cost_estimate=pl.CostEstimate(flops=1 << 20, bytes_accessed=1 << 20, transcendentals=0),
         interpret=INTERPRET,
     )
 
@@ -40,8 +42,10 @@
     return jnp.broadcast_to(values[:, lane : lane + 1], shape)
 
 
-def pack_kernel(levels, tiles, owner, unit, valid, rows, out, count, source, label, flat):
+def pack_kernel(levels, tiles, owner, unit, valid, stored, sent, count, source, label, flat, rows, out, sem_in, sem_out):
     slots, width = rows.shape[0], rows.shape[3]
+    fetch = pltpu.make_async_copy(stored, rows, sem_in)
+    fetch.start()
     capacity = slots // tiles
 
     def clear(i, c):
@@ -68,7 +72,8 @@
 
         return c
 
-    lax.fori_loop(0, slots, place, 0)
+    lax.fori_loop(0, slots, place, 0, unroll=4)
+    fetch.wait()
 
     lane = lanes(levels, width)
 
@@ -96,7 +101,15 @@
         out[p, 1, levels:PAD, :] = zeros
         return c
 
-    lax.fori_loop(0, slots, fill, 0, unroll=4)
+    chunk = slots // CHUNKS
+    copies = []
+    for i in range(CHUNKS):
+        lax.fori_loop(i * chunk, (i + 1) * chunk, fill, 0, unroll=4)
+        span = pl.ds(i * chunk, chunk)
+        copies.append(pltpu.make_async_copy(out.at[span], sent.at[span], sem_out.at[i]))
+        copies[-1].start()
+    for copy in copies:
+        copy.wait()
 
 
 def edges_kernel(levels, row_count, adj, turned, item, last_out, head_out):
@@ -345,16 +358,20 @@
     payload = call(
         functools.partial(pack_kernel, levels, tiles),
         sds((slots, 2, PAD, width), BF16),
-        [SM, SM, SM, VM],
-        VM,
+        [SM, SM, SM, HBM],
+        HBM,
         [
             pltpu.SMEM((tiles,), jnp.int32),
             pltpu.SMEM((slots,), jnp.int32),
             pltpu.SMEM((slots,), jnp.int32),
             pltpu.VMEM((width, width), F32),
+            pltpu.VMEM(stored_rows.shape[1:], BF16),
+            pltpu.VMEM((slots, 2, PAD, width), BF16),
+            pltpu.SemaphoreType.DMA,
+            pltpu.SemaphoreType.DMA((CHUNKS,)),
         ],
+        62 << 20,
     )(stored_owner, stored_unit, stored_valid, stored_rows[0])
-    winds = lax.all_to_all(payload, tile, 0, 0, tiled=True)
 
     turned, item, *sides = call(
         functools.partial(edges_kernel, levels, row_count),
@@ -371,17 +388,22 @@
         back = [((i + 1) % tiles, i) for i in range(tiles)]
         return lax.ppermute(sides[0], tile, ahead), lax.ppermute(sides[1], tile, back)
 
-    def gathered(item, north_from, shifted):
-        mates = lax.all_gather(item, group, axis=0, tiled=False)
+    def gather(item):
+        return lax.all_gather(item, group, axis=0, tiled=False)
+
+    def chosen(mates, north_from, shifted):
+        shape_of_one = mates.shape[1:]
         if shifted:
-            shape, spec = (sds(item.shape, BF16),) * planes, (VM,) * planes
+            shape, spec = (sds(shape_of_one, BF16),) * planes, (VM,) * planes
         else:
-            shape, spec = sds((planes,) + item.shape, BF16), VM
+            shape, spec = sds((planes,) + shape_of_one, BF16), VM
         kernel = functools.partial(choose_kernel, sizes, north_from, shifted)
         return call(kernel, shape, [SM, SM, VM], spec, [inverse])(code, where, mates)
 
+    payload, mates = lax.optimization_barrier((payload, gather(item)))
+    winds = lax.all_to_all(payload, tile, 0, 0, tiled=True)
     from_west, from_east = to_sides(sides)
-    parts = gathered(item, 2, True)
+    parts = chosen(mates, 2, True)
     moved = [parts[0]]
     for d in range(1, planes):
         moved.append(lax.ppermute(parts[d], "y", [(i, (i + d) % planes) for i in range(planes)]))
@@ -403,7 +425,7 @@
         [inverse, pltpu.SMEM((1, width), jnp.int32), pltpu.SemaphoreType.DMA],
     )(code, where, winds, turned, edge, from_west, from_east)
 
-    edge = lax.all_to_all(gathered(item, 4, False), "y", 0, 0, tiled=True)
+    edge = lax.all_to_all(chosen(gather(item), 4, False), "y", 0, 0, tiled=True)
     ends, *sides = call(
         functools.partial(mend_kernel, sizes, row_count),
         (sds((7, PAD, width), F32), side, side),
@@ -421,7 +443,7 @@
     )(found, winds, adj, ends, from_west, from_east, east_wind)
 
     from_west, from_east = to_sides(sides)
-    edge = lax.all_to_all(gathered(item, 3, False), "y", 0, 0, tiled=True)
+    edge = lax.all_to_all(chosen(gather(item), 3, False), "y", 0, 0, tiled=True)
     out = call(
         functools.partial(last_kernel, STEPS - 3, levels, sizes),
         sds((2 * levels * row_count, width), F32),

time: 211 us -> 188 us (0.89)
  blocking collectives: 79.8 us -> 42.6 us
  waiting for transfers between devices: 10.1 us -> 23.3 us
    all_gather x3, blocking collectives: 59.4 us -> 19 us  [gather(): return lax.all_gather(item, group, axis=0, tiled=False)]
    ppermute x3, waiting for transfers between devices: 0.01 us -> 9.76 us  [to_sides(): lax.ppermute(sides[0], tile, ahead)]
    all_to_all x1, waiting for transfers between devices: 0.01 us -> 5.34 us  [shards(): winds = lax.all_to_all(payload, tile, 0, 0, tiled=True)]
    ppermute x3, starting transfers between devices: 17 us -> 21.3 us  [to_sides(): lax.ppermute(sides[1], tile, back)]
    ppermute x3, starting transfers between devices: 11.5 us -> 7.83 us  [to_sides(): lax.ppermute(sides[0], tile, ahead)]
    all_to_all x1, blocking collectives: 20.4 us -> 23.6 us  [shards(): edge = lax.all_to_all(chosen(gather(item), 4, False), 'y', 0, 0, tiled=True)]
  transfers between devices with their start and end apart: 16 -> 16, of which waited for: 5 -> 7; matrix products, arithmetic and copies ran while one was open for 1% -> 2% of each run, Pallas kernels for 3% -> 3%
where the time goes in v3:
time: 188 us; the launch traced here: 187 us
  starting transfers between devices  91.8 us (49%)
  blocking collectives  42.6 us (23%)
  waiting for transfers between devices  23.3 us (12%)
  Pallas kernels  22.3 us (12%)
  local copies, waits for them, and re-layouts  4.81 us (3%)
    ppermute x7, starting transfers between devices, shards(): lax.ppermute(parts[d], 'y', [(i, (i + d) % planes) for i in range(planes)])  28.2 us
    all_to_all x1, blocking collectives, shards(): edge = lax.all_to_all(chosen(gather(item), 4, False), 'y', 0, 0, tiled=True)  23.6 us
    ppermute x3, starting transfers between devices, to_sides(): lax.ppermute(sides[1], tile, back)  21.3 us
    all_to_all x1, starting transfers between devices, shards(): winds = lax.all_to_all(payload, tile, 0, 0, tiled=True)  19.8 us
    all_gather x3, blocking collectives, gather(): return lax.all_gather(item, group, axis=0, tiled=False)  19 us
    all_to_all x1, starting transfers between devices, shards(): lax.all_to_all(jnp.broadcast_to(code, (faces, 1)), face, 0, 0, tiled=True)  11.1 us
    ppermute x3, waiting for transfers between devices, to_sides(): lax.ppermute(sides[0], tile, ahead)  9.76 us
    ppermute x3, starting transfers between devices, to_sides(): lax.ppermute(sides[0], tile, ahead)  7.83 us
  transfers between devices with their start and end apart: 16, of which 7 were waited for; matrix products, arithmetic and copies ran while one was open for 2% of the time, Pallas kernels for 3%

profile of v3, /device:TPU:9, one launch (start us, length us, event | category | flops | bytes accessed | tf_op | source)
XLA Modules:
  0.0 187.2 jit_solution(5685659291659537815)
XLA Ops:
  1.9 11.1 %all-to-all-start = ((s32[32,1,1]{2,1,0:T(1,128)}), s32[32,1,1]{2,1,0:T(1,128)S(1)}, u32[]{:S(2)}, u32[]{:S(2)}) async-start(s32[32,1,1]{2,1,0:T(1,128)} %broadcast_in_dim.8), calls=%async_computation | async-start | bytes 32768 | tf_op jit(solution)/shard_map/all_to_all | solution.py:356
  14.6 5.6 %all-gather = bf16[16,40,128]{2,1,0:T(8,128)(2,1)S(1)} all-gather(bf16[4,40,128]{2,1,0:T(8,128)(2,1)S(1)} %get-tuple-element.33), channel_id=2, replica_groups=mesh['zl'=2,'y'=8,'c'=2,'x'=8,'zh'=4] {'zl','c'}, dimensions={0}, use_global_device_ids=true | all-gather | bytes 204800 | tf_op jit(solution)/shard_map/all_gather | solution.py:392
  23.3 4.9 %shard_map.73 = bf16[96,2,40,128]{3,2,1,0:T(8,128)(2,1)} custom-call(s32[1,96]{1,0:T(1,128)} %owner.1, s32[1,96]{1,0:T(1,128)} %unit.1, s32[1,96]{1,0:T(1,128)} %valid.1, bf16[96,2,36,128]{3,2,1,0:T(8,128)(2,1)} %bitcast.41), custom_call_target="tpu_custom_call" | custom-call | flops 1048576 | bytes 1048576 | tf_op jit(solution)/shard_map/pallas_call | solution.py:358
  28.2 19.8 %all-to-all-start.1 = ((bf16[96,2,40,128]{3,2,1,0:T(8,128)(2,1)}), bf16[96,2,40,128]{3,2,1,0:T(8,128)(2,1)S(1)}, u32[]{:S(2)}, u32[]{:S(2)}) async-start(bf16[96,2,40,128]{3,2,1,0:T(8,128)(2,1)} %shard_map.73), calls=%async_computation.1 | async-start | bytes 3932160 | tf_op jit(solution)/shard_map/all_to_all | solution.py:404
  48.1 4.0 %collective-permute-start.7 = (f32[40,128]{1,0:T(8,128)S(1)}, f32[40,128]{1,0:T(8,128)S(1)}, u32[]{:S(2)}, u32[]{:S(2)}) collective-permute-start(f32[40,128]{1,0:T(8,128)S(1)} %get-tuple-element.45), channel_id=1, source_target_pairs={{0,1},{1,2},{2,3},{3,4},{4,5},{5,6},{6,7},{7,8},{8,9},{9,10},{10,1... | collective-permute-start | bytes 61448 | tf_op jit(solution)/shard_map/ppermute | solution.py:389
  52.1 5.5 %collective-permute-start.8 = (f32[40,128]{1,0:T(8,128)S(1)}, f32[40,128]{1,0:T(8,128)S(1)}, u32[]{:S(2)}, u32[]{:S(2)}) collective-permute-start(f32[40,128]{1,0:T(8,128)S(1)} %get-tuple-element.46), channel_id=1, source_target_pairs={{1,0},{2,1},{3,2},{4,3},{5,4},{6,5},{7,6},{8,7},{9,8},{10,9},{11,1... | collective-permute-start | bytes 61448 | tf_op jit(solution)/shard_map/ppermute | solution.py:389
  59.4 3.4 %collective-permute-start = (bf16[4,40,128]{2,1,0:T(8,128)(2,1)S(1)}, bf16[4,40,128]{2,1,0:T(8,128)(2,1)S(1)}, u32[]{:S(2)}, u32[]{:S(2)}) collective-permute-start(bf16[4,40,128]{2,1,0:T(8,128)(2,1)S(1)} %get-tuple-element.38), channel_id=1, source_target_pairs={{0,64},{64,128},{128,192},{192,256},{256,320},{320,384},{384,448},... | collective-permute-start | bytes 122888 | tf_op jit(solution)/shard_map/ppermute | solution.py:409
  62.7 4.0 %collective-permute-start.1 = (bf16[4,40,128]{2,1,0:T(8,128)(2,1)S(1)}, bf16[4,40,128]{2,1,0:T(8,128)(2,1)S(1)}, u32[]{:S(2)}, u32[]{:S(2)}) collective-permute-start(bf16[4,40,128]{2,1,0:T(8,128)(2,1)S(1)} %get-tuple-element.39), channel_id=1, source_target_pairs={{0,128},{64,192},{128,256},{192,320},{256,384},{320,448},{384,0},{... | collective-permute-start | bytes 122888 | tf_op jit(solution)/shard_map/ppermute | solution.py:409
  66.7 4.3 %collective-permute-start.2 = (bf16[4,40,128]{2,1,0:T(8,128)(2,1)S(1)}, bf16[4,40,128]{2,1,0:T(8,128)(2,1)S(1)}, u32[]{:S(2)}, u32[]{:S(2)}) collective-permute-start(bf16[4,40,128]{2,1,0:T(8,128)(2,1)S(1)} %get-tuple-element.40), channel_id=1, source_target_pairs={{0,192},{64,256},{128,320},{192,384},{256,448},{320,0},{384,64},{4... | collective-permute-start | bytes 122888 | tf_op jit(solution)/shard_map/ppermute | solution.py:409
  71.1 4.0 %collective-permute-start.3 = (bf16[4,40,128]{2,1,0:T(8,128)(2,1)S(1)}, bf16[4,40,128]{2,1,0:T(8,128)(2,1)S(1)}, u32[]{:S(2)}, u32[]{:S(2)}) collective-permute-start(bf16[4,40,128]{2,1,0:T(8,128)(2,1)S(1)} %get-tuple-element.41), channel_id=1, source_target_pairs={{0,256},{64,320},{128,384},{192,448},{256,0},{320,64},{384,128},{4... | collective-permute-start | bytes 122888 | tf_op jit(solution)/shard_map/ppermute | solution.py:409
  75.1 4.3 %collective-permute-start.4 = (bf16[4,40,128]{2,1,0:T(8,128)(2,1)S(1)}, bf16[4,40,128]{2,1,0:T(8,128)(2,1)S(1)}, u32[]{:S(2)}, u32[]{:S(2)}) collective-permute-start(bf16[4,40,128]{2,1,0:T(8,128)(2,1)S(1)} %get-tuple-element.42), channel_id=1, source_target_pairs={{0,320},{64,384},{128,448},{192,0},{256,64},{320,128},{384,192},{4... | collective-permute-start | bytes 122888 | tf_op jit(solution)/shard_map/ppermute | solution.py:409
  79.4 5.2 %collective-permute-start.5 = (bf16[4,40,128]{2,1,0:T(8,128)(2,1)S(1)}, bf16[4,40,128]{2,1,0:T(8,128)(2,1)S(1)}, u32[]{:S(2)}, u32[]{:S(2)}) collective-permute-start(bf16[4,40,128]{2,1,0:T(8,128)(2,1)S(1)} %get-tuple-element.43), channel_id=1, source_target_pairs={{0,384},{64,448},{128,0},{192,64},{256,128},{320,192},{384,256},{4... | collective-permute-start | bytes 122888 | tf_op jit(solution)/shard_map/ppermute | solution.py:409
  84.7 3.1 %collective-permute-start.6 = (bf16[4,40,128]{2,1,0:T(8,128)(2,1)S(1)}, bf16[4,40,128]{2,1,0:T(8,128)(2,1)S(1)}, u32[]{:S(2)}, u32[]{:S(2)}) collective-permute-start(bf16[4,40,128]{2,1,0:T(8,128)(2,1)S(1)} %get-tuple-element.44), channel_id=1, source_target_pairs={{0,448},{64,0},{128,64},{192,128},{256,192},{320,256},{384,320},{4... | collective-permute-start | bytes 122888 | tf_op jit(solution)/shard_map/ppermute | solution.py:409
  89.7 9.8 %collective-permute-done.7.from_west = f32[40,128]{1,0:T(8,128)S(1)} collective-permute-done((f32[40,128]{1,0:T(8,128)S(1)}, f32[40,128]{1,0:T(8,128)S(1)}, u32[]{:S(2)}, u32[]{:S(2)}) %collective-permute-start.7) | collective-permute-done | bytes 20512 | tf_op jit(solution)/shard_map/ppermute | solution.py:389
  99.7 5.3 %all-to-all-done.1.winds = bf16[96,2,40,128]{3,2,1,0:T(8,128)(2,1)S(1)} async-done(((bf16[96,2,40,128]{3,2,1,0:T(8,128)(2,1)}), bf16[96,2,40,128]{3,2,1,0:T(8,128)(2,1)S(1)}, u32[]{:S(2)}, u32[]{:S(2)}) %all-to-all-start.1) | async-done | bytes 1966112 | tf_op jit(solution)/shard_map/all_to_all | solution.py:404
  105.0 5.2 %shard_map.76 = (f32[16,2,40,128]{3,2,1,0:T(8,128)S(1)}, bf16[6,40,128]{2,1,0:T(8,128)(2,1)S(1)}, f32[11,40,128]{2,1,0:T(8,128)S(1)}, f32[40,128]{1,0:T(8,128)S(...) custom-call(s32[1,32]{1,0:T(1,128)S(1)} %bitcast.36, s32[1,3]{1,0:T(1,128)S(1)} %add_bitcast_fusion.where, ...), custom_call_target="tpu_custom_call" | custom-call | flops 1048576 | bytes 1048576 | tf_op jit(solution)/shard_map/pallas_call | solution.py:412
  110.3 6.2 %all-gather.1 = bf16[24,40,128]{2,1,0:T(8,128)(2,1)S(1)} all-gather(bf16[6,40,128]{2,1,0:T(8,128)(2,1)S(1)} %get-tuple-element.49), channel_id=3, replica_groups=mesh['zl'=2,'y'=8,'c'=2,'x'=8,'zh'=4] {'zl','c'}, dimensions={0}, use_global_device_ids=true | all-gather | bytes 307200 | tf_op jit(solution)/shard_map/all_gather | solution.py:392
  117.4 23.6 %all_to_all.21.edge = bf16[8,6,40,128]{3,2,1,0:T(8,128)(2,1)S(1)} all-to-all(bf16[8,6,40,128]{3,2,1,0:T(8,128)(2,1)S(1)} %shard_map.77), channel_id=1, replica_groups=mesh['zl'=2,'y'=8,'c'=2,'x'=8,'zh'=4] {'y'}, dimensions={0} | all-to-all | bytes 983040 | tf_op jit(solution)/shard_map/all_to_all | solution.py:428
  144.0 7.6 %collective-permute-start.10 = (f32[40,128]{1,0:T(8,128)S(1)}, f32[40,128]{1,0:T(8,128)S(1)}, u32[]{:S(2)}, u32[]{:S(2)}) collective-permute-start(f32[40,128]{1,0:T(8,128)S(1)} %get-tuple-element.55), channel_id=1, source_target_pairs={{1,0},{2,1},{3,2},{4,3},{5,4},{6,5},{7,6},{8,7},{9,8},{10,9},{11,1... | collective-permute-start | bytes 61448 | tf_op jit(solution)/shard_map/ppermute | solution.py:389
  152.5 4.1 %shard_map.79 = (f32[16,2,40,128]{3,2,1,0:T(8,128)S(1)}, bf16[5,40,128]{2,1,0:T(8,128)(2,1)S(1)}, f32[40,128]{1,0:T(8,128)S(1)}, f32[40,128]{1,0:T(8,128)S(1)}) custom-call(s32[1,128]{1,0:T(1,128)S(1)} %get-tuple-element.47.found, bf16[96,2,40,128]{3,2,1,0:T(8,128)(2,1)S(1)} %all-to-all-done.1.winds, f32[16,2,40,128]{3,2,1,0:T(8,128)S(1)} %get-tuple-element.48.adj, ...), custom_call_target="tpu_custom_call" | custom-call | flops 1048576 | bytes 1048576 | tf_op jit(solution)/shard_map/pallas_call | solution.py:438
  156.6 7.2 %all-gather.2 = bf16[20,40,128]{2,1,0:T(8,128)(2,1)S(1)} all-gather(bf16[5,40,128]{2,1,0:T(8,128)(2,1)S(1)} %get-tuple-element.58), channel_id=4, replica_groups=mesh['zl'=2,'y'=8,'c'=2,'x'=8,'zh'=4] {'zl','c'}, dimensions={0}, use_global_device_ids=true | all-gather | bytes 256000 | tf_op jit(solution)/shard_map/all_gather | solution.py:392
  165.5 3.5 %all-to-all-start.3 = ((bf16[8,5,40,128]{3,2,1,0:T(8,128)(2,1)}), bf16[8,5,40,128]{3,2,1,0:T(8,128)(2,1)S(1)}, u32[]{:S(2)}, u32[]{:S(2)}) async-start(bf16[8,5,40,128]{3,2,1,0:T(8,128)(2,1)} %shard_map.80), calls=%async_computation.3 | async-start | bytes 819200 | tf_op jit(solution)/shard_map/all_to_all | solution.py:446
  170.9 8.3 %collective-permute-start.12 = (f32[40,128]{1,0:T(8,128)S(1)}, f32[40,128]{1,0:T(8,128)S(1)}, u32[]{:S(2)}, u32[]{:S(2)}) collective-permute-start(f32[40,128]{1,0:T(8,128)S(1)} %get-tuple-element.60), channel_id=1, source_target_pairs={{1,0},{2,1},{3,2},{4,3},{5,4},{6,5},{7,6},{8,7},{9,8},{10,9},{11,1... | collective-permute-start | bytes 61448 | tf_op jit(solution)/shard_map/ppermute | solution.py:389
  180.1 4.4 %all-to-all-done.3.edge = bf16[8,5,40,128]{3,2,1,0:T(8,128)(2,1)S(1)} async-done(((bf16[8,5,40,128]{3,2,1,0:T(8,128)(2,1)}), bf16[8,5,40,128]{3,2,1,0:T(8,128)(2,1)S(1)}, u32[]{:S(2)}, u32[]{:S(2)}) %all-to-all-start.3) | async-done | bytes 409632 | tf_op jit(solution)/shard_map/all_to_all | solution.py:446
  (35 shorter events, 21.3 us)
Async XLA Ops:
  1.9 26.3 %all-to-all-start = ((s32[32,1,1]{2,1,0:T(1,128)}), s32[32,1,1]{2,1,0:T(1,128)S(1)}, u32[]{:S(2)}, u32[]{:S(2)}) async-start(s32[32,1,1]{2,1,0:T(1,128)} %broadcast_in_dim.8), calls=%async_computation | async-start | bytes 32768 | tf_op jit(solution)/shard_map/all_to_all | solution.py:356
  13.0 1.1 copy-start
  28.2 76.8 %all-to-all-start.1 = ((bf16[96,2,40,128]{3,2,1,0:T(8,128)(2,1)}), bf16[96,2,40,128]{3,2,1,0:T(8,128)(2,1)S(1)}, u32[]{:S(2)}, u32[]{:S(2)}) async-start(bf16[96,2,40,128]{3,2,1,0:T(8,128)(2,1)} %shard_map.73), calls=%async_computation.1 | async-start | bytes 3932160 | tf_op jit(solution)/shard_map/all_to_all | solution.py:404
  48.1 51.4 %collective-permute-start.7 = (f32[40,128]{1,0:T(8,128)S(1)}, f32[40,128]{1,0:T(8,128)S(1)}, u32[]{:S(2)}, u32[]{:S(2)}) collective-permute-start(f32[40,128]{1,0:T(8,128)S(1)} %get-tuple-element.45), channel_id=1, source_target_pairs={{0,1},{1,2},{2,3},{3,4},{4,5},{5,6},{6,7},{7,8},{8,9},{9,10},{10,1... | collective-permute-start | bytes 61448 | tf_op jit(solution)/shard_map/ppermute | solution.py:389
  52.1 47.6 %collective-permute-start.8 = (f32[40,128]{1,0:T(8,128)S(1)}, f32[40,128]{1,0:T(8,128)S(1)}, u32[]{:S(2)}, u32[]{:S(2)}) collective-permute-start(f32[40,128]{1,0:T(8,128)S(1)} %get-tuple-element.46), channel_id=1, source_target_pairs={{1,0},{2,1},{3,2},{4,3},{5,4},{6,5},{7,6},{8,7},{9,8},{10,9},{11,1... | collective-permute-start | bytes 61448 | tf_op jit(solution)/shard_map/ppermute | solution.py:389
  59.4 11.7 %collective-permute-start = (bf16[4,40,128]{2,1,0:T(8,128)(2,1)S(1)}, bf16[4,40,128]{2,1,0:T(8,128)(2,1)S(1)}, u32[]{:S(2)}, u32[]{:S(2)}) collective-permute-start(bf16[4,40,128]{2,1,0:T(8,128)(2,1)S(1)} %get-tuple-element.38), channel_id=1, source_target_pairs={{0,64},{64,128},{128,192},{192,256},{256,320},{320,384},{384,448},... | collective-permute-start | bytes 122888 | tf_op jit(solution)/shard_map/ppermute | solution.py:409
  62.7 12.4 %collective-permute-start.1 = (bf16[4,40,128]{2,1,0:T(8,128)(2,1)S(1)}, bf16[4,40,128]{2,1,0:T(8,128)(2,1)S(1)}, u32[]{:S(2)}, u32[]{:S(2)}) collective-permute-start(bf16[4,40,128]{2,1,0:T(8,128)(2,1)S(1)} %get-tuple-element.39), channel_id=1, source_target_pairs={{0,128},{64,192},{128,256},{192,320},{256,384},{320,448},{384,0},{... | collective-permute-start | bytes 122888 | tf_op jit(solution)/shard_map/ppermute | solution.py:409
  66.7 12.7 %collective-permute-start.2 = (bf16[4,40,128]{2,1,0:T(8,128)(2,1)S(1)}, bf16[4,40,128]{2,1,0:T(8,128)(2,1)S(1)}, u32[]{:S(2)}, u32[]{:S(2)}) collective-permute-start(bf16[4,40,128]{2,1,0:T(8,128)(2,1)S(1)} %get-tuple-element.40), channel_id=1, source_target_pairs={{0,192},{64,256},{128,320},{192,384},{256,448},{320,0},{384,64},{4... | collective-permute-start | bytes 122888 | tf_op jit(solution)/shard_map/ppermute | solution.py:409
  71.1 13.6 %collective-permute-start.3 = (bf16[4,40,128]{2,1,0:T(8,128)(2,1)S(1)}, bf16[4,40,128]{2,1,0:T(8,128)(2,1)S(1)}, u32[]{:S(2)}, u32[]{:S(2)}) collective-permute-start(bf16[4,40,128]{2,1,0:T(8,128)(2,1)S(1)} %get-tuple-element.41), channel_id=1, source_target_pairs={{0,256},{64,320},{128,384},{192,448},{256,0},{320,64},{384,128},{4... | collective-permute-start | bytes 122888 | tf_op jit(solution)/shard_map/ppermute | solution.py:409
  75.1 12.7 %collective-permute-start.4 = (bf16[4,40,128]{2,1,0:T(8,128)(2,1)S(1)}, bf16[4,40,128]{2,1,0:T(8,128)(2,1)S(1)}, u32[]{:S(2)}, u32[]{:S(2)}) collective-permute-start(bf16[4,40,128]{2,1,0:T(8,128)(2,1)S(1)} %get-tuple-element.42), channel_id=1, source_target_pairs={{0,320},{64,384},{128,448},{192,0},{256,64},{320,128},{384,192},{4... | collective-permute-start | bytes 122888 | tf_op jit(solution)/shard_map/ppermute | solution.py:409
  79.4 8.4 %collective-permute-start.5 = (bf16[4,40,128]{2,1,0:T(8,128)(2,1)S(1)}, bf16[4,40,128]{2,1,0:T(8,128)(2,1)S(1)}, u32[]{:S(2)}, u32[]{:S(2)}) collective-permute-start(bf16[4,40,128]{2,1,0:T(8,128)(2,1)S(1)} %get-tuple-element.43), channel_id=1, source_target_pairs={{0,384},{64,448},{128,0},{192,64},{256,128},{320,192},{384,256},{4... | collective-permute-start | bytes 122888 | tf_op jit(solution)/shard_map/ppermute | solution.py:409
  84.7 5.0 %collective-permute-start.6 = (bf16[4,40,128]{2,1,0:T(8,128)(2,1)S(1)}, bf16[4,40,128]{2,1,0:T(8,128)(2,1)S(1)}, u32[]{:S(2)}, u32[]{:S(2)}) collective-permute-start(bf16[4,40,128]{2,1,0:T(8,128)(2,1)S(1)} %get-tuple-element.44), channel_id=1, source_target_pairs={{0,448},{64,0},{128,64},{192,128},{256,192},{320,256},{384,320},{4... | collective-permute-start | bytes 122888 | tf_op jit(solution)/shard_map/ppermute | solution.py:409
  142.1 9.5 %collective-permute-start.9 = (f32[40,128]{1,0:T(8,128)S(1)}, f32[40,128]{1,0:T(8,128)S(1)}, u32[]{:S(2)}, u32[]{:S(2)}) collective-permute-start(f32[40,128]{1,0:T(8,128)S(1)} %get-tuple-element.54), channel_id=1, source_target_pairs={{0,1},{1,2},{2,3},{3,4},{4,5},{5,6},{6,7},{7,8},{8,9},{9,10},{10,1... | collective-permute-start | bytes 61448 | tf_op jit(solution)/shard_map/ppermute | solution.py:389
  144.0 8.5 %collective-permute-start.10 = (f32[40,128]{1,0:T(8,128)S(1)}, f32[40,128]{1,0:T(8,128)S(1)}, u32[]{:S(2)}, u32[]{:S(2)}) collective-permute-start(f32[40,128]{1,0:T(8,128)S(1)} %get-tuple-element.55), channel_id=1, source_target_pairs={{1,0},{2,1},{3,2},{4,3},{5,4},{6,5},{7,6},{8,7},{9,8},{10,9},{11,1... | collective-permute-start | bytes 61448 | tf_op jit(solution)/shard_map/ppermute | solution.py:389
  165.5 18.9 %all-to-all-start.3 = ((bf16[8,5,40,128]{3,2,1,0:T(8,128)(2,1)}), bf16[8,5,40,128]{3,2,1,0:T(8,128)(2,1)S(1)}, u32[]{:S(2)}, u32[]{:S(2)}) async-start(bf16[8,5,40,128]{3,2,1,0:T(8,128)(2,1)} %shard_map.80), calls=%async_computation.3 | async-start | bytes 819200 | tf_op jit(solution)/shard_map/all_to_all | solution.py:446
  169.0 10.2 %collective-permute-start.11 = (f32[40,128]{1,0:T(8,128)S(1)}, f32[40,128]{1,0:T(8,128)S(1)}, u32[]{:S(2)}, u32[]{:S(2)}) collective-permute-start(f32[40,128]{1,0:T(8,128)S(1)} %get-tuple-element.59), channel_id=1, source_target_pairs={{0,1},{1,2},{2,3},{3,4},{4,5},{5,6},{6,7},{7,8},{8,9},{9,10},{10,1... | collective-permute-start | bytes 61448 | tf_op jit(solution)/shard_map/ppermute | solution.py:389
  170.9 9.1 %collective-permute-start.12 = (f32[40,128]{1,0:T(8,128)S(1)}, f32[40,128]{1,0:T(8,128)S(1)}, u32[]{:S(2)}, u32[]{:S(2)}) collective-permute-start(f32[40,128]{1,0:T(8,128)S(1)} %get-tuple-element.60), channel_id=1, source_target_pairs={{1,0},{2,1},{3,2},{4,3},{5,4},{6,5},{7,6},{8,7},{9,8},{10,9},{11,1... | collective-permute-start | bytes 61448 | tf_op jit(solution)/shard_map/ppermute | solution.py:389

commit v4 on v3

--- a/solution.py
+++ b/solution.py
@@ -9,6 +9,7 @@
 from jax.sharding import PartitionSpec as P
 
 STEPS = 3
+ROWS = 16
 COURANT = 0.2
 PAD = 40
 LABEL, LABEL_EAST = 64, 65
@@ -21,7 +22,7 @@
 F32, BF16 = jnp.float32, jnp.bfloat16
 
 
-def call(kernel, out_shape, in_specs, out_specs, scratch=(), vmem=40 << 20):
+def call(kernel, out_shape, in_specs, out_specs, scratch=(), vmem=24 << 20):
     return pl.pallas_call(
         kernel,
         out_shape=out_shape,
@@ -112,7 +113,7 @@
         copy.wait()
 
 
-def edges_kernel(levels, row_count, adj, turned, item, last_out, head_out):
+def edges_kernel(levels, row_count, match, turn, adj, turned, item, last_out, head_out):
     width = adj.shape[1]
     lane = lanes(PAD, width)
     last = jnp.zeros((PAD, width), F32)
@@ -130,49 +131,82 @@
             if r == 0:
                 item[f] = v.astype(BF16)
             if r == row_count - 1:
+                if f == 0:
+                    level = lax.broadcasted_iota(jnp.int32, v.shape, 0)
+                    v = jnp.where(level == levels, match[0, 0].astype(F32), v)
+                    v = jnp.where(level == levels + 1, turn[0, 0].astype(F32), v)
                 item[2 + f] = v.astype(BF16)
     last_out[...] = last
     head_out[...] = head
 
 
-def invert(code, inverse):
+def tail(tile, levels):
+    return tile[PAD - 8 : PAD, :].astype(F32)[levels - (PAD - 8) :, :]
+
+
+def first_send_kernel(sizes, levels, where, mates, *outs):
+    nz, ny, nc = sizes
+    zl, y, c = where[0, 0], where[0, 1], where[0, 2]
+    order = [(i, lax.rem(j + zl, nz)) for j in range(nz) for i in range(nc)]
+    shape = mates.shape[3:]
+    match = [jnp.broadcast_to(tail(mates[i, z, 2], levels)[0:1], shape) for i, z in order]
+    first = [[mates[i, z, f].astype(F32) for f in range(2)] for i, z in order]
+    for d, out in enumerate(outs):
+        dest = ((zl * ny + lax.rem(y + d, ny)) * nc + c).astype(F32)
+        for m, (i, z) in enumerate(order):
+            for f in range(2):
+                out[2 * m + f] = mates[i, z, 2 + f]
+        for f in range(2):
+            v = first[0][f]
+            for m in range(1, len(order)):
+                v = jnp.where(match[m] == dest, first[m][f], v)
+            out[2 * len(order) + f] = v.astype(BF16)
+
+
+def code_kernel(sizes, levels, where, edge, code):
+    nz, ny, nc = sizes
+    lane = lanes(1, code.shape[1])
+    codes = jnp.zeros(code.shape, F32)
+    for d in range(ny):
+        plane = lax.rem(where[0, 1] - d + ny, ny)
+        for m in range(nz * nc):
+            t = tail(edge[d, 2 * m], levels)
+            face = ((m // nc) * ny + plane) * nc + m % nc
+            codes = jnp.where(lane == face, 2.0 * t[0:1] + t[1:2], codes)
+    code[...] = codes.astype(jnp.int32)
+
+
+def invert(sizes, code, inverse):
     def one(f, c):
         inverse[lax.shift_right_logical(code[0, f], 1)] = f
         return c
 
-    lax.fori_loop(0, code.shape[1], one, 0)
-
-
-def choose_kernel(sizes, north_from, shifted, code, where, gathered, *refs):
+    lax.fori_loop(0, sizes[0] * sizes[1] * sizes[2], one, 0, unroll=8)
+
+
+def choose_kernel(sizes, north_from, code, where, gathered, out, inverse):
     _, ny, nc = sizes
-    outs, inverse = refs[:-1], refs[-1]
-    invert(code, inverse)
-    zl, y, c = where[0, 0], where[0, 1], where[0, 2]
+    invert(sizes, code, inverse)
+    zl, c = where[0, 0], where[0, 2]
     for d in range(ny):
-        plane = lax.rem(y + d, ny) if shifted else d
-        dest = (zl * ny + plane) * nc + c
+        dest = (zl * ny + d) * nc + c
         for source, a, b in (
             (inverse[dest], 0, north_from),
             (lax.shift_right_logical(code[0, dest], 1), north_from, gathered.shape[1]),
         ):
             group = (source // (ny * nc)) * nc + source % nc
             for i in range(a, b):
-                if shifted:
-                    outs[d][i] = gathered[group, i]
-                else:
-                    outs[0][d, i] = gathered[group, i]
-
-
-def neighbours(sizes, shifted, code, where, inverse):
+                out[d, i] = gathered[group, i]
+
+
+def neighbours(sizes, code, where, inverse):
     _, ny, nc = sizes
-    invert(code, inverse)
-    y = where[0, 1]
-    me = (where[0, 0] * ny + y) * nc + where[0, 2]
-    north, south = lax.shift_right_logical(code[0, me], 1), inverse[me]
-    north_plane, south_plane = (north // nc) % ny, (south // nc) % ny
-    if shifted:
-        north_plane, south_plane = lax.rem(y - north_plane + ny, ny), lax.rem(y - south_plane + ny, ny)
-    return north_plane, code[0, me] & 1, south_plane, code[0, south] & 1
+    invert(sizes, code, inverse)
+    me = (where[0, 0] * ny + where[0, 1]) * nc + where[0, 2]
+    found = []
+    for face, turn in ((lax.shift_right_logical(code[0, me], 1), code[0, me] & 1), (inverse[me], code[0, inverse[me]] & 1)):
+        found += [(face // nc) % ny, (face // (ny * nc)) * nc + face % nc, turn]
+    return found
 
 
 def oriented(block, turn):
@@ -208,23 +242,19 @@
     copy.wait()
 
 
-def advance(step, winds, found, east_wind, adj, final, upper, lower, south_end, from_west, from_east, put, sides):
-    row_count, width = adj.shape[0], adj.shape[3]
+def advance(step, rows, winds, found, east_wind, row, upper, lower, south_end, from_west, from_east, put):
+    row_count, width = ROWS, winds.shape[3]
     lane = lanes(PAD, width)
-    last = jnp.zeros((PAD, width), F32)
-    head = jnp.zeros((PAD, width), F32)
     base = step * row_count
 
-    def row(r, f):
-        return final[f] if final is not None and r == row_count - 1 else adj[r, f]
-
-    north_wind = winds[found[0, base], 1].astype(F32)
-    for r in range(row_count):
-        west_wind = winds[found[0, base + r], 0].astype(F32)
-        if r + 1 < row_count:
-            south_wind = winds[found[0, base + r + 1], 1].astype(F32)
-        else:
-            south_wind = south_end
+    def wind(r, i):
+        return winds[found[0, base + r], i].astype(F32)
+
+    south_wind, at = None, None
+    for r in rows:
+        west_wind = wind(r, 0)
+        north_wind = south_wind if at == r - 1 else wind(r, 1)
+        south_wind, at = (wind(r + 1, 1) if r + 1 < row_count else south_end), r
         eastern_wind = jnp.where(
             lane == width - 1, spread(east_wind, base + r, lane.shape), pltpu.roll(west_wind, width - 1, 1)
         )
@@ -244,61 +274,85 @@
             if south_wind is not None:
                 v = v + cs * ((row(r + 1, f) if r + 1 < row_count else lower[f]) - a)
             put(r, f, v)
-            if sides is not None:
-                last = jnp.where(lane == q, spread(v, width - 1, v.shape), last)
-                head = jnp.where(lane == q, spread(v, 0, v.shape), head)
-        north_wind = south_wind
-    if sides is not None:
-        sides[0][...] = last
-        sides[1][...] = head
+
+
+class Columns:
+    def __init__(self, width):
+        self.lane = lanes(PAD, width)
+        self.last = self.head = jnp.zeros((PAD, width), F32)
+
+    def add(self, r, f, v):
+        here = self.lane == r * 2 + f
+        self.last = jnp.where(here, spread(v, v.shape[1] - 1, v.shape), self.last)
+        self.head = jnp.where(here, spread(v, 0, v.shape), self.head)
+
+    def write(self, last_out, head_out):
+        last_out[...] = self.last
+        head_out[...] = self.head
 
 
 def first_kernel(
     step, levels, sizes,
     code, where, winds, adj, edge, from_west, from_east,
-    out, item, kept, last_out, head_out, found_out, east_wind,
+    item, kept, found_out, east_wind,
     inverse, found, sem,
 ):
-    row_count = adj.shape[0]
-    end = row_count - 1
+    end = adj.shape[0] - 1
+    mates = sizes[0] * sizes[2]
     find_slots(levels, winds, found_out, found, sem, east_wind)
-    north, turn_north, south, turn_south = neighbours(sizes, True, code, where, inverse)
-    upper = oriented(edge[north, 2:4], turn_north)
-    lower = oriented(edge[south, 0:2], turn_south)
+    north, north_mate, turn_north, south, _, turn_south = neighbours(sizes, code, where, inverse)
+    y, ny = where[0, 1], sizes[1]
+    upper = oriented(edge[lax.rem(y - north + ny, ny), pl.ds(2 * north_mate, 2)], turn_north)
+    lower = oriented(edge[lax.rem(y - south + ny, ny), 2 * mates : 2 * mates + 2], turn_south)
 
     def put(r, f, v):
-        out[r, f] = v
-        if r == 0:
-            item[f] = v.astype(BF16)
-        if r == end:
-            item[4 + f] = v.astype(BF16)
-            kept[9 + f] = v
-
-    advance(step, winds, found, east_wind, adj, None, upper, None, None, from_west, from_east, put, (last_out, head_out))
-    item[2] = winds[found[0, step * row_count], 1]
-    item[3] = winds[found[0, (step - 1) * row_count], 1]
+        item[f if r == 0 else 4 + f] = v.astype(BF16)
+        kept[(11 if r == 0 else 9) + f] = v
+
+    def row(r, f):
+        return adj[r, f]
+
+    advance(step, (0, end), winds, found, east_wind, row, upper, None, None, from_west, from_east, put)
+    item[2] = winds[found[0, step * ROWS], 1]
+    item[3] = winds[found[0, (step - 1) * ROWS], 1]
     kept[0:2] = upper
     kept[2:4] = lower
     kept[4:6] = adj[end]
     kept[6:8] = adj[0]
-    kept[8] = winds[found[0, step * row_count], 1].astype(F32)
+    kept[8] = winds[found[0, step * ROWS], 1].astype(F32)
+
+
+def inner_kernel(step, first_at, last_at, replaced, found, winds, adj, ends, from_west, from_east, east_wind, out, last_out, head_out):
+    row_count, width = adj.shape[0], adj.shape[3]
+    columns = Columns(width)
+
+    def put(r, f, v):
+        out[r, f] = v
+        columns.add(r, f, v)
+
+    def row(r, f):
+        return ends[f] if replaced and r == row_count - 1 else adj[r, f]
+
+    rows = range(1, row_count - 1)
+    advance(step, rows, winds, found, east_wind, row, None, None, None, from_west, from_east, put)
+    for f in range(2):
+        put(0, f, ends[first_at + f])
+        put(row_count - 1, f, ends[last_at + f])
+    columns.write(last_out, head_out)
 
 
 def mend_kernel(sizes, row_count, code, where, edge, kept, last_in, head_in, ends, last_out, head_out, inverse):
     width = kept.shape[2]
-    north, turn_north, south, turn_south = neighbours(sizes, False, code, where, inverse)
+    north, _, turn_north, south, _, turn_south = neighbours(sizes, code, where, inverse)
     lower = oriented(edge[south, 0:4], turn_south)
     cs = COURANT * jnp.maximum(lower[2], 0.0)
-    lane = lanes(PAD, width)
-    last, head = last_in[...], head_in[...]
+    columns = Columns(width)
+    columns.last, columns.head = last_in[...], head_in[...]
     for f in range(2):
         v = kept[9 + f] + cs * (kept[2 + f] - kept[4 + f])
         ends[f] = v
-        q = 2 * (row_count - 1) + f
-        last = jnp.where(lane == q, spread(v, width - 1, v.shape), last)
-        head = jnp.where(lane == q, spread(v, 0, v.shape), head)
-    last_out[...] = last
-    head_out[...] = head
+        columns.add(row_count - 1, f, v)
+    columns.write(last_out, head_out)
     upper = oriented(edge[north, 4:6], turn_north)
     cs = COURANT * jnp.maximum(kept[8], 0.0)
     for f in range(2):
@@ -309,37 +363,57 @@
     ends[6] = lower[3]
 
 
-def middle_kernel(step, found, winds, adj, ends, from_west, from_east, east_wind, out, item, last_out, head_out):
-    row_count = adj.shape[0]
+def middle_kernel(step, found, winds, adj, ends, from_west, from_east, east_wind, item, both):
+    end = adj.shape[0] - 1
 
     def put(r, f, v):
-        out[r, f] = v
-        if r == 0:
-            item[f] = v.astype(BF16)
-        if r == row_count - 1:
-            item[3 + f] = v.astype(BF16)
+        item[f if r == 0 else 3 + f] = v.astype(BF16)
+        both[(2 if r == 0 else 4) + f] = v
+
+    def row(r, f):
+        return ends[f] if r == end else adj[r, f]
 
     advance(
-        step, winds, found, east_wind, adj, (ends[0], ends[1]), (ends[2], ends[3]), (ends[4], ends[5]), ends[6],
-        from_west, from_east, put, (last_out, head_out),
+        step, (0, end), winds, found, east_wind, row, (ends[2], ends[3]), (ends[4], ends[5]), ends[6],
+        from_west, from_east, put,
     )
-    item[2] = winds[found[0, (step - 1) * row_count], 1]
+    both[0] = ends[0]
+    both[1] = ends[1]
+    item[2] = winds[found[0, (step - 1) * ROWS], 1]
+
+
+def late_kernel(step, found, winds, adj, from_west, from_east, east_wind, out):
+    rows = range(1, adj.shape[0] - 1)
+
+    def put(r, f, v):
+        out[r - 1, f] = v
+
+    def row(r, f):
+        return adj[r, f]
+
+    advance(step, rows, winds, found, east_wind, row, None, None, None, from_west, from_east, put)
 
 
 def last_kernel(
-    step, levels, sizes, code, where, found, winds, adj, edge, from_west, from_east, east_wind, out, inverse
+    step, levels, sizes, code, where, found, winds, adj, edge, from_west, from_east, east_wind, inner, out, inverse
 ):
-    row_count = adj.shape[0]
-    north, turn_north, south, turn_south = neighbours(sizes, False, code, where, inverse)
+    end = adj.shape[0] - 1
+    north, _, turn_north, south, _, turn_south = neighbours(sizes, code, where, inverse)
     upper = oriented(edge[north, 3:5], turn_north)
     lower = oriented(edge[south, 0:3], turn_south)
 
     def put(r, f, v):
         for l0 in range(0, levels, 8):
             n = min(8, levels - l0)
-            out[pl.ds((f * levels + l0) * row_count + r, n, stride=row_count), :] = v[l0 : l0 + n]
-
-    advance(step, winds, found, east_wind, adj, None, upper, lower, lower[2], from_west, from_east, put, None)
+            out[pl.ds((f * levels + l0) * ROWS + r, n, stride=ROWS), :] = v[l0 : l0 + n]
+
+    def row(r, f):
+        return adj[r, f]
+
+    for r in range(1, end):
+        for f in range(2):
+            put(r, f, inner[r - 1, f])
+    advance(step, (0, end), winds, found, east_wind, row, upper, lower, lower[2], from_west, from_east, put)
 
 
 def shards(sizes, tile_sizes, adjoint_end, stored_rows, stored_owner, stored_unit, stored_valid, edge_match, edge_turn):
@@ -352,9 +426,6 @@
     side = sds((PAD, width), F32)
 
     where = jnp.stack([lax.axis_index(a) for a in face]).astype(jnp.int32).reshape(1, 3)
-    code = edge_match * 2 + edge_turn
-    code = lax.all_to_all(jnp.broadcast_to(code, (faces, 1)), face, 0, 0, tiled=True).reshape(1, faces)
-
     payload = call(
         functools.partial(pack_kernel, levels, tiles),
         sds((slots, 2, PAD, width), BF16),
@@ -376,56 +447,67 @@
     turned, item, *sides = call(
         functools.partial(edges_kernel, levels, row_count),
         (sds((row_count, 2, PAD, width), F32), sds((4, PAD, width), BF16), side, side),
-        [VM],
+        [SM, SM, VM],
         (VM,) * 4,
-    )(adjoint_end.reshape(2 * levels * row_count, width))
+    )(edge_match, edge_turn, adjoint_end.reshape(2 * levels * row_count, width))
 
     inverse = pltpu.SMEM((faces,), jnp.int32)
-    planes = sizes[1]
+    planes, mates = sizes[1], sizes[0] * sizes[2]
 
     def to_sides(sides):
         ahead = [(i, (i + 1) % tiles) for i in range(tiles)]
         back = [((i + 1) % tiles, i) for i in range(tiles)]
         return lax.ppermute(sides[0], tile, ahead), lax.ppermute(sides[1], tile, back)
 
-    def gather(item):
-        return lax.all_gather(item, group, axis=0, tiled=False)
-
-    def chosen(mates, north_from, shifted):
-        shape_of_one = mates.shape[1:]
-        if shifted:
-            shape, spec = (sds(shape_of_one, BF16),) * planes, (VM,) * planes
-        else:
-            shape, spec = sds((planes,) + shape_of_one, BF16), VM
-        kernel = functools.partial(choose_kernel, sizes, north_from, shifted)
-        return call(kernel, shape, [SM, SM, VM], spec, [inverse])(code, where, mates)
-
-    payload, mates = lax.optimization_barrier((payload, gather(item)))
+    def exchange(item, north_from):
+        gathered = lax.all_gather(item, group, axis=0, tiled=False)
+        chosen = call(
+            functools.partial(choose_kernel, sizes, north_from),
+            sds((planes,) + item.shape, BF16),
+            [SM, SM, VM],
+            VM,
+            [inverse],
+        )(code, where, gathered)
+        return lax.all_to_all(chosen, "y", 0, 0, tiled=True)
+
+    other = lax.ppermute(item, "zl", [(i, (i + 1) % sizes[0]) for i in range(sizes[0])])
+    payload, other = lax.optimization_barrier((payload, other))
     winds = lax.all_to_all(payload, tile, 0, 0, tiled=True)
     from_west, from_east = to_sides(sides)
-    parts = chosen(mates, 2, True)
+    near = lax.all_gather(jnp.stack([item, other]), "c", axis=0, tiled=False)
+    parts = call(
+        functools.partial(first_send_kernel, sizes, levels),
+        (sds((2 * mates + 2, PAD, width), BF16),) * planes,
+        [SM, VM],
+        (VM,) * planes,
+    )(where, near)
     moved = [parts[0]]
     for d in range(1, planes):
         moved.append(lax.ppermute(parts[d], "y", [(i, (i + d) % planes) for i in range(planes)]))
     edge = jnp.stack(moved)
-
-    adj, item, kept, *sides, found, east_wind = call(
+    code = call(
+        functools.partial(code_kernel, sizes, levels), sds((1, width), jnp.int32), [SM, VM], VM
+    )(where, edge)
+
+    item, kept, found, east_wind = call(
         functools.partial(first_kernel, STEPS - 1, levels, sizes),
-        (
-            sds(turned.shape, F32),
-            sds((6, PAD, width), BF16),
-            sds((11, PAD, width), F32),
-            side,
-            side,
-            sds((1, width), jnp.int32),
-            side,
-        ),
+        (sds((6, PAD, width), BF16), sds((13, PAD, width), F32), sds((1, width), jnp.int32), side),
         [SM, SM] + [VM] * 5,
-        (VM,) * 7,
+        (VM,) * 4,
         [inverse, pltpu.SMEM((1, width), jnp.int32), pltpu.SemaphoreType.DMA],
     )(code, where, winds, turned, edge, from_west, from_east)
-
-    edge = lax.all_to_all(chosen(gather(item), 4, False), "y", 0, 0, tiled=True)
+    edge = exchange(item, 4)
+
+    def inner(step, first_at, last_at, replaced, adj, ends):
+        adj, *sides = call(
+            functools.partial(inner_kernel, step, first_at, last_at, replaced),
+            (sds(turned.shape, F32), side, side),
+            [SM] + [VM] * 6,
+            (VM,) * 3,
+        )(found, winds, adj, ends, from_west, from_east, east_wind)
+        return adj, sides
+
+    adj, sides = inner(STEPS - 1, 11, 9, False, turned, kept)
     ends, *sides = call(
         functools.partial(mend_kernel, sizes, row_count),
         (sds((7, PAD, width), F32), side, side),
@@ -435,22 +517,29 @@
     )(code, where, edge, kept, *sides)
 
     from_west, from_east = to_sides(sides)
-    adj, item, *sides = call(
+    item, both = call(
         functools.partial(middle_kernel, STEPS - 2),
-        (sds(turned.shape, F32), sds((5, PAD, width), BF16), side, side),
+        (sds((5, PAD, width), BF16), sds((6, PAD, width), F32)),
         [SM] + [VM] * 6,
-        (VM,) * 4,
+        (VM,) * 2,
     )(found, winds, adj, ends, from_west, from_east, east_wind)
+    edge = exchange(item, 3)
+    adj, sides = inner(STEPS - 2, 2, 4, True, adj, both)
 
     from_west, from_east = to_sides(sides)
-    edge = lax.all_to_all(chosen(gather(item), 3, False), "y", 0, 0, tiled=True)
+    late = call(
+        functools.partial(late_kernel, STEPS - 3),
+        sds((row_count - 2,) + turned.shape[1:], F32),
+        [SM] + [VM] * 5,
+        VM,
+    )(found, winds, adj, from_west, from_east, east_wind)
     out = call(
         functools.partial(last_kernel, STEPS - 3, levels, sizes),
         sds((2 * levels * row_count, width), F32),
-        [SM, SM, SM] + [VM] * 6,
+        [SM, SM, SM] + [VM] * 7,
         VM,
         [inverse],
-    )(code, where, found, winds, adj, edge, from_west, from_east, east_wind)
+    )(code, where, found, winds, adj, edge, from_west, from_east, east_wind, late)
     return out.reshape(adjoint_end.shape)
 
 

time: 188 us -> 171 us (0.910)
  the two profiles are of different devices: /device:TPU:9 before, /device:TPU:24 now
where the time goes in v4:
time: 171 us; the launch traced here: 170 us
  starting transfers between devices  97.8 us (57%)
  waiting for transfers between devices  25.6 us (15%)
  Pallas kernels  24.6 us (14%)
  blocking collectives  13.3 us (8%)
  local copies, waits for them, and re-layouts  6.87 us (4%)
    ppermute x7, starting transfers between devices, shards(): lax.ppermute(parts[d], 'y', [(i, (i + d) % planes) for i in range(planes)])  28.2 us
    all_to_all x1, starting transfers between devices, shards(): winds = lax.all_to_all(payload, tile, 0, 0, tiled=True)  20.4 us
    ppermute x3, starting transfers between devices, to_sides(): lax.ppermute(sides[1], tile, back)  19.8 us
    all_to_all x2, starting transfers between devices, exchange(): return lax.all_to_all(chosen, 'y', 0, 0, tiled=True)  13.3 us
    all_gather x2, blocking collectives, exchange(): gathered = lax.all_gather(item, group, axis=0, tiled=False)  11.4 us
    all_to_all x2, waiting for transfers between devices, exchange(): return lax.all_to_all(chosen, 'y', 0, 0, tiled=True)  11.2 us
    ppermute x3, starting transfers between devices, to_sides(): lax.ppermute(sides[0], tile, ahead)  10.9 us
    ppermute x7, waiting for transfers between devices, shards(): lax.ppermute(parts[d], 'y', [(i, (i + d) % planes) for i in range(planes)])  9.35 us
  transfers between devices with their start and end apart: 17, of which 8 were waited for; matrix products, arithmetic and copies ran while one was open for 2% of the time, Pallas kernels for 9%

profile of v4, /device:TPU:24, one launch (start us, length us, event | category | flops | bytes accessed | tf_op | source)
XLA Modules:
  0.0 169.9 jit_solution(1721715242776410669)
XLA Ops:
  2.9 5.2 %collective-permute-start = (bf16[4,40,128]{2,1,0:T(8,128)(2,1)S(1)}, bf16[4,40,128]{2,1,0:T(8,128)(2,1)S(1)}, u32[]{:S(2)}, u32[]{:S(2)}) collective-permute-start(bf16[4,40,128]{2,1,0:T(8,128)(2,1)S(1)} %get-tuple-element.34), channel_id=1, source_target_pairs={{0,512},{512,0},{1,513},{513,1},{2,514},{514,2},{3,515},{515,3},{4... | collective-permute-start | bytes 122888 | tf_op jit(solution)/shard_map/ppermute | solution.py:473
  8.1 3.1 %copy.11 = bf16[1,96,2,36,128]{4,3,2,1,0:T(8,128)(2,1)} copy(bf16[1,96,2,36,128]{4,2,3,1,0:T(2,128)(2,1)} %param.8) | data formatting | bytes 3538944 | tf_op args[1]
  11.2 4.9 %shard_map.74 = bf16[96,2,40,128]{3,2,1,0:T(8,128)(2,1)} custom-call(s32[1,96]{1,0:T(1,128)} %owner.1, s32[1,96]{1,0:T(1,128)} %unit.1, s32[1,96]{1,0:T(1,128)} %valid.1, bf16[96,2,36,128]{3,2,1,0:T(8,128)(2,1)} %bitcast.36), custom_call_target="tpu_custom_call" | custom-call | flops 1048576 | bytes 1048576 | tf_op jit(solution)/shard_map/pallas_call | solution.py:429
  16.1 20.4 %all-to-all-start = ((bf16[96,2,40,128]{3,2,1,0:T(8,128)(2,1)}), bf16[96,2,40,128]{3,2,1,0:T(8,128)(2,1)S(1)}, u32[]{:S(2)}, u32[]{:S(2)}) async-start(bf16[96,2,40,128]{3,2,1,0:T(8,128)(2,1)} %shard_map.74), calls=%async_computation | async-start | bytes 3932160 | tf_op jit(solution)/shard_map/all_to_all | solution.py:475
  36.5 4.3 %collective-permute-start.8 = (f32[40,128]{1,0:T(8,128)S(1)}, f32[40,128]{1,0:T(8,128)S(1)}, u32[]{:S(2)}, u32[]{:S(2)}) collective-permute-start(f32[40,128]{1,0:T(8,128)S(1)} %get-tuple-element.46), channel_id=1, source_target_pairs={{0,1},{1,2},{2,3},{3,4},{4,5},{5,6},{6,7},{7,8},{8,9},{9,10},{10,1... | collective-permute-start | bytes 61448 | tf_op jit(solution)/shard_map/ppermute | solution.py:460
  40.8 5.8 %collective-permute-start.9 = (f32[40,128]{1,0:T(8,128)S(1)}, f32[40,128]{1,0:T(8,128)S(1)}, u32[]{:S(2)}, u32[]{:S(2)}) collective-permute-start(f32[40,128]{1,0:T(8,128)S(1)} %get-tuple-element.47), channel_id=1, source_target_pairs={{1,0},{2,1},{3,2},{4,3},{5,4},{6,5},{7,6},{8,7},{9,8},{10,9},{11,1... | collective-permute-start | bytes 61448 | tf_op jit(solution)/shard_map/ppermute | solution.py:460
  49.3 3.6 %collective-permute-start.1 = (bf16[10,40,128]{2,1,0:T(8,128)(2,1)S(1)}, bf16[10,40,128]{2,1,0:T(8,128)(2,1)S(1)}, u32[]{:S(2)}, u32[]{:S(2)}) collective-permute-start(bf16[10,40,128]{2,1,0:T(8,128)(2,1)S(1)} %get-tuple-element.37), channel_id=1, source_target_pairs={{0,64},{64,128},{128,192},{192,256},{256,320},{320,384},{384,448},... | collective-permute-start | bytes 307208 | tf_op jit(solution)/shard_map/ppermute | solution.py:486
  52.9 5.9 %collective-permute-start.2 = (bf16[10,40,128]{2,1,0:T(8,128)(2,1)S(1)}, bf16[10,40,128]{2,1,0:T(8,128)(2,1)S(1)}, u32[]{:S(2)}, u32[]{:S(2)}) collective-permute-start(bf16[10,40,128]{2,1,0:T(8,128)(2,1)S(1)} %get-tuple-element.38), channel_id=1, source_target_pairs={{0,128},{64,192},{128,256},{192,320},{256,384},{320,448},{384,0},{... | collective-permute-start | bytes 307208 | tf_op jit(solution)/shard_map/ppermute | solution.py:486
  58.8 3.2 %collective-permute-start.3 = (bf16[10,40,128]{2,1,0:T(8,128)(2,1)S(1)}, bf16[10,40,128]{2,1,0:T(8,128)(2,1)S(1)}, u32[]{:S(2)}, u32[]{:S(2)}) collective-permute-start(bf16[10,40,128]{2,1,0:T(8,128)(2,1)S(1)} %get-tuple-element.39), channel_id=1, source_target_pairs={{0,192},{64,256},{128,320},{192,384},{256,448},{320,0},{384,64},{4... | collective-permute-start | bytes 307208 | tf_op jit(solution)/shard_map/ppermute | solution.py:486
  62.0 4.3 %collective-permute-start.4 = (bf16[10,40,128]{2,1,0:T(8,128)(2,1)S(1)}, bf16[10,40,128]{2,1,0:T(8,128)(2,1)S(1)}, u32[]{:S(2)}, u32[]{:S(2)}) collective-permute-start(bf16[10,40,128]{2,1,0:T(8,128)(2,1)S(1)} %get-tuple-element.40), channel_id=1, source_target_pairs={{0,256},{64,320},{128,384},{192,448},{256,0},{320,64},{384,128},{4... | collective-permute-start | bytes 307208 | tf_op jit(solution)/shard_map/ppermute | solution.py:486
  66.3 4.0 %collective-permute-start.5 = (bf16[10,40,128]{2,1,0:T(8,128)(2,1)S(1)}, bf16[10,40,128]{2,1,0:T(8,128)(2,1)S(1)}, u32[]{:S(2)}, u32[]{:S(2)}) collective-permute-start(bf16[10,40,128]{2,1,0:T(8,128)(2,1)S(1)} %get-tuple-element.41), channel_id=1, source_target_pairs={{0,320},{64,384},{128,448},{192,0},{256,64},{320,128},{384,192},{4... | collective-permute-start | bytes 307208 | tf_op jit(solution)/shard_map/ppermute | solution.py:486
  70.4 3.6 %collective-permute-done.3 = bf16[10,40,128]{2,1,0:T(8,128)(2,1)S(1)} collective-permute-done((bf16[10,40,128]{2,1,0:T(8,128)(2,1)S(1)}, bf16[10,40,128]{2,1,0:T(8,128)(2,1)S(1)}, u32[]{:S(2)}, u32[]{:S(2)}) %collective-permute-start.3) | collective-permute-done | bytes 102432 | tf_op jit(solution)/shard_map/ppermute | solution.py:486
  74.0 5.3 %collective-permute-start.6 = (bf16[10,40,128]{2,1,0:T(8,128)(2,1)S(1)}, bf16[10,40,128]{2,1,0:T(8,128)(2,1)S(1)}, u32[]{:S(2)}, u32[]{:S(2)}) collective-permute-start(bf16[10,40,128]{2,1,0:T(8,128)(2,1)S(1)} %get-tuple-element.42), channel_id=1, source_target_pairs={{0,384},{64,448},{128,0},{192,64},{256,128},{320,192},{384,256},{4... | collective-permute-start | bytes 307208 | tf_op jit(solution)/shard_map/ppermute | solution.py:486
  82.7 4.4 %collective-permute-done.7 = bf16[10,40,128]{2,1,0:T(8,128)(2,1)S(1)} collective-permute-done((bf16[10,40,128]{2,1,0:T(8,128)(2,1)S(1)}, bf16[10,40,128]{2,1,0:T(8,128)(2,1)S(1)}, u32[]{:S(2)}, u32[]{:S(2)}) %collective-permute-start.7) | collective-permute-done | bytes 102432 | tf_op jit(solution)/shard_map/ppermute | solution.py:486
  92.1 5.7 %all-gather.1 = bf16[24,40,128]{2,1,0:T(8,128)(2,1)S(1)} all-gather(bf16[6,40,128]{2,1,0:T(8,128)(2,1)S(1)} %get-tuple-element.52), channel_id=3, replica_groups=mesh['zl'=2,'y'=8,'c'=2,'x'=8,'zh'=4] {'zl','c'}, dimensions={0}, use_global_device_ids=true | all-gather | bytes 307200 | tf_op jit(solution)/shard_map/all_gather | solution.py:463
  99.4 7.9 %all-to-all-start.1 = ((bf16[8,6,40,128]{3,2,1,0:T(8,128)(2,1)}), bf16[8,6,40,128]{3,2,1,0:T(8,128)(2,1)}, u32[]{:S(2)}, u32[]{:S(2)}) async-start(bf16[8,6,40,128]{3,2,1,0:T(8,128)(2,1)} %shard_map.79), calls=%async_computation.1 | async-start | bytes 983040 | tf_op jit(solution)/shard_map/all_to_all | solution.py:471
  108.2 3.8 %shard_map.78 = (f32[16,2,40,128]{3,2,1,0:T(8,128)S(1)}, f32[40,128]{1,0:T(8,128)S(1)}, f32[40,128]{1,0:T(8,128)S(1)}) custom-call(s32[1,128]{1,0:T(1,128)S(1)} %get-tuple-element.48.found, bf16[96,2,40,128]{3,2,1,0:T(8,128)(2,1)S(1)} %all-to-all-done.winds, f32[16,2,40,128]{3,2,1,0:T(8,128)S(1)} %get-tuple-element.45.adj, f32[13,40,128]{2,1,0:T(8,128)S(1)} %copy-done.1, ...), custom_call_target="tpu_custom_call" | custom-call | flops 1048576 | bytes 1048576 | tf_op jit(solution)/shard_map/pallas_call | solution.py:502
  112.0 11.2 %all-to-all-done.1.edge = bf16[8,6,40,128]{3,2,1,0:T(8,128)(2,1)} async-done(((bf16[8,6,40,128]{3,2,1,0:T(8,128)(2,1)}), bf16[8,6,40,128]{3,2,1,0:T(8,128)(2,1)}, u32[]{:S(2)}, u32[]{:S(2)}) %all-to-all-start.1) | async-done | bytes 491552 | tf_op jit(solution)/shard_map/all_to_all | solution.py:471
  125.5 4.2 %collective-permute-start.10 = (f32[40,128]{1,0:T(8,128)S(1)}, f32[40,128]{1,0:T(8,128)S(1)}, u32[]{:S(2)}, u32[]{:S(2)}) collective-permute-start(f32[40,128]{1,0:T(8,128)S(1)} %get-tuple-element.56), channel_id=1, source_target_pairs={{0,1},{1,2},{2,3},{3,4},{4,5},{5,6},{6,7},{7,8},{8,9},{9,10},{10,1... | collective-permute-start | bytes 61448 | tf_op jit(solution)/shard_map/ppermute | solution.py:460
  129.7 5.9 %collective-permute-start.11 = (f32[40,128]{1,0:T(8,128)S(1)}, f32[40,128]{1,0:T(8,128)S(1)}, u32[]{:S(2)}, u32[]{:S(2)}) collective-permute-start(f32[40,128]{1,0:T(8,128)S(1)} %get-tuple-element.57), channel_id=1, source_target_pairs={{1,0},{2,1},{3,2},{4,3},{5,4},{6,5},{7,6},{8,7},{9,8},{10,9},{11,1... | collective-permute-start | bytes 61448 | tf_op jit(solution)/shard_map/ppermute | solution.py:460
  137.8 5.6 %all-gather.2 = bf16[20,40,128]{2,1,0:T(8,128)(2,1)S(1)} all-gather(bf16[5,40,128]{2,1,0:T(8,128)(2,1)S(1)} %get-tuple-element.60), channel_id=4, replica_groups=mesh['zl'=2,'y'=8,'c'=2,'x'=8,'zh'=4] {'zl','c'}, dimensions={0}, use_global_device_ids=true | all-gather | bytes 256000 | tf_op jit(solution)/shard_map/all_gather | solution.py:463
  144.9 5.4 %all-to-all-start.2 = ((bf16[8,5,40,128]{3,2,1,0:T(8,128)(2,1)}), bf16[8,5,40,128]{3,2,1,0:T(8,128)(2,1)}, u32[]{:S(2)}, u32[]{:S(2)}) async-start(bf16[8,5,40,128]{3,2,1,0:T(8,128)(2,1)} %shard_map.83), calls=%async_computation.2 | async-start | bytes 819200 | tf_op jit(solution)/shard_map/all_to_all | solution.py:471
  150.3 3.8 %shard_map.82 = (f32[16,2,40,128]{3,2,1,0:T(8,128)S(1)}, f32[40,128]{1,0:T(8,128)S(1)}, f32[40,128]{1,0:T(8,128)S(1)}) custom-call(s32[1,128]{1,0:T(1,128)S(1)} %get-tuple-element.48.found, bf16[96,2,40,128]{3,2,1,0:T(8,128)(2,1)S(1)} %all-to-all-done.winds, f32[16,2,40,128]{3,2,1,0:T(8,128)S(1)} %get-tuple-element.51.adj, ...), custom_call_target="tpu_custom_call" | custom-call | flops 1048576 | bytes 1048576 | tf_op jit(solution)/shard_map/pallas_call | solution.py:502
  156.5 8.1 %collective-permute-start.13 = (f32[40,128]{1,0:T(8,128)S(1)}, f32[40,128]{1,0:T(8,128)S(1)}, u32[]{:S(2)}, u32[]{:S(2)}) collective-permute-start(f32[40,128]{1,0:T(8,128)S(1)} %get-tuple-element.62), channel_id=1, source_target_pairs={{1,0},{2,1},{3,2},{4,3},{5,4},{6,5},{7,6},{8,7},{9,8},{10,9},{11,1... | collective-permute-start | bytes 61448 | tf_op jit(solution)/shard_map/ppermute | solution.py:460
  (45 shorter events, 28.7 us)
Async XLA Ops:
  1.3 1.1 copy-start.3
  2.9 13.2 %collective-permute-start = (bf16[4,40,128]{2,1,0:T(8,128)(2,1)S(1)}, bf16[4,40,128]{2,1,0:T(8,128)(2,1)S(1)}, u32[]{:S(2)}, u32[]{:S(2)}) collective-permute-start(bf16[4,40,128]{2,1,0:T(8,128)(2,1)S(1)} %get-tuple-element.34), channel_id=1, source_target_pairs={{0,512},{512,0},{1,513},{513,1},{2,514},{514,2},{3,515},{515,3},{4... | collective-permute-start | bytes 122888 | tf_op jit(solution)/shard_map/ppermute | solution.py:473
  16.1 73.7 %all-to-all-start = ((bf16[96,2,40,128]{3,2,1,0:T(8,128)(2,1)}), bf16[96,2,40,128]{3,2,1,0:T(8,128)(2,1)S(1)}, u32[]{:S(2)}, u32[]{:S(2)}) async-start(bf16[96,2,40,128]{3,2,1,0:T(8,128)(2,1)} %shard_map.74), calls=%async_computation | async-start | bytes 3932160 | tf_op jit(solution)/shard_map/all_to_all | solution.py:475
  36.5 51.2 %collective-permute-start.8 = (f32[40,128]{1,0:T(8,128)S(1)}, f32[40,128]{1,0:T(8,128)S(1)}, u32[]{:S(2)}, u32[]{:S(2)}) collective-permute-start(f32[40,128]{1,0:T(8,128)S(1)} %get-tuple-element.46), channel_id=1, source_target_pairs={{0,1},{1,2},{2,3},{3,4},{4,5},{5,6},{6,7},{7,8},{8,9},{9,10},{10,1... | collective-permute-start | bytes 61448 | tf_op jit(solution)/shard_map/ppermute | solution.py:460
  40.8 46.9 %collective-permute-start.9 = (f32[40,128]{1,0:T(8,128)S(1)}, f32[40,128]{1,0:T(8,128)S(1)}, u32[]{:S(2)}, u32[]{:S(2)}) collective-permute-start(f32[40,128]{1,0:T(8,128)S(1)} %get-tuple-element.47), channel_id=1, source_target_pairs={{1,0},{2,1},{3,2},{4,3},{5,4},{6,5},{7,6},{8,7},{9,8},{10,9},{11,1... | collective-permute-start | bytes 61448 | tf_op jit(solution)/shard_map/ppermute | solution.py:460
  49.3 12.7 %collective-permute-start.1 = (bf16[10,40,128]{2,1,0:T(8,128)(2,1)S(1)}, bf16[10,40,128]{2,1,0:T(8,128)(2,1)S(1)}, u32[]{:S(2)}, u32[]{:S(2)}) collective-permute-start(bf16[10,40,128]{2,1,0:T(8,128)(2,1)S(1)} %get-tuple-element.37), channel_id=1, source_target_pairs={{0,64},{64,128},{128,192},{192,256},{256,320},{320,384},{384,448},... | collective-permute-start | bytes 307208 | tf_op jit(solution)/shard_map/ppermute | solution.py:486
  52.9 13.4 %collective-permute-start.2 = (bf16[10,40,128]{2,1,0:T(8,128)(2,1)S(1)}, bf16[10,40,128]{2,1,0:T(8,128)(2,1)S(1)}, u32[]{:S(2)}, u32[]{:S(2)}) collective-permute-start(bf16[10,40,128]{2,1,0:T(8,128)(2,1)S(1)} %get-tuple-element.38), channel_id=1, source_target_pairs={{0,128},{64,192},{128,256},{192,320},{256,384},{320,448},{384,0},{... | collective-permute-start | bytes 307208 | tf_op jit(solution)/shard_map/ppermute | solution.py:486
  58.8 15.2 %collective-permute-start.3 = (bf16[10,40,128]{2,1,0:T(8,128)(2,1)S(1)}, bf16[10,40,128]{2,1,0:T(8,128)(2,1)S(1)}, u32[]{:S(2)}, u32[]{:S(2)}) collective-permute-start(bf16[10,40,128]{2,1,0:T(8,128)(2,1)S(1)} %get-tuple-element.39), channel_id=1, source_target_pairs={{0,192},{64,256},{128,320},{192,384},{256,448},{320,0},{384,64},{4... | collective-permute-start | bytes 307208 | tf_op jit(solution)/shard_map/ppermute | solution.py:486
  62.0 17.3 %collective-permute-start.4 = (bf16[10,40,128]{2,1,0:T(8,128)(2,1)S(1)}, bf16[10,40,128]{2,1,0:T(8,128)(2,1)S(1)}, u32[]{:S(2)}, u32[]{:S(2)}) collective-permute-start(bf16[10,40,128]{2,1,0:T(8,128)(2,1)S(1)} %get-tuple-element.40), channel_id=1, source_target_pairs={{0,256},{64,320},{128,384},{192,448},{256,0},{320,64},{384,128},{4... | collective-permute-start | bytes 307208 | tf_op jit(solution)/shard_map/ppermute | solution.py:486
  66.3 15.6 %collective-permute-start.5 = (bf16[10,40,128]{2,1,0:T(8,128)(2,1)S(1)}, bf16[10,40,128]{2,1,0:T(8,128)(2,1)S(1)}, u32[]{:S(2)}, u32[]{:S(2)}) collective-permute-start(bf16[10,40,128]{2,1,0:T(8,128)(2,1)S(1)} %get-tuple-element.41), channel_id=1, source_target_pairs={{0,320},{64,384},{128,448},{192,0},{256,64},{320,128},{384,192},{4... | collective-permute-start | bytes 307208 | tf_op jit(solution)/shard_map/ppermute | solution.py:486
  74.0 8.7 %collective-permute-start.6 = (bf16[10,40,128]{2,1,0:T(8,128)(2,1)S(1)}, bf16[10,40,128]{2,1,0:T(8,128)(2,1)S(1)}, u32[]{:S(2)}, u32[]{:S(2)}) collective-permute-start(bf16[10,40,128]{2,1,0:T(8,128)(2,1)S(1)} %get-tuple-element.42), channel_id=1, source_target_pairs={{0,384},{64,448},{128,0},{192,64},{256,128},{320,192},{384,256},{4... | collective-permute-start | bytes 307208 | tf_op jit(solution)/shard_map/ppermute | solution.py:486
  79.4 7.7 %collective-permute-start.7 = (bf16[10,40,128]{2,1,0:T(8,128)(2,1)S(1)}, bf16[10,40,128]{2,1,0:T(8,128)(2,1)S(1)}, u32[]{:S(2)}, u32[]{:S(2)}) collective-permute-start(bf16[10,40,128]{2,1,0:T(8,128)(2,1)S(1)} %get-tuple-element.43), channel_id=1, source_target_pairs={{0,448},{64,0},{128,64},{192,128},{256,192},{320,256},{384,320},{4... | collective-permute-start | bytes 307208 | tf_op jit(solution)/shard_map/ppermute | solution.py:486
  91.4 0.7 copy-start
  99.4 23.8 %all-to-all-start.1 = ((bf16[8,6,40,128]{3,2,1,0:T(8,128)(2,1)}), bf16[8,6,40,128]{3,2,1,0:T(8,128)(2,1)}, u32[]{:S(2)}, u32[]{:S(2)}) async-start(bf16[8,6,40,128]{3,2,1,0:T(8,128)(2,1)} %shard_map.79), calls=%async_computation.1 | async-start | bytes 983040 | tf_op jit(solution)/shard_map/all_to_all | solution.py:471
  107.2 1.0 copy-start.1
  123.2 1.0 copy-start.2
  125.5 10.1 %collective-permute-start.10 = (f32[40,128]{1,0:T(8,128)S(1)}, f32[40,128]{1,0:T(8,128)S(1)}, u32[]{:S(2)}, u32[]{:S(2)}) collective-permute-start(f32[40,128]{1,0:T(8,128)S(1)} %get-tuple-element.56), channel_id=1, source_target_pairs={{0,1},{1,2},{2,3},{3,4},{4,5},{5,6},{6,7},{7,8},{8,9},{9,10},{10,1... | collective-permute-start | bytes 61448 | tf_op jit(solution)/shard_map/ppermute | solution.py:460
  129.7 7.4 %collective-permute-start.11 = (f32[40,128]{1,0:T(8,128)S(1)}, f32[40,128]{1,0:T(8,128)S(1)}, u32[]{:S(2)}, u32[]{:S(2)}) collective-permute-start(f32[40,128]{1,0:T(8,128)S(1)} %get-tuple-element.57), channel_id=1, source_target_pairs={{1,0},{2,1},{3,2},{4,3},{5,4},{6,5},{7,6},{8,7},{9,8},{10,9},{11,1... | collective-permute-start | bytes 61448 | tf_op jit(solution)/shard_map/ppermute | solution.py:460
  144.9 22.7 %all-to-all-start.2 = ((bf16[8,5,40,128]{3,2,1,0:T(8,128)(2,1)}), bf16[8,5,40,128]{3,2,1,0:T(8,128)(2,1)}, u32[]{:S(2)}, u32[]{:S(2)}) async-start(bf16[8,5,40,128]{3,2,1,0:T(8,128)(2,1)} %shard_map.83), calls=%async_computation.2 | async-start | bytes 819200 | tf_op jit(solution)/shard_map/all_to_all | solution.py:471
  154.1 10.6 %collective-permute-start.12 = (f32[40,128]{1,0:T(8,128)S(1)}, f32[40,128]{1,0:T(8,128)S(1)}, u32[]{:S(2)}, u32[]{:S(2)}) collective-permute-start(f32[40,128]{1,0:T(8,128)S(1)} %get-tuple-element.61), channel_id=1, source_target_pairs={{0,1},{1,2},{2,3},{3,4},{4,5},{5,6},{6,7},{7,8},{8,9},{9,10},{10,1... | collective-permute-start | bytes 61448 | tf_op jit(solution)/shard_map/ppermute | solution.py:460
  156.5 9.6 %collective-permute-start.13 = (f32[40,128]{1,0:T(8,128)S(1)}, f32[40,128]{1,0:T(8,128)S(1)}, u32[]{:S(2)}, u32[]{:S(2)}) collective-permute-start(f32[40,128]{1,0:T(8,128)S(1)} %get-tuple-element.62), channel_id=1, source_target_pairs={{1,0},{2,1},{3,2},{4,3},{5,4},{6,5},{7,6},{8,7},{9,8},{10,9},{11,1... | collective-permute-start | bytes 61448 | tf_op jit(solution)/shard_map/ppermute | solution.py:460

commit v5 on v4

v5 whole, which is shorter than its diff:
```python
import functools

import jax
import jax.numpy as jnp
from jax import lax
from jax.experimental import pallas as pl
from jax.experimental.pallas import tpu as pltpu
from jax.sharding import Mesh
from jax.sharding import PartitionSpec as P

STEPS = 3
ROWS = 16
CAPACITY = 3
COURANT = 0.2
PAD = 40
LABEL, LABEL_EAST = 64, 65
CHUNKS = 4
HALF = 64
MATCH, TURN = 40, 41
EDGE_COLUMN = 32
INTERPRET = False

VM = pl.BlockSpec(memory_space=pltpu.VMEM)
SM = pl.BlockSpec(memory_space=pltpu.SMEM)
HBM = pl.BlockSpec(memory_space=pltpu.HBM)
F32, BF16 = jnp.float32, jnp.bfloat16


def call(kernel, out_shape, in_specs, out_specs, scratch=(), vmem=24 << 20):
    return pl.pallas_call(
        kernel,
        out_shape=out_shape,
        in_specs=in_specs,
        out_specs=out_specs,
        scratch_shapes=list(scratch),
        compiler_params=pltpu.CompilerParams(vmem_limit_bytes=vmem),
        cost_estimate=pl.CostEstimate(flops=1 << 20, bytes_accessed=1 << 20, transcendentals=0),
        interpret=INTERPRET,
    )


def lanes(rows, width):
    return lax.broadcasted_iota(jnp.int32, (rows, width), 1)


def spread(values, lane, shape):
    return jnp.broadcast_to(values[:, lane : lane + 1], shape)


def pack_kernel(
    levels, tiles, edge_unit, owner, unit, valid, rows, sent, count, source, label, first, flat, corner, out, sem_out
):
    slots, width = rows.shape[0], rows.shape[3]
    capacity = slots // tiles
    block = out.shape[0] // tiles
    whole = levels // 8 * 8

    def clear(i, c):
        count[i] = 0
        first[i] = -1
        return c

    lax.fori_loop(0, tiles, clear, 0, unroll=8)

    def blank(i, c):
        source[i] = 0
        label[i] = -1
        return c

    lax.fori_loop(0, slots, blank, 0, unroll=8)

    def place(s, c):
        @pl.when(valid[0, s] == 1)
        def _():
            o, u = owner[0, s], unit[0, s]
            p = o * capacity + count[o]
            source[p] = s
            label[p] = u
            count[o] = count[o] + 1

            @pl.when(u == edge_unit)
            def _():
                first[o] = s

        return c

    lax.fori_loop(0, slots, place, 0, unroll=4)

    lane = lanes(levels, width)

    def column(s, held):
        v = rows[s, 0].astype(F32)
        return jnp.where(lane == s, spread(v, 0, v.shape), held)

    def corners(o, held):
        v = rows[jnp.maximum(first[o], 0), 1].astype(F32)
        held = jnp.where(lane == o, spread(v, 0, v.shape), held)
        return jnp.where(lane == tiles + o, spread(v, width - 1, v.shape), held)

    for ref, one, n in ((flat, column, slots), (corner, corners, tiles)):
        held = lax.fori_loop(0, n, one, jnp.zeros((levels, width), F32), unroll=8)
        ref[...] = jnp.zeros_like(ref)
        ref[0:levels, :] = held
        ref[...] = ref[...].T

    extra_lane = lanes(8, width)
    extra_row = lax.broadcasted_iota(jnp.int32, (8, width), 0)

    def at(ref, i):
        return jnp.broadcast_to(ref[pl.ds(i, 1), :], (8, width))

    def fill(o, c):
        base = o * block
        east = jnp.where(o + 1 == tiles, 0, o + 1)
        west = jnp.where(o == 0, tiles - 1, o - 1)
        extra = jnp.zeros((8, width), F32)
        for i in range(capacity):
            p, q = o * capacity + i, east * capacity + i
            s = source[p]
            at_slot = base + i * (2 * levels // 8)
            for j in range(2):
                v = rows[s, j, 0:whole].astype(F32).reshape(whole // 8, 8, width)
                out[pl.ds(at_slot + j * (whole // 8), whole // 8)] = v.astype(BF16)
            rest = [rows[s, j, whole:levels].astype(F32) for j in range(2)]
            out[at_slot + 2 * whole // 8] = jnp.concatenate(rest, axis=0).astype(BF16)
            line = at(flat, source[q])
            line = jnp.where(extra_lane == LABEL, label[p].astype(F32), line)
            line = jnp.where(extra_lane == LABEL_EAST, label[q].astype(F32), line)
            extra = jnp.where(extra_row == i, line, extra)
        for i, side in ((capacity, east), (capacity + 1, west)):
            line = jnp.where(extra_lane < HALF, at(corner, side), pltpu.roll(at(corner, tiles + side), HALF, 1))
            line = jnp.where(extra_lane == width - 1, jnp.where(first[side] >= 0, 1.0, 0.0), line)
            extra = jnp.where(extra_row == i, line, extra)
        out[base + block - 1] = extra.astype(BF16)
        return c

    chunk = tiles // CHUNKS
    copies = []
    for i in range(CHUNKS):
        lax.fori_loop(i * chunk, (i + 1) * chunk, fill, 0)
        span = pl.ds(i * chunk * block, chunk * block)
        copies.append(pltpu.make_async_copy(out.at[span], sent.at[span], sem_out.at[i]))
        copies[-1].start()
    for copy in copies:
        copy.wait()


def edges_kernel(levels, row_count, match, turn, adj, turned, item, last_out, head_out):
    width = adj.shape[1]
    lane = lanes(PAD, width)
    last = jnp.zeros((PAD, width), F32)
    head = jnp.zeros((PAD, width), F32)
    for r in range(row_count):
        for f in range(2):
            for l0 in range(0, levels, 8):
                n = min(8, levels - l0)
                turned[r, f, l0 : l0 + n, :] = adj[pl.ds((f * levels + l0) * row_count + r, n, stride=row_count), :]
            turned[r, f, levels:PAD, :] = jnp.zeros((PAD - levels, width), F32)
            v = turned[r, f]
            q = r * 2 + f
            last = jnp.where(lane == q, spread(v, width - 1, v.shape), last)
            head = jnp.where(lane == q, spread(v, 0, v.shape), head)
            if r == 0:
                item[f] = v.astype(BF16)
            if r == row_count - 1:
                if f == 0:
                    level = lax.broadcasted_iota(jnp.int32, v.shape, 0)
                    v = jnp.where(level == levels, match[0, 0].astype(F32), v)
                    v = jnp.where(level == levels + 1, turn[0, 0].astype(F32), v)
                item[2 + f] = v.astype(BF16)
    for out, v in ((last_out, last), (head_out, head)):
        v = jnp.where(lane == MATCH, match[0, 0].astype(F32), v)
        out[...] = jnp.where(lane == TURN, turn[0, 0].astype(F32), v)


def tail(tile, levels):
    return tile[PAD - 8 : PAD, :].astype(F32)[levels - (PAD - 8) :, :]


def first_send_kernel(sizes, levels, where, mates, *outs):
    nz, ny, nc = sizes
    zl, y, c = where[0, 0], where[0, 1], where[0, 2]
    order = [(i, lax.rem(j + zl, nz)) for j in range(nz) for i in range(nc)]
    shape = mates.shape[3:]
    match = [jnp.broadcast_to(tail(mates[i, z, 2], levels)[0:1], shape) for i, z in order]
    first = [[mates[i, z, f].astype(F32) for f in range(2)] for i, z in order]
    for d, out in enumerate(outs):
        dest = ((zl * ny + lax.rem(y + d, ny)) * nc + c).astype(F32)
        for m, (i, z) in enumerate(order):
            for f in range(2):
                out[2 * m + f] = mates[i, z, 2 + f]
        for f in range(2):
            v = first[0][f]
            for m in range(1, len(order)):
                v = jnp.where(match[m] == dest, first[m][f], v)
            out[2 * len(order) + f] = v.astype(BF16)


def code_kernel(sizes, levels, where, edge, code, inverse):
    nz, ny, nc = sizes
    lane = lanes(1, code.shape[1])
    codes = jnp.zeros(code.shape, F32)
    south = jnp.zeros(code.shape, jnp.int32)
    for d in range(ny):
        plane = lax.rem(where[0, 1] - d + ny, ny)
        for m in range(nz * nc):
            t = tail(edge[d, 2 * m], levels)
            face = ((m // nc) * ny + plane) * nc + m % nc
            codes = jnp.where(lane == face, 2.0 * t[0:1] + t[1:2], codes)
            south = jnp.where(lane.astype(F32) == t[0:1], face, south)
    code[...] = codes.astype(jnp.int32)
    inverse[...] = south


def choose_kernel(sizes, levels, north_from, rows, code, inverse, where, gathered, out):
    _, ny, nc = sizes
    zl, c = where[0, 0], where[0, 2]
    if gathered.shape[1] > rows:
        corner = [gathered[m, rows].astype(F32) for m in range(gathered.shape[0])]
        shape = corner[0].shape
        lane = lanes(*shape)
        to = [[jnp.broadcast_to(tail(k, levels)[i : i + 1], shape) for i in range(2)] for k in corner]
    for d in range(ny):
        dest = (zl * ny + d) * nc + c
        for source, a, b in (
            (inverse[0, dest], 0, north_from),
            (lax.shift_right_logical(code[0, dest], 1), north_from, rows),
        ):
            group = (source // (ny * nc)) * nc + source % nc
            for i in range(a, b):
                out[d, i] = gathered[group, i]
        if gathered.shape[1] > rows:
            v = jnp.zeros(shape, F32)
            for k, both in zip(corner, to):
                for i in range(2):
                    hit = both[i] == dest.astype(F32)
                    v = jnp.where(hit & (lane == i), k, v)
                    v = jnp.where(hit & (lane == 2 + i), 1.0, v)
            out[d, rows] = v.astype(BF16)


def neighbours(sizes, code, inverse, where):
    _, ny, nc = sizes
    me = (where[0, 0] * ny + where[0, 1]) * nc + where[0, 2]
    south = inverse[0, me]
    found = []
    for face, turn in ((lax.shift_right_logical(code[0, me], 1), code[0, me] & 1), (south, code[0, south] & 1)):
        found += [(face // nc) % ny, (face // (ny * nc)) * nc + face % nc, turn]
    return found


def oriented(block, turn):
    n, rows, width = block.shape
    i = lax.broadcasted_iota(jnp.int32, (width, width), 0)
    j = lax.broadcasted_iota(jnp.int32, (width, width), 1)
    source = jnp.where(turn == 1, width - 1 - j, j)
    matrix = jnp.where(i == source, 1.0, 0.0).astype(BF16)
    out = jnp.dot(block.reshape(n * rows, width), matrix, preferred_element_type=F32)
    return out.reshape(n, rows, width)


def find_slots(levels, tiles, capacity, winds, found_out, found, sem, extras):
    block = winds.shape[0] // tiles
    extra = jnp.concatenate([winds[h * block + block - 1].astype(F32) for h in range(tiles)], axis=0)
    row = lax.broadcasted_iota(jnp.int32, extra.shape, 0)
    holder, at = lax.shift_right_logical(row, 3), row & 7
    lane = lanes(*extra.shape)
    here = (at < capacity) & (spread(extra, LABEL, extra.shape) == lane.astype(F32))
    there = (at < capacity) & (spread(extra, LABEL_EAST, extra.shape) == lane.astype(F32))
    sides = (at - capacity == lane - HALF) & (at >= capacity) & (at < capacity + 2)
    there = there | (sides & (spread(extra, extra.shape[1] - 1, extra.shape) > 0.5))
    place = (holder * block + at * (2 * levels // 8)).astype(F32)
    index = jnp.sum(jnp.where(here, place, 0.0), axis=0, keepdims=True)
    found_out[...] = index.astype(jnp.int32)
    copy = pltpu.make_async_copy(found_out, found, sem)
    copy.start()
    extras[...] = lax.dot_general(
        extra.astype(BF16), jnp.where(there, 1.0, 0.0).astype(BF16), (((0,), (0,)), ((), ())), preferred_element_type=F32
    )
    copy.wait()


def wind(levels, winds, found, unit, i):
    whole = levels // 8 * 8
    base = found[0, unit]
    rest = winds[base + 2 * whole // 8].astype(F32)
    if i == 1:
        rest = pltpu.roll(rest, 8 - (levels - whole), 0)
    main = winds[pl.ds(base + i * (whole // 8), whole // 8)].astype(F32).reshape(whole, rest.shape[1])
    return jnp.concatenate([main, rest], axis=0)


def advance(step, rows, levels, winds, found, east_wind, row, upper, lower, south_end, from_west, from_east, put):
    row_count, width = ROWS, winds.shape[2]
    lane = lanes(PAD, width)
    base = step * row_count

    def of(r, i):
        return wind(levels, winds, found, base + r, i)

    south_wind, at = None, None
    for r in rows:
        west_wind = of(r, 0)
        north_wind = south_wind if at == r - 1 else of(r, 1)
        south_wind, at = (of(r + 1, 1) if r + 1 < row_count else south_end), r
        eastern_wind = jnp.where(
            lane == width - 1, spread(east_wind, base + r, lane.shape), pltpu.roll(west_wind, width - 1, 1)
        )
        cw = COURANT * jnp.minimum(west_wind, 0.0)
        ce = COURANT * jnp.maximum(eastern_wind, 0.0)
        cn = COURANT * jnp.minimum(north_wind, 0.0)
        if south_wind is not None:
            cs = COURANT * jnp.maximum(south_wind, 0.0)
        for f in range(2):
            q = r * 2 + f
            a = row(r, f)
            west = jnp.where(lane == 0, spread(from_west, q, a.shape), pltpu.roll(a, 1, 1))
            east = jnp.where(lane == width - 1, spread(from_east, q, a.shape), pltpu.roll(a, width - 1, 1))
            v = a + cw * (a - west)
            v = v + ce * (east - a)
            v = v + cn * (a - (row(r - 1, f) if r > 0 else upper[f]))
            if south_wind is not None:
                v = v + cs * ((row(r + 1, f) if r + 1 < row_count else lower[f]) - a)
            put(r, f, v)


class Columns:
    def __init__(self, width):
        self.lane = lanes(PAD, width)
        self.last = self.head = jnp.zeros((PAD, width), F32)

    def add(self, r, f, v):
        here = self.lane == r * 2 + f
        self.last = jnp.where(here, spread(v, v.shape[1] - 1, v.shape), self.last)
        self.head = jnp.where(here, spread(v, 0, v.shape), self.head)

    def write(self, last_out, head_out):
        last_out[...] = self.last
        head_out[...] = self.head


def first_kernel(
    step, levels, sizes, tiles,
    code, inverse, where, winds, adj, edge, from_west, from_east,
    item, kept, found_out, east_wind,
    found, sem, extras,
):
    end, width = adj.shape[0] - 1, adj.shape[3]
    mates = sizes[0] * sizes[2]
    find_slots(levels, tiles, CAPACITY, winds, found_out, found, sem, extras)
    east_wind[...] = extras[0:PAD, :]
    north, north_mate, turn_north, south, _, turn_south = neighbours(sizes, code, inverse, where)
    y, ny = where[0, 1], sizes[1]
    upper = oriented(edge[lax.rem(y - north + ny, ny), pl.ds(2 * north_mate, 2)], turn_north)
    lower = oriented(edge[lax.rem(y - south + ny, ny), 2 * mates : 2 * mates + 2], turn_south)

    def put(r, f, v):
        item[f if r == 0 else 4 + f] = v.astype(BF16)
        kept[(11 if r == 0 else 9) + f] = v

    def row(r, f):
        return adj[r, f]

    advance(step, (0, end), levels, winds, found, east_wind, row, upper, None, None, from_west, from_east, put)
    edge_wind = wind(levels, winds, found, step * ROWS, 1)
    item[2] = edge_wind.astype(BF16)
    item[3] = wind(levels, winds, found, (step - 1) * ROWS, 1).astype(BF16)
    kept[0:2] = upper
    kept[2:4] = lower
    kept[4:6] = adj[end]
    kept[6:8] = adj[0]
    kept[8] = edge_wind

    shape = (PAD, width)
    lane, level = lanes(*shape), lax.broadcasted_iota(jnp.int32, shape, 0)
    head, last = extras[0:PAD, :], extras[HALF : HALF + PAD, :]
    turned_west = spread(from_west, TURN, shape) > 0.5
    turned_east = spread(from_east, TURN, shape) > 0.5
    west = jnp.where(turned_west, spread(head, HALF + 1, shape), spread(last, HALF + 1, shape))
    east = jnp.where(turned_east, spread(last, HALF, shape), spread(head, HALF, shape))
    v = jnp.where(lane == 0, west, jnp.where(lane == 1, east, 0.0))
    v = jnp.where(level == levels, spread(from_west, MATCH, shape), v)
    v = jnp.where(level == levels + 1, spread(from_east, MATCH, shape), v)
    item[6] = v.astype(BF16)


def inner_kernel(
    step, levels, opening, found, winds, adj, ends, from_west, from_east, east_wind, out, last_out, head_out
):
    row_count, width = adj.shape[0], adj.shape[3]
    columns = Columns(width)
    first_at, last_at = (11, 9) if opening else (2, 4)

    def put(r, f, v):
        out[r, f] = v
        columns.add(r, f, v)

    def row(r, f):
        return ends[f] if r == row_count - 1 and not opening else adj[r, f]

    rows = range(1, row_count - 1)
    advance(step, rows, levels, winds, found, east_wind, row, None, None, None, from_west, from_east, put)
    for f in range(2):
        put(0, f, ends[first_at + f])
        put(row_count - 1, f, ends[last_at + f])
    if opening:
        for f in range(2):
            v = ends[2 + f] - ends[4 + f]
            here = columns.lane == EDGE_COLUMN + f
            columns.last = jnp.where(here, spread(v, width - 1, v.shape), columns.last)
            columns.head = jnp.where(here, spread(v, 0, v.shape), columns.head)
    columns.write(last_out, head_out)


def middle_kernel(
    step, levels, sizes,
    code, inverse, where, found, winds, adj, edge, kept, from_west, from_east, east_wind,
    item, both,
):
    end = adj.shape[0] - 1
    north, _, turn_north, south, _, turn_south = neighbours(sizes, code, inverse, where)
    lower = oriented(edge[south, 0:4], turn_south)
    upper = oriented(edge[north, 4:6], turn_north)
    cs = COURANT * jnp.maximum(lower[2], 0.0)
    final = [kept[9 + f] + cs * (kept[2 + f] - kept[4 + f]) for f in range(2)]
    cs = COURANT * jnp.maximum(kept[8], 0.0)
    northern = []
    for f in range(2):
        v = upper[f] + cs * (kept[6 + f].astype(BF16).astype(F32) - kept[f])
        northern.append(v.astype(BF16).astype(F32))
    shape = final[0].shape
    lane = lanes(*shape)
    sides = []
    for i, columns in enumerate((from_west[...], from_east[...])):
        corner = jnp.zeros(shape, F32)
        for d in range(sizes[1]):
            k = edge[d, 6].astype(F32)
            corner = jnp.where(spread(k, 2 + i, shape) > 0.5, spread(k, i, shape), corner)
        cs = COURANT * jnp.maximum(corner, 0.0)
        mended = columns
        for f in range(2):
            mended = jnp.where(lane == 2 * end + f, columns + cs * spread(columns, EDGE_COLUMN + f, shape), mended)
        sides.append(mended)

    def put(r, f, v):
        item[f if r == 0 else 3 + f] = v.astype(BF16)
        both[(2 if r == 0 else 4) + f] = v

    def row(r, f):
        return final[f] if r == end else adj[r, f]

    advance(step, (0, end), levels, winds, found, east_wind, row, northern, lower, lower[3], *sides, put)
    both[0] = final[0]
    both[1] = final[1]
    item[2] = wind(levels, winds, found, (step - 1) * ROWS, 1).astype(BF16)


def late_kernel(step, levels, found, winds, adj, from_west, from_east, east_wind, out):
    rows = range(1, adj.shape[0] - 1)

    def put(r, f, v):
        out[r - 1, f] = v

    def row(r, f):
        return adj[r, f]

    advance(step, rows, levels, winds, found, east_wind, row, None, None, None, from_west, from_east, put)


def last_kernel(
    step, levels, sizes, code, inverse, where, found, winds, adj, edge, from_west, from_east, east_wind, inner, out
):
    end = adj.shape[0] - 1
    north, _, turn_north, south, _, turn_south = neighbours(sizes, code, inverse, where)
    upper = oriented(edge[north, 3:5], turn_north)
    lower = oriented(edge[south, 0:3], turn_south)

    def put(r, f, v):
        for l0 in range(0, levels, 8):
            n = min(8, levels - l0)
            out[pl.ds((f * levels + l0) * ROWS + r, n, stride=ROWS), :] = v[l0 : l0 + n]

    def row(r, f):
        return adj[r, f]

    for r in range(1, end):
        for f in range(2):
            put(r, f, inner[r - 1, f])
    advance(step, (0, end), levels, winds, found, east_wind, row, upper, lower, lower[2], from_west, from_east, put)


def shards(sizes, tile_sizes, adjoint_end, stored_rows, stored_owner, stored_unit, stored_valid, edge_match, edge_turn):
    face, tile, group = ("zl", "y", "c"), ("x", "zh"), ("zl", "c")
    faces = sizes[0] * sizes[1] * sizes[2]
    tiles = tile_sizes[0] * tile_sizes[1]
    levels, row_count, width = adjoint_end.shape[1:]
    slots = stored_rows.shape[1]
    sds = jax.ShapeDtypeStruct
    side = sds((PAD, width), F32)

    where = jnp.stack([lax.axis_index(a) for a in face]).astype(jnp.int32).reshape(1, 3)
    block = CAPACITY * 2 * levels // 8 + 1
    payload = call(
        functools.partial(pack_kernel, levels, tiles, (STEPS - 1) * row_count),
        sds((tiles * block, 8, width), BF16),
        [SM, SM, SM, VM],
        HBM,
        [
            pltpu.SMEM((tiles,), jnp.int32),
            pltpu.SMEM((slots,), jnp.int32),
            pltpu.SMEM((slots,), jnp.int32),
            pltpu.SMEM((tiles,), jnp.int32),
            pltpu.VMEM((width, width), F32),
            pltpu.VMEM((width, width), F32),
            pltpu.VMEM((tiles * block, 8, width), BF16),
            pltpu.SemaphoreType.DMA((CHUNKS,)),
        ],
        61 << 20,
    )(stored_owner, stored_unit, stored_valid, stored_rows[0])

    turned, item, *sides = call(
        functools.partial(edges_kernel, levels, row_count),
        (sds((row_count, 2, PAD, width), F32), sds((4, PAD, width), BF16), side, side),
        [SM, SM, VM],
        (VM,) * 4,
    )(edge_match, edge_turn, adjoint_end.reshape(2 * levels * row_count, width))

    planes, mates = sizes[1], sizes[0] * sizes[2]

    def to_sides(sides):
        ahead = [(i, (i + 1) % tiles) for i in range(tiles)]
        back = [((i + 1) % tiles, i) for i in range(tiles)]
        return lax.ppermute(sides[0], tile, ahead), lax.ppermute(sides[1], tile, back)

    def exchange(item, north_from, rows):
        gathered = lax.all_gather(item, group, axis=0, tiled=False)
        chosen = call(
            functools.partial(choose_kernel, sizes, levels, north_from, rows),
            sds((planes,) + item.shape, BF16),
            [SM, SM, SM, VM],
            VM,
        )(code, inverse, where, gathered)
        return lax.all_to_all(chosen, "y", 0, 0, tiled=True)

    other = lax.ppermute(item, "zl", [(i, (i + 1) % sizes[0]) for i in range(sizes[0])])
    payload, other = lax.optimization_barrier((payload, other))
    winds = lax.all_to_all(payload, tile, 0, 0, tiled=True)
    from_west, from_east = to_sides(sides)
    near = lax.all_gather(jnp.stack([item, other]), "c", axis=0, tiled=False)
    parts = call(
        functools.partial(first_send_kernel, sizes, levels),
        (sds((2 * mates + 2, PAD, width), BF16),) * planes,
        [SM, VM],
        (VM,) * planes,
    )(where, near)
    moved = [parts[0]]
    for d in range(1, planes):
        moved.append(lax.ppermute(parts[d], "y", [(i, (i + d) % planes) for i in range(planes)]))
    edge = jnp.stack(moved)
    table = sds((1, width), jnp.int32)
    code, inverse = call(
        functools.partial(code_kernel, sizes, levels), (table, table), [SM, VM], (VM, VM)
    )(where, edge)

    item, kept, found, east_wind = call(
        functools.partial(first_kernel, STEPS - 1, levels, sizes, tiles),
        (sds((7, PAD, width), BF16), sds((13, PAD, width), F32), table, side),
        [SM, SM, SM] + [VM] * 5,
        (VM,) * 4,
        [pltpu.SMEM((1, width), jnp.int32), pltpu.SemaphoreType.DMA, pltpu.VMEM((width, width), F32)],
    )(code, inverse, where, winds, turned, edge, from_west, from_east)
    edge = exchange(item, 4, 6)

    def inner(step, opening, adj, ends):
        adj, *sides = call(
            functools.partial(inner_kernel, step, levels, opening),
            (sds(turned.shape, F32), side, side),
            [SM] + [VM] * 6,
            (VM,) * 3,
        )(found, winds, adj, ends, from_west, from_east, east_wind)
        return adj, sides

    adj, sides = inner(STEPS - 1, True, turned, kept)
    from_west, from_east = to_sides(sides)
    item, both = call(
        functools.partial(middle_kernel, STEPS - 2, levels, sizes),
        (sds((5, PAD, width), BF16), sds((6, PAD, width), F32)),
        [SM] * 4 + [VM] * 7,
        (VM,) * 2,
    )(code, inverse, where, found, winds, adj, edge, kept, from_west, from_east, east_wind)
    edge = exchange(item, 3, 5)
    adj, sides = inner(STEPS - 2, False, adj, both)

    from_west, from_east = to_sides(sides)
    late = call(
        functools.partial(late_kernel, STEPS - 3, levels),
        sds((row_count - 2,) + turned.shape[1:], F32),
        [SM] + [VM] * 5,
        VM,
    )(found, winds, adj, from_west, from_east, east_wind)
    out = call(
        functools.partial(last_kernel, STEPS - 3, levels, sizes),
        sds((2 * levels * row_count, width), F32),
        [SM] * 4 + [VM] * 7,
        VM,
    )(code, inverse, where, found, winds, adj, edge, from_west, from_east, east_wind, late)
    return out.reshape(adjoint_end.shape)


def solution(mesh, sizes=(2, 8, 2), tile_sizes=(8, 4)):
    fine = Mesh(mesh.devices.reshape(sizes + tile_sizes), ("zl", "y", "c", "x", "zh"))
    face, tile = ("zl", "y", "c"), ("x", "zh")
    placed = (
        P(None, None, face, tile),
        P(face, tile, None, None, None),
        P(face, tile),
        P(face, tile),
        P(face, tile),
        P(face, tile),
        P(face, tile),
    )
    return jax.shard_map(
        functools.partial(shards, sizes, tile_sizes),
        mesh=fine,
        in_specs=placed,
        out_specs=P(None, None, face, tile),
        check_vma=False,
    )
```

time: 171 us -> 161 us (0.942)
  waiting for transfers between devices: 25.6 us -> 13.7 us
    all_to_all x2, waiting for transfers between devices: 11.2 us -> 1.43 us  [exchange(): return lax.all_to_all(chosen, 'y', 0, 0, tiled=True)]
    pallas_call x10 -> x9, Pallas kernels: 21.1 us -> 23.3 us  [the longest x1 7.75 us: shards(): call(functools.partial(pack_kernel, levels, tiles, (STEPS - 1) * row_coun...]
    all_to_all x1, waiting for transfers between devices: 2.06 us -> 0.01 us  [shards(): winds = lax.all_to_all(payload, tile, 0, 0, tiled=True)]
    unnamed x16 -> x20, local copies, waits for them, and re-layouts: 6.85 us -> 7.95 us
  transfers between devices with their start and end apart: 17 -> 17, of which waited for: 8 -> 7; matrix products, arithmetic and copies ran while one was open for 2% -> 2% of each run, Pallas kernels for 9% -> 11%
where the time goes in v5:
time: 161 us; the launch traced here: 160 us
  starting transfers between devices  97.3 us (60%)
  Pallas kernels  26.3 us (16%)
  waiting for transfers between devices  13.7 us (9%)
  blocking collectives  13.4 us (8%)
  local copies, waits for them, and re-layouts  7.96 us (5%)
  between operations  1.65 us (1%)
    ppermute x7, starting transfers between devices, shards(): lax.ppermute(parts[d], 'y', [(i, (i + d) % planes) for i in range(planes)])  28.2 us
    ppermute x3, starting transfers between devices, to_sides(): lax.ppermute(sides[1], tile, back)  20.8 us
    all_to_all x1, starting transfers between devices, shards(): winds = lax.all_to_all(payload, tile, 0, 0, tiled=True)  20.4 us
    all_to_all x2, starting transfers between devices, exchange(): return lax.all_to_all(chosen, 'y', 0, 0, tiled=True)  12.8 us
    all_gather x2, blocking collectives, exchange(): gathered = lax.all_gather(item, group, axis=0, tiled=False)  11.5 us
    ppermute x3, starting transfers between devices, to_sides(): lax.ppermute(sides[0], tile, ahead)  9.9 us
    ppermute x7, waiting for transfers between devices, shards(): lax.ppermute(parts[d], 'y', [(i, (i + d) % planes) for i in range(planes)])  9.35 us
    unnamed x20, local copies, waits for them, and re-layouts  7.95 us
  transfers between devices with their start and end apart: 17, of which 7 were waited for; matrix products, arithmetic and copies ran while one was open for 2% of the time, Pallas kernels for 11%

profile of v5, /device:TPU:24, one launch (start us, length us, event | category | flops | bytes accessed | tf_op | source)
XLA Modules:
  0.0 160.4 jit_solution(4226369052829741174)
XLA Ops:
  2.9 5.2 %collective-permute-start = (bf16[4,40,128]{2,1,0:T(8,128)(2,1)S(1)}, bf16[4,40,128]{2,1,0:T(8,128)(2,1)S(1)}, u32[]{:S(2)}, u32[]{:S(2)}) collective-permute-start(bf16[4,40,128]{2,1,0:T(8,128)(2,1)S(1)} %get-tuple-element.33), channel_id=1, source_target_pairs={{0,512},{512,0},{1,513},{513,1},{2,514},{514,2},{3,515},{515,3},{4... | collective-permute-start | bytes 122888 | tf_op jit(solution)/shard_map/ppermute | solution.py:545
  8.1 3.1 %copy.11 = bf16[1,96,2,36,128]{4,3,2,1,0:T(8,128)(2,1)} copy(bf16[1,96,2,36,128]{4,2,3,1,0:T(2,128)(2,1)} %param.8) | data formatting | bytes 3538944 | tf_op args[1]
  11.2 7.7 %shard_map.74 = bf16[896,8,128]{2,1,0:T(8,128)(2,1)} custom-call(s32[1,96]{1,0:T(1,128)} %owner.1, s32[1,96]{1,0:T(1,128)} %unit.1, s32[1,96]{1,0:T(1,128)} %valid.1, bf16[96,2,36,128]{3,2,1,0:T(8,128)(2,1)} %bitcast.36), custom_call_target="tpu_custom_call" | custom-call | flops 1048576 | bytes 1048576 | tf_op jit(solution)/shard_map/pallas_call | solution.py:503
  19.0 20.4 %all-to-all-start = ((bf16[896,8,128]{2,1,0:T(8,128)(2,1)}), bf16[896,8,128]{2,1,0:T(8,128)(2,1)S(1)}, u32[]{:S(2)}, u32[]{:S(2)}) async-start(bf16[896,8,128]{2,1,0:T(8,128)(2,1)} %shard_map.74), calls=%async_computation | async-start | bytes 3670016 | tf_op jit(solution)/shard_map/all_to_all | solution.py:547
  39.4 4.3 %collective-permute-start.8 = (f32[40,128]{1,0:T(8,128)S(1)}, f32[40,128]{1,0:T(8,128)S(1)}, u32[]{:S(2)}, u32[]{:S(2)}) collective-permute-start(f32[40,128]{1,0:T(8,128)S(1)} %get-tuple-element.47), channel_id=1, source_target_pairs={{0,1},{1,2},{2,3},{3,4},{4,5},{5,6},{6,7},{7,8},{8,9},{9,10},{10,1... | collective-permute-start | bytes 61448 | tf_op jit(solution)/shard_map/ppermute | solution.py:533
  43.7 5.8 %collective-permute-start.9 = (f32[40,128]{1,0:T(8,128)S(1)}, f32[40,128]{1,0:T(8,128)S(1)}, u32[]{:S(2)}, u32[]{:S(2)}) collective-permute-start(f32[40,128]{1,0:T(8,128)S(1)} %get-tuple-element.48), channel_id=1, source_target_pairs={{1,0},{2,1},{3,2},{4,3},{5,4},{6,5},{7,6},{8,7},{9,8},{10,9},{11,1... | collective-permute-start | bytes 61448 | tf_op jit(solution)/shard_map/ppermute | solution.py:533
  52.1 3.6 %collective-permute-start.1 = (bf16[10,40,128]{2,1,0:T(8,128)(2,1)S(1)}, bf16[10,40,128]{2,1,0:T(8,128)(2,1)S(1)}, u32[]{:S(2)}, u32[]{:S(2)}) collective-permute-start(bf16[10,40,128]{2,1,0:T(8,128)(2,1)S(1)} %get-tuple-element.36), channel_id=1, source_target_pairs={{0,64},{64,128},{128,192},{192,256},{256,320},{320,384},{384,448},... | collective-permute-start | bytes 307208 | tf_op jit(solution)/shard_map/ppermute | solution.py:558
  55.8 5.9 %collective-permute-start.2 = (bf16[10,40,128]{2,1,0:T(8,128)(2,1)S(1)}, bf16[10,40,128]{2,1,0:T(8,128)(2,1)S(1)}, u32[]{:S(2)}, u32[]{:S(2)}) collective-permute-start(bf16[10,40,128]{2,1,0:T(8,128)(2,1)S(1)} %get-tuple-element.37), channel_id=1, source_target_pairs={{0,128},{64,192},{128,256},{192,320},{256,384},{320,448},{384,0},{... | collective-permute-start | bytes 307208 | tf_op jit(solution)/shard_map/ppermute | solution.py:558
  61.7 3.2 %collective-permute-start.3 = (bf16[10,40,128]{2,1,0:T(8,128)(2,1)S(1)}, bf16[10,40,128]{2,1,0:T(8,128)(2,1)S(1)}, u32[]{:S(2)}, u32[]{:S(2)}) collective-permute-start(bf16[10,40,128]{2,1,0:T(8,128)(2,1)S(1)} %get-tuple-element.38), channel_id=1, source_target_pairs={{0,192},{64,256},{128,320},{192,384},{256,448},{320,0},{384,64},{4... | collective-permute-start | bytes 307208 | tf_op jit(solution)/shard_map/ppermute | solution.py:558
  64.9 4.3 %collective-permute-start.4 = (bf16[10,40,128]{2,1,0:T(8,128)(2,1)S(1)}, bf16[10,40,128]{2,1,0:T(8,128)(2,1)S(1)}, u32[]{:S(2)}, u32[]{:S(2)}) collective-permute-start(bf16[10,40,128]{2,1,0:T(8,128)(2,1)S(1)} %get-tuple-element.39), channel_id=1, source_target_pairs={{0,256},{64,320},{128,384},{192,448},{256,0},{320,64},{384,128},{4... | collective-permute-start | bytes 307208 | tf_op jit(solution)/shard_map/ppermute | solution.py:558
  69.2 4.0 %collective-permute-start.5 = (bf16[10,40,128]{2,1,0:T(8,128)(2,1)S(1)}, bf16[10,40,128]{2,1,0:T(8,128)(2,1)S(1)}, u32[]{:S(2)}, u32[]{:S(2)}) collective-permute-start(bf16[10,40,128]{2,1,0:T(8,128)(2,1)S(1)} %get-tuple-element.40), channel_id=1, source_target_pairs={{0,320},{64,384},{128,448},{192,0},{256,64},{320,128},{384,192},{4... | collective-permute-start | bytes 307208 | tf_op jit(solution)/shard_map/ppermute | solution.py:558
  73.3 3.6 %collective-permute-done.3 = bf16[10,40,128]{2,1,0:T(8,128)(2,1)S(1)} collective-permute-done((bf16[10,40,128]{2,1,0:T(8,128)(2,1)S(1)}, bf16[10,40,128]{2,1,0:T(8,128)(2,1)S(1)}, u32[]{:S(2)}, u32[]{:S(2)}) %collective-permute-start.3) | collective-permute-done | bytes 102432 | tf_op jit(solution)/shard_map/ppermute | solution.py:558
  76.9 5.3 %collective-permute-start.6 = (bf16[10,40,128]{2,1,0:T(8,128)(2,1)S(1)}, bf16[10,40,128]{2,1,0:T(8,128)(2,1)S(1)}, u32[]{:S(2)}, u32[]{:S(2)}) collective-permute-start(bf16[10,40,128]{2,1,0:T(8,128)(2,1)S(1)} %get-tuple-element.41), channel_id=1, source_target_pairs={{0,384},{64,448},{128,0},{192,64},{256,128},{320,192},{384,256},{4... | collective-permute-start | bytes 307208 | tf_op jit(solution)/shard_map/ppermute | solution.py:558
  85.6 4.4 %collective-permute-done.7 = bf16[10,40,128]{2,1,0:T(8,128)(2,1)S(1)} collective-permute-done((bf16[10,40,128]{2,1,0:T(8,128)(2,1)S(1)}, bf16[10,40,128]{2,1,0:T(8,128)(2,1)S(1)}, u32[]{:S(2)}, u32[]{:S(2)}) %collective-permute-start.7) | collective-permute-done | bytes 102432 | tf_op jit(solution)/shard_map/ppermute | solution.py:558
  92.9 5.8 %all-gather.1 = bf16[28,40,128]{2,1,0:T(8,128)(2,1)S(1)} all-gather(bf16[7,40,128]{2,1,0:T(8,128)(2,1)S(1)} %get-tuple-element.53), channel_id=3, replica_groups=mesh['zl'=2,'y'=8,'c'=2,'x'=8,'zh'=4] {'zl','c'}, dimensions={0}, use_global_device_ids=true | all-gather | bytes 358400 | tf_op jit(solution)/shard_map/all_gather | solution.py:536
  100.3 7.0 %all-to-all-start.1 = ((bf16[8,7,40,128]{3,2,1,0:T(8,128)(2,1)}), bf16[8,7,40,128]{3,2,1,0:T(8,128)(2,1)}, u32[]{:S(2)}, u32[]{:S(2)}) async-start(bf16[8,7,40,128]{3,2,1,0:T(8,128)(2,1)} %shard_map.79), calls=%async_computation.1 | async-start | bytes 1146880 | tf_op jit(solution)/shard_map/all_to_all | solution.py:543
  108.2 3.8 %shard_map.78 = (f32[16,2,40,128]{3,2,1,0:T(8,128)S(1)}, f32[40,128]{1,0:T(8,128)S(1)}, f32[40,128]{1,0:T(8,128)S(1)}) custom-call(s32[1,128]{1,0:T(1,128)S(1)} %get-tuple-element.49.found, bf16[896,8,128]{2,1,0:T(8,128)(2,1)S(1)} %all-to-all-done.winds, f32[16,2,40,128]{3,2,1,0:T(8,128)S(1)} %get-tuple-element.46.adj, f32[13,40,128]{2,1,0:T(8,128)S(1)} %copy-done.3, ...), custom_call_target="tpu_custom_call" | custom-call | flops 1048576 | bytes 1048576 | tf_op jit(solution)/shard_map/pallas_call | solution.py:575
  112.0 3.3 %collective-permute-start.10 = (f32[40,128]{1,0:T(8,128)S(1)}, f32[40,128]{1,0:T(8,128)S(1)}, u32[]{:S(2)}, u32[]{:S(2)}) collective-permute-start(f32[40,128]{1,0:T(8,128)S(1)} %get-tuple-element.54), channel_id=1, source_target_pairs={{0,1},{1,2},{2,3},{3,4},{4,5},{5,6},{6,7},{7,8},{8,9},{9,10},{10,1... | collective-permute-start | bytes 61448 | tf_op jit(solution)/shard_map/ppermute | solution.py:533
  115.3 6.8 %collective-permute-start.11 = (f32[40,128]{1,0:T(8,128)S(1)}, f32[40,128]{1,0:T(8,128)S(1)}, u32[]{:S(2)}, u32[]{:S(2)}) collective-permute-start(f32[40,128]{1,0:T(8,128)S(1)} %get-tuple-element.55), channel_id=1, source_target_pairs={{1,0},{2,1},{3,2},{4,3},{5,4},{6,5},{7,6},{8,7},{9,8},{10,9},{11,1... | collective-permute-start | bytes 61448 | tf_op jit(solution)/shard_map/ppermute | solution.py:533
  127.4 5.6 %all-gather.2 = bf16[20,40,128]{2,1,0:T(8,128)(2,1)S(1)} all-gather(bf16[5,40,128]{2,1,0:T(8,128)(2,1)S(1)} %get-tuple-element.58), channel_id=4, replica_groups=mesh['zl'=2,'y'=8,'c'=2,'x'=8,'zh'=4] {'zl','c'}, dimensions={0}, use_global_device_ids=true | all-gather | bytes 256000 | tf_op jit(solution)/shard_map/all_gather | solution.py:536
  134.5 5.8 %all-to-all-start.2 = ((bf16[8,5,40,128]{3,2,1,0:T(8,128)(2,1)}), bf16[8,5,40,128]{3,2,1,0:T(8,128)(2,1)S(1)}, u32[]{:S(2)}, u32[]{:S(2)}) async-start(bf16[8,5,40,128]{3,2,1,0:T(8,128)(2,1)} %shard_map.82), calls=%async_computation.2 | async-start | bytes 819200 | tf_op jit(solution)/shard_map/all_to_all | solution.py:543
  141.3 3.8 %shard_map.81 = (f32[16,2,40,128]{3,2,1,0:T(8,128)S(1)}, f32[40,128]{1,0:T(8,128)S(1)}, f32[40,128]{1,0:T(8,128)S(1)}) custom-call(s32[1,128]{1,0:T(1,128)S(1)} %get-tuple-element.49.found, bf16[896,8,128]{2,1,0:T(8,128)(2,1)S(1)} %all-to-all-done.winds, f32[16,2,40,128]{3,2,1,0:T(8,128)S(1)} %copy-done.1, f32[6,40,128]{2,1,0:T(8,128)S(1)} %get-tuple-element.56.ends, ...), custom_call_target="tpu_custom_call" | custom-call | flops 1048576 | bytes 1048576 | tf_op jit(solution)/shard_map/pallas_call | solution.py:575
  145.1 2.4 %collective-permute-start.12 = (f32[40,128]{1,0:T(8,128)S(1)}, f32[40,128]{1,0:T(8,128)S(1)}, u32[]{:S(2)}, u32[]{:S(2)}) collective-permute-start(f32[40,128]{1,0:T(8,128)S(1)} %get-tuple-element.59), channel_id=1, source_target_pairs={{0,1},{1,2},{2,3},{3,4},{4,5},{5,6},{6,7},{7,8},{8,9},{9,10},{10,1... | collective-permute-start | bytes 61448 | tf_op jit(solution)/shard_map/ppermute | solution.py:533
  147.4 8.2 %collective-permute-start.13 = (f32[40,128]{1,0:T(8,128)S(1)}, f32[40,128]{1,0:T(8,128)S(1)}, u32[]{:S(2)}, u32[]{:S(2)}) collective-permute-start(f32[40,128]{1,0:T(8,128)S(1)} %get-tuple-element.60), channel_id=1, source_target_pairs={{1,0},{2,1},{3,2},{4,3},{5,4},{6,5},{7,6},{8,7},{9,8},{10,9},{11,1... | collective-permute-start | bytes 61448 | tf_op jit(solution)/shard_map/ppermute | solution.py:533
  (48 shorter events, 25.5 us)
Async XLA Ops:
  1.3 1.1 copy-start.5
  2.9 16.0 %collective-permute-start = (bf16[4,40,128]{2,1,0:T(8,128)(2,1)S(1)}, bf16[4,40,128]{2,1,0:T(8,128)(2,1)S(1)}, u32[]{:S(2)}, u32[]{:S(2)}) collective-permute-start(bf16[4,40,128]{2,1,0:T(8,128)(2,1)S(1)} %get-tuple-element.33), channel_id=1, source_target_pairs={{0,512},{512,0},{1,513},{513,1},{2,514},{514,2},{3,515},{515,3},{4... | collective-permute-start | bytes 122888 | tf_op jit(solution)/shard_map/ppermute | solution.py:545
  19.0 71.7 %all-to-all-start = ((bf16[896,8,128]{2,1,0:T(8,128)(2,1)}), bf16[896,8,128]{2,1,0:T(8,128)(2,1)S(1)}, u32[]{:S(2)}, u32[]{:S(2)}) async-start(bf16[896,8,128]{2,1,0:T(8,128)(2,1)} %shard_map.74), calls=%async_computation | async-start | bytes 3670016 | tf_op jit(solution)/shard_map/all_to_all | solution.py:547
  39.4 51.2 %collective-permute-start.8 = (f32[40,128]{1,0:T(8,128)S(1)}, f32[40,128]{1,0:T(8,128)S(1)}, u32[]{:S(2)}, u32[]{:S(2)}) collective-permute-start(f32[40,128]{1,0:T(8,128)S(1)} %get-tuple-element.47), channel_id=1, source_target_pairs={{0,1},{1,2},{2,3},{3,4},{4,5},{5,6},{6,7},{7,8},{8,9},{9,10},{10,1... | collective-permute-start | bytes 61448 | tf_op jit(solution)/shard_map/ppermute | solution.py:533
  43.7 47.0 %collective-permute-start.9 = (f32[40,128]{1,0:T(8,128)S(1)}, f32[40,128]{1,0:T(8,128)S(1)}, u32[]{:S(2)}, u32[]{:S(2)}) collective-permute-start(f32[40,128]{1,0:T(8,128)S(1)} %get-tuple-element.48), channel_id=1, source_target_pairs={{1,0},{2,1},{3,2},{4,3},{5,4},{6,5},{7,6},{8,7},{9,8},{10,9},{11,1... | collective-permute-start | bytes 61448 | tf_op jit(solution)/shard_map/ppermute | solution.py:533
  52.1 12.7 %collective-permute-start.1 = (bf16[10,40,128]{2,1,0:T(8,128)(2,1)S(1)}, bf16[10,40,128]{2,1,0:T(8,128)(2,1)S(1)}, u32[]{:S(2)}, u32[]{:S(2)}) collective-permute-start(bf16[10,40,128]{2,1,0:T(8,128)(2,1)S(1)} %get-tuple-element.36), channel_id=1, source_target_pairs={{0,64},{64,128},{128,192},{192,256},{256,320},{320,384},{384,448},... | collective-permute-start | bytes 307208 | tf_op jit(solution)/shard_map/ppermute | solution.py:558
  55.8 13.4 %collective-permute-start.2 = (bf16[10,40,128]{2,1,0:T(8,128)(2,1)S(1)}, bf16[10,40,128]{2,1,0:T(8,128)(2,1)S(1)}, u32[]{:S(2)}, u32[]{:S(2)}) collective-permute-start(bf16[10,40,128]{2,1,0:T(8,128)(2,1)S(1)} %get-tuple-element.37), channel_id=1, source_target_pairs={{0,128},{64,192},{128,256},{192,320},{256,384},{320,448},{384,0},{... | collective-permute-start | bytes 307208 | tf_op jit(solution)/shard_map/ppermute | solution.py:558
  61.7 15.2 %collective-permute-start.3 = (bf16[10,40,128]{2,1,0:T(8,128)(2,1)S(1)}, bf16[10,40,128]{2,1,0:T(8,128)(2,1)S(1)}, u32[]{:S(2)}, u32[]{:S(2)}) collective-permute-start(bf16[10,40,128]{2,1,0:T(8,128)(2,1)S(1)} %get-tuple-element.38), channel_id=1, source_target_pairs={{0,192},{64,256},{128,320},{192,384},{256,448},{320,0},{384,64},{4... | collective-permute-start | bytes 307208 | tf_op jit(solution)/shard_map/ppermute | solution.py:558
  64.9 17.3 %collective-permute-start.4 = (bf16[10,40,128]{2,1,0:T(8,128)(2,1)S(1)}, bf16[10,40,128]{2,1,0:T(8,128)(2,1)S(1)}, u32[]{:S(2)}, u32[]{:S(2)}) collective-permute-start(bf16[10,40,128]{2,1,0:T(8,128)(2,1)S(1)} %get-tuple-element.39), channel_id=1, source_target_pairs={{0,256},{64,320},{128,384},{192,448},{256,0},{320,64},{384,128},{4... | collective-permute-start | bytes 307208 | tf_op jit(solution)/shard_map/ppermute | solution.py:558
  69.2 15.6 %collective-permute-start.5 = (bf16[10,40,128]{2,1,0:T(8,128)(2,1)S(1)}, bf16[10,40,128]{2,1,0:T(8,128)(2,1)S(1)}, u32[]{:S(2)}, u32[]{:S(2)}) collective-permute-start(bf16[10,40,128]{2,1,0:T(8,128)(2,1)S(1)} %get-tuple-element.40), channel_id=1, source_target_pairs={{0,320},{64,384},{128,448},{192,0},{256,64},{320,128},{384,192},{4... | collective-permute-start | bytes 307208 | tf_op jit(solution)/shard_map/ppermute | solution.py:558
  76.9 8.7 %collective-permute-start.6 = (bf16[10,40,128]{2,1,0:T(8,128)(2,1)S(1)}, bf16[10,40,128]{2,1,0:T(8,128)(2,1)S(1)}, u32[]{:S(2)}, u32[]{:S(2)}) collective-permute-start(bf16[10,40,128]{2,1,0:T(8,128)(2,1)S(1)} %get-tuple-element.41), channel_id=1, source_target_pairs={{0,384},{64,448},{128,0},{192,64},{256,128},{320,192},{384,256},{4... | collective-permute-start | bytes 307208 | tf_op jit(solution)/shard_map/ppermute | solution.py:558
  82.2 7.7 %collective-permute-start.7 = (bf16[10,40,128]{2,1,0:T(8,128)(2,1)S(1)}, bf16[10,40,128]{2,1,0:T(8,128)(2,1)S(1)}, u32[]{:S(2)}, u32[]{:S(2)}) collective-permute-start(bf16[10,40,128]{2,1,0:T(8,128)(2,1)S(1)} %get-tuple-element.42), channel_id=1, source_target_pairs={{0,448},{64,0},{128,64},{192,128},{256,192},{320,256},{384,320},{4... | collective-permute-start | bytes 307208 | tf_op jit(solution)/shard_map/ppermute | solution.py:558
  92.2 0.7 copy-start.2
  100.3 24.7 %all-to-all-start.1 = ((bf16[8,7,40,128]{3,2,1,0:T(8,128)(2,1)}), bf16[8,7,40,128]{3,2,1,0:T(8,128)(2,1)}, u32[]{:S(2)}, u32[]{:S(2)}) async-start(bf16[8,7,40,128]{3,2,1,0:T(8,128)(2,1)} %shard_map.79), calls=%async_computation.1 | async-start | bytes 1146880 | tf_op jit(solution)/shard_map/all_to_all | solution.py:543
  107.3 1.0 copy-start.3
  112.0 22.4 %copy-start = (f32[16,2,40,128]{3,2,1,0:T(8,128)}, f32[16,2,40,128]{3,2,1,0:T(8,128)S(1)}, u32[]{:S(2)}) copy-start(f32[16,2,40,128]{3,2,1,0:T(8,128)S(1)} %get-tuple-element.52.adj) | copy-start | bytes 1966084
  112.0 10.1 %collective-permute-start.10 = (f32[40,128]{1,0:T(8,128)S(1)}, f32[40,128]{1,0:T(8,128)S(1)}, u32[]{:S(2)}, u32[]{:S(2)}) collective-permute-start(f32[40,128]{1,0:T(8,128)S(1)} %get-tuple-element.54), channel_id=1, source_target_pairs={{0,1},{1,2},{2,3},{3,4},{4,5},{5,6},{6,7},{7,8},{8,9},{9,10},{10,1... | collective-permute-start | bytes 61448 | tf_op jit(solution)/shard_map/ppermute | solution.py:533
  115.3 8.3 %collective-permute-start.11 = (f32[40,128]{1,0:T(8,128)S(1)}, f32[40,128]{1,0:T(8,128)S(1)}, u32[]{:S(2)}, u32[]{:S(2)}) collective-permute-start(f32[40,128]{1,0:T(8,128)S(1)} %get-tuple-element.55), channel_id=1, source_target_pairs={{1,0},{2,1},{3,2},{4,3},{5,4},{6,5},{7,6},{8,7},{9,8},{10,9},{11,1... | collective-permute-start | bytes 61448 | tf_op jit(solution)/shard_map/ppermute | solution.py:533
  125.0 1.0 copy-start.4
  134.5 24.1 %all-to-all-start.2 = ((bf16[8,5,40,128]{3,2,1,0:T(8,128)(2,1)}), bf16[8,5,40,128]{3,2,1,0:T(8,128)(2,1)S(1)}, u32[]{:S(2)}, u32[]{:S(2)}) async-start(bf16[8,5,40,128]{3,2,1,0:T(8,128)(2,1)} %shard_map.82), calls=%async_computation.2 | async-start | bytes 819200 | tf_op jit(solution)/shard_map/all_to_all | solution.py:543
  140.2 1.1 copy-start.1
  145.1 10.6 %collective-permute-start.12 = (f32[40,128]{1,0:T(8,128)S(1)}, f32[40,128]{1,0:T(8,128)S(1)}, u32[]{:S(2)}, u32[]{:S(2)}) collective-permute-start(f32[40,128]{1,0:T(8,128)S(1)} %get-tuple-element.59), channel_id=1, source_target_pairs={{0,1},{1,2},{2,3},{3,4},{4,5},{5,6},{6,7},{7,8},{8,9},{9,10},{10,1... | collective-permute-start | bytes 61448 | tf_op jit(solution)/shard_map/ppermute | solution.py:533
  147.4 9.7 %collective-permute-start.13 = (f32[40,128]{1,0:T(8,128)S(1)}, f32[40,128]{1,0:T(8,128)S(1)}, u32[]{:S(2)}, u32[]{:S(2)}) collective-permute-start(f32[40,128]{1,0:T(8,128)S(1)} %get-tuple-element.60), channel_id=1, source_target_pairs={{1,0},{2,1},{3,2},{4,3},{5,4},{6,5},{7,6},{8,7},{9,8},{10,9},{11,1... | collective-permute-start | bytes 61448 | tf_op jit(solution)/shard_map/ppermute | solution.py:533

commit v6 on v5

--- a/solution.py
+++ b/solution.py
@@ -48,8 +48,10 @@
 
 
 def pack_kernel(
-    levels, tiles, edge_unit, owner, unit, valid, rows, sent, count, source, label, first, flat, corner, out, sem_out
+    levels, tiles, edge_unit, owner, unit, valid, stored, sent, count, source, label, first, flat, corner, rows, out, sem_in, sem_out
 ):
+    fetch = pltpu.make_async_copy(stored, rows, sem_in)
+    fetch.start()
     slots, width = rows.shape[0], rows.shape[3]
     capacity = slots // tiles
     block = out.shape[0] // tiles
@@ -70,21 +72,17 @@
     lax.fori_loop(0, slots, blank, 0, unroll=8)
 
     def place(s, c):
-        @pl.when(valid[0, s] == 1)
-        def _():
-            o, u = owner[0, s], unit[0, s]
-            p = o * capacity + count[o]
-            source[p] = s
-            label[p] = u
-            count[o] = count[o] + 1
-
-            @pl.when(u == edge_unit)
-            def _():
-                first[o] = s
-
+        o, u, v = owner[0, s], unit[0, s], valid[0, s]
+        have = count[o]
+        p = jnp.where(v == 1, o * capacity + have, slots)
+        source[p] = s
+        label[p] = u
+        count[o] = have + v
+        first[jnp.where((v == 1) & (u == edge_unit), o, tiles)] = s
         return c
 
-    lax.fori_loop(0, slots, place, 0, unroll=4)
+    lax.fori_loop(0, slots, place, 0, unroll=8)
+    fetch.wait()
 
     lane = lanes(levels, width)
 
@@ -119,8 +117,8 @@
             s = source[p]
             at_slot = base + i * (2 * levels // 8)
             for j in range(2):
-                v = rows[s, j, 0:whole].astype(F32).reshape(whole // 8, 8, width)
-                out[pl.ds(at_slot + j * (whole // 8), whole // 8)] = v.astype(BF16)
+                for k in range(whole // 8):
+                    out[at_slot + j * (whole // 8) + k] = rows[s, j, 8 * k : 8 * k + 8]
             rest = [rows[s, j, whole:levels].astype(F32) for j in range(2)]
             out[at_slot + 2 * whole // 8] = jnp.concatenate(rest, axis=0).astype(BF16)
             line = at(flat, source[q])
@@ -137,7 +135,7 @@
     chunk = tiles // CHUNKS
     copies = []
     for i in range(CHUNKS):
-        lax.fori_loop(i * chunk, (i + 1) * chunk, fill, 0)
+        lax.fori_loop(i * chunk, (i + 1) * chunk, fill, 0, unroll=2)
         span = pl.ds(i * chunk * block, chunk * block)
         copies.append(pltpu.make_async_copy(out.at[span], sent.at[span], sem_out.at[i]))
         copies[-1].start()
@@ -185,26 +183,29 @@
     match = [jnp.broadcast_to(tail(mates[i, z, 2], levels)[0:1], shape) for i, z in order]
     first = [[mates[i, z, f].astype(F32) for f in range(2)] for i, z in order]
     for d, out in enumerate(outs):
-        dest = ((zl * ny + lax.rem(y + d, ny)) * nc + c).astype(F32)
+        plane = lax.rem(jnp.where(c == 0, y + d, y - d + ny), ny)
         for m, (i, z) in enumerate(order):
             for f in range(2):
                 out[2 * m + f] = mates[i, z, 2 + f]
-        for f in range(2):
-            v = first[0][f]
-            for m in range(1, len(order)):
-                v = jnp.where(match[m] == dest, first[m][f], v)
-            out[2 * len(order) + f] = v.astype(BF16)
-
-
-def code_kernel(sizes, levels, where, edge, code, inverse):
+        for core in range(nc):
+            dest = ((zl * ny + plane) * nc + core).astype(F32)
+            for f in range(2):
+                v = first[0][f]
+                for m in range(1, len(order)):
+                    v = jnp.where(match[m] == dest, first[m][f], v)
+                out[2 * (len(order) + core) + f] = v.astype(BF16)
+
+
+def code_kernel(sizes, levels, where, own, edge, code, inverse):
     nz, ny, nc = sizes
+    half = ny // 2
     lane = lanes(1, code.shape[1])
     codes = jnp.zeros(code.shape, F32)
     south = jnp.zeros(code.shape, jnp.int32)
     for d in range(ny):
         plane = lax.rem(where[0, 1] - d + ny, ny)
         for m in range(nz * nc):
-            t = tail(edge[d, 2 * m], levels)
+            t = tail(own[2 * m] if d == 0 else edge[d - 1 if d <= half else half + ny - d - 1, 2 * m], levels)
             face = ((m // nc) * ny + plane) * nc + m % nc
             codes = jnp.where(lane == face, 2.0 * t[0:1] + t[1:2], codes)
             south = jnp.where(lane.astype(F32) == t[0:1], face, south)
@@ -341,7 +342,7 @@
 
 def first_kernel(
     step, levels, sizes, tiles,
-    code, inverse, where, winds, adj, edge, from_west, from_east,
+    code, inverse, where, winds, adj, own, edge, from_west, from_east,
     item, kept, found_out, east_wind,
     found, sem, extras,
 ):
@@ -350,13 +351,21 @@
     find_slots(levels, tiles, CAPACITY, winds, found_out, found, sem, extras)
     east_wind[...] = extras[0:PAD, :]
     north, north_mate, turn_north, south, _, turn_south = neighbours(sizes, code, inverse, where)
-    y, ny = where[0, 1], sizes[1]
-    upper = oriented(edge[lax.rem(y - north + ny, ny), pl.ds(2 * north_mate, 2)], turn_north)
-    lower = oriented(edge[lax.rem(y - south + ny, ny), 2 * mates : 2 * mates + 2], turn_south)
+    y, c, ny = where[0, 1], where[0, 2], sizes[1]
+    half = ny // 2
+
+    def arrived(plane, row):
+        d = lax.rem(y - plane + ny, ny)
+        i = jnp.where(d <= half, jnp.maximum(d - 1, 0), half + ny - d - 1)
+        both = own[pl.ds(row, 2)].astype(F32), edge[i, pl.ds(row, 2)].astype(F32)
+        return jnp.where(d == 0, *both).astype(BF16)
+
+    upper = oriented(arrived(north, 2 * north_mate), turn_north)
+    lower = oriented(arrived(south, 2 * (mates + c)), turn_south)
 
     def put(r, f, v):
         item[f if r == 0 else 4 + f] = v.astype(BF16)
-        kept[(11 if r == 0 else 9) + f] = v
+        kept[(7 if r == 0 else 5) + f] = v
 
     def row(r, f):
         return adj[r, f]
@@ -365,11 +374,10 @@
     edge_wind = wind(levels, winds, found, step * ROWS, 1)
     item[2] = edge_wind.astype(BF16)
     item[3] = wind(levels, winds, found, (step - 1) * ROWS, 1).astype(BF16)
-    kept[0:2] = upper
-    kept[2:4] = lower
-    kept[4:6] = adj[end]
-    kept[6:8] = adj[0]
-    kept[8] = edge_wind
+    for f in range(2):
+        kept[f] = lower[f] - adj[end, f]
+        kept[2 + f] = adj[0, f].astype(BF16).astype(F32) - upper[f]
+    kept[4] = edge_wind
 
     shape = (PAD, width)
     lane, level = lanes(*shape), lax.broadcasted_iota(jnp.int32, shape, 0)
@@ -389,7 +397,7 @@
 ):
     row_count, width = adj.shape[0], adj.shape[3]
     columns = Columns(width)
-    first_at, last_at = (11, 9) if opening else (2, 4)
+    first_at, last_at = (7, 5) if opening else (2, 4)
 
     def put(r, f, v):
         out[r, f] = v
@@ -405,7 +413,7 @@
         put(row_count - 1, f, ends[last_at + f])
     if opening:
         for f in range(2):
-            v = ends[2 + f] - ends[4 + f]
+            v = ends[f]
             here = columns.lane == EDGE_COLUMN + f
             columns.last = jnp.where(here, spread(v, width - 1, v.shape), columns.last)
             columns.head = jnp.where(here, spread(v, 0, v.shape), columns.head)
@@ -422,11 +430,11 @@
     lower = oriented(edge[south, 0:4], turn_south)
     upper = oriented(edge[north, 4:6], turn_north)
     cs = COURANT * jnp.maximum(lower[2], 0.0)
-    final = [kept[9 + f] + cs * (kept[2 + f] - kept[4 + f]) for f in range(2)]
-    cs = COURANT * jnp.maximum(kept[8], 0.0)
+    final = [kept[5 + f] + cs * kept[f] for f in range(2)]
+    cs = COURANT * jnp.maximum(kept[4], 0.0)
     northern = []
     for f in range(2):
-        v = upper[f] + cs * (kept[6 + f].astype(BF16).astype(F32) - kept[f])
+        v = upper[f] + cs * kept[2 + f]
         northern.append(v.astype(BF16).astype(F32))
     shape = final[0].shape
     lane = lanes(*shape)
@@ -503,16 +511,18 @@
     payload = call(
         functools.partial(pack_kernel, levels, tiles, (STEPS - 1) * row_count),
         sds((tiles * block, 8, width), BF16),
-        [SM, SM, SM, VM],
+        [SM, SM, SM, HBM],
         HBM,
         [
             pltpu.SMEM((tiles,), jnp.int32),
-            pltpu.SMEM((slots,), jnp.int32),
-            pltpu.SMEM((slots,), jnp.int32),
-            pltpu.SMEM((tiles,), jnp.int32),
+            pltpu.SMEM((slots + 1,), jnp.int32),
+            pltpu.SMEM((slots + 1,), jnp.int32),
+            pltpu.SMEM((tiles + 1,), jnp.int32),
             pltpu.VMEM((width, width), F32),
             pltpu.VMEM((width, width), F32),
+            pltpu.VMEM(stored_rows.shape[1:], BF16),
             pltpu.VMEM((tiles * block, 8, width), BF16),
+            pltpu.SemaphoreType.DMA,
             pltpu.SemaphoreType.DMA((CHUNKS,)),
         ],
         61 << 20,
@@ -547,28 +557,31 @@
     winds = lax.all_to_all(payload, tile, 0, 0, tiled=True)
     from_west, from_east = to_sides(sides)
     near = lax.all_gather(jnp.stack([item, other]), "c", axis=0, tiled=False)
-    parts = call(
+    half, cores = planes // 2, sizes[2]
+    own, *parts = call(
         functools.partial(first_send_kernel, sizes, levels),
-        (sds((2 * mates + 2, PAD, width), BF16),) * planes,
+        (sds((2 * (mates + cores), PAD, width), BF16),) * (half + 1),
         [SM, VM],
-        (VM,) * planes,
+        (VM,) * (half + 1),
     )(where, near)
-    moved = [parts[0]]
-    for d in range(1, planes):
-        moved.append(lax.ppermute(parts[d], "y", [(i, (i + d) % planes) for i in range(planes)]))
-    edge = jnp.stack(moved)
+    moved = []
+    for d, part in enumerate(parts, 1):
+        ways = [(c, d if c == 0 else -d) for c in range(cores) if c == 0 or d < half]
+        route = [(y * cores + c, (y + way) % planes * cores + c) for y in range(planes) for c, way in ways]
+        moved.append(lax.ppermute(part, ("y", "c"), route))
+    edge = lax.all_gather(jnp.stack(moved), "c", axis=0, tiled=True)
     table = sds((1, width), jnp.int32)
     code, inverse = call(
-        functools.partial(code_kernel, sizes, levels), (table, table), [SM, VM], (VM, VM)
-    )(where, edge)
+        functools.partial(code_kernel, sizes, levels), (table, table), [SM, VM, VM], (VM, VM)
+    )(where, own, edge)
 
     item, kept, found, east_wind = call(
         functools.partial(first_kernel, STEPS - 1, levels, sizes, tiles),
-        (sds((7, PAD, width), BF16), sds((13, PAD, width), F32), table, side),
-        [SM, SM, SM] + [VM] * 5,
+        (sds((7, PAD, width), BF16), sds((9, PAD, width), F32), table, side),
+        [SM, SM, SM] + [VM] * 6,
         (VM,) * 4,
         [pltpu.SMEM((1, width), jnp.int32), pltpu.SemaphoreType.DMA, pltpu.VMEM((width, width), F32)],
-    )(code, inverse, where, winds, turned, edge, from_west, from_east)
+    )(code, inverse, where, winds, turned, own, edge, from_west, from_east)
     edge = exchange(item, 4, 6)
 
     def inner(step, opening, adj, ends):

time: 161 us -> 159 us (0.988)
  starting transfers between devices: 97.3 us -> 85.8 us
  waiting for transfers between devices: 13.7 us -> 22.6 us
  blocking collectives: 13.4 us -> 16 us
    ppermute x3, waiting for transfers between devices: 0.01 us -> 13.7 us  [to_sides(): lax.ppermute(sides[0], tile, ahead)]
    ppermute x7 -> x4, starting transfers between devices: 28.2 us -> 16.9 us  [shards(): moved.append(lax.ppermute(part, ('y', 'c'), route))]
    ppermute x7 -> x4, waiting for transfers between devices: 9.35 us -> 0.01 us  [shards(): moved.append(lax.ppermute(part, ('y', 'c'), route))]
    all_to_all x1, waiting for transfers between devices: 0.01 us -> 3.58 us  [shards(): winds = lax.all_to_all(payload, tile, 0, 0, tiled=True)]
    all_gather x0 -> x1, blocking collectives: none -> 2.51 us  [shards(): edge = lax.all_gather(jnp.stack(moved), 'c', axis=0, tiled=True)]
    pallas_call x1, Pallas kernels: 7.75 us -> 6.08 us  [shards(): call(functools.partial(pack_kernel, levels, tiles, (STEPS - 1) * row_coun...]
    unnamed x20 -> x15, local copies, waits for them, and re-layouts: 7.95 us -> 6.79 us
  transfers between devices with their start and end apart: 17 -> 14, of which waited for: 7 -> 5; matrix products, arithmetic and copies ran while one was open for 2% -> 2% of each run, Pallas kernels for 11% -> 10%
where the time goes in v6:
time: 159 us; the launch traced here: 158 us
  starting transfers between devices  85.8 us (54%)
  Pallas kernels  25.2 us (16%)
  waiting for transfers between devices  22.6 us (14%)
  blocking collectives  16 us (10%)
  local copies, waits for them, and re-layouts  6.79 us (4%)
    all_to_all x1, starting transfers between devices, shards(): winds = lax.all_to_all(payload, tile, 0, 0, tiled=True)  20.4 us
    ppermute x3, starting transfers between devices, to_sides(): lax.ppermute(sides[1], tile, back)  19.9 us
    ppermute x4, starting transfers between devices, shards(): moved.append(lax.ppermute(part, ('y', 'c'), route))  16.9 us
    ppermute x3, waiting for transfers between devices, to_sides(): lax.ppermute(sides[0], tile, ahead)  13.7 us
    all_to_all x2, starting transfers between devices, exchange(): return lax.all_to_all(chosen, 'y', 0, 0, tiled=True)  12.7 us
    all_gather x2, blocking collectives, exchange(): gathered = lax.all_gather(item, group, axis=0, tiled=False)  11.6 us
    ppermute x3, starting transfers between devices, to_sides(): lax.ppermute(sides[0], tile, ahead)  10.8 us
    pallas_call x2, Pallas kernels, inner(): call(functools.partial(inner_kernel, step, levels, opening), (sds(turned....  7.53 us
  transfers between devices with their start and end apart: 14, of which 5 were waited for; matrix products, arithmetic and copies ran while one was open for 2% of the time, Pallas kernels for 10%

profile of v6, /device:TPU:24, one launch (start us, length us, event | category | flops | bytes accessed | tf_op | source)
XLA Modules:
  0.0 158.1 jit_solution(645436138408062249)
XLA Ops:
  3.5 5.2 %collective-permute-start = (bf16[4,40,128]{2,1,0:T(8,128)(2,1)S(1)}, bf16[4,40,128]{2,1,0:T(8,128)(2,1)S(1)}, u32[]{:S(2)}, u32[]{:S(2)}) collective-permute-start(bf16[4,40,128]{2,1,0:T(8,128)(2,1)S(1)} %get-tuple-element.30), channel_id=1, source_target_pairs={{0,512},{512,0},{1,513},{513,1},{2,514},{514,2},{3,515},{515,3},{4... | collective-permute-start | bytes 122888 | tf_op jit(solution)/shard_map/ppermute | solution.py:555
  8.7 3.1 %copy.11 = bf16[1,96,2,36,128]{4,3,2,1,0:T(8,128)(2,1)} copy(bf16[1,96,2,36,128]{4,2,3,1,0:T(2,128)(2,1)} %param.8) | data formatting | bytes 3538944 | tf_op args[1]
  11.8 6.1 %shard_map.74 = bf16[896,8,128]{2,1,0:T(8,128)(2,1)} custom-call(s32[1,96]{1,0:T(1,128)} %owner.1, s32[1,96]{1,0:T(1,128)} %unit.1, s32[1,96]{1,0:T(1,128)} %valid.1, bf16[96,2,36,128]{3,2,1,0:T(8,128)(2,1)} %bitcast.24), custom_call_target="tpu_custom_call" | custom-call | flops 1048576 | bytes 1048576 | tf_op jit(solution)/shard_map/pallas_call | solution.py:511
  17.9 20.4 %all-to-all-start = ((bf16[896,8,128]{2,1,0:T(8,128)(2,1)}), bf16[896,8,128]{2,1,0:T(8,128)(2,1)S(1)}, u32[]{:S(2)}, u32[]{:S(2)}) async-start(bf16[896,8,128]{2,1,0:T(8,128)(2,1)} %shard_map.74), calls=%async_computation | async-start | bytes 3670016 | tf_op jit(solution)/shard_map/all_to_all | solution.py:557
  41.0 3.6 %collective-permute-start.1 = (bf16[12,40,128]{2,1,0:T(8,128)(2,1)S(1)}, bf16[12,40,128]{2,1,0:T(8,128)(2,1)S(1)}, u32[]{:S(2)}, u32[]{:S(2)}) collective-permute-start(bf16[12,40,128]{2,1,0:T(8,128)(2,1)S(1)} %get-tuple-element.33), channel_id=1, source_target_pairs={{0,64},{32,480},{64,128},{96,32},{128,192},{160,96},{192,256},{224... | collective-permute-start | bytes 368648 | tf_op jit(solution)/shard_map/ppermute | solution.py:571
  44.6 5.9 %collective-permute-start.2 = (bf16[12,40,128]{2,1,0:T(8,128)(2,1)S(1)}, bf16[12,40,128]{2,1,0:T(8,128)(2,1)S(1)}, u32[]{:S(2)}, u32[]{:S(2)}) collective-permute-start(bf16[12,40,128]{2,1,0:T(8,128)(2,1)S(1)} %get-tuple-element.34), channel_id=1, source_target_pairs={{0,128},{32,416},{64,192},{96,480},{128,256},{160,32},{192,320},{2... | collective-permute-start | bytes 368648 | tf_op jit(solution)/shard_map/ppermute | solution.py:571
  50.5 3.2 %collective-permute-start.3 = (bf16[12,40,128]{2,1,0:T(8,128)(2,1)S(1)}, bf16[12,40,128]{2,1,0:T(8,128)(2,1)S(1)}, u32[]{:S(2)}, u32[]{:S(2)}) collective-permute-start(bf16[12,40,128]{2,1,0:T(8,128)(2,1)S(1)} %get-tuple-element.35), channel_id=1, source_target_pairs={{0,192},{32,352},{64,256},{96,416},{128,320},{160,480},{192,384},{... | collective-permute-start | bytes 368648 | tf_op jit(solution)/shard_map/ppermute | solution.py:571
  53.7 4.3 %collective-permute-start.4 = (bf16[12,40,128]{2,1,0:T(8,128)(2,1)S(1)}, bf16[12,40,128]{2,1,0:T(8,128)(2,1)S(1)}, u32[]{:S(2)}, u32[]{:S(2)}) collective-permute-start(bf16[12,40,128]{2,1,0:T(8,128)(2,1)S(1)} %get-tuple-element.36), channel_id=1, source_target_pairs={{0,256},{64,320},{128,384},{192,448},{256,0},{320,64},{384,128},{4... | collective-permute-start | bytes 368648 | tf_op jit(solution)/shard_map/ppermute | solution.py:571
  57.9 4.3 %collective-permute-start.5 = (f32[40,128]{1,0:T(8,128)}, f32[40,128]{1,0:T(8,128)S(1)}, u32[]{:S(2)}, u32[]{:S(2)}) collective-permute-start(f32[40,128]{1,0:T(8,128)} %get-tuple-element.41), channel_id=1, source_target_pairs={{0,1},{1,2},{2,3},{3,4},{4,5},{5,6},{6,7},{7,8},{8,9},{9,10},{10,1... | collective-permute-start | bytes 61448 | tf_op jit(solution)/shard_map/ppermute | solution.py:543
  62.2 5.8 %collective-permute-start.6 = (f32[40,128]{1,0:T(8,128)S(1)}, f32[40,128]{1,0:T(8,128)S(1)}, u32[]{:S(2)}, u32[]{:S(2)}) collective-permute-start(f32[40,128]{1,0:T(8,128)S(1)} %get-tuple-element.42), channel_id=1, source_target_pairs={{1,0},{2,1},{3,2},{4,3},{5,4},{6,5},{7,6},{8,7},{9,8},{10,9},{11,1... | collective-permute-start | bytes 61448 | tf_op jit(solution)/shard_map/ppermute | solution.py:543
  68.1 2.5 %all_gather.23.edge = bf16[8,12,40,128]{3,2,1,0:T(8,128)(2,1)S(1)} all-gather(bf16[4,12,40,128]{3,2,1,0:T(8,128)(2,1)S(1)} %pad_maximum_fusion), channel_id=1, replica_groups=mesh['zl'=2,'y'=8,'c'=2,'x'=8,'zh'=4] {'c'}, dimensions={0}, use_global_device_ids=true | all-gather | bytes 1474560 | tf_op jit(solution)/shard_map/all_gather | solution.py:572
  71.2 13.7 %collective-permute-done.5.from_west = f32[40,128]{1,0:T(8,128)S(1)} collective-permute-done((f32[40,128]{1,0:T(8,128)}, f32[40,128]{1,0:T(8,128)S(1)}, u32[]{:S(2)}, u32[]{:S(2)}) %collective-permute-start.5) | collective-permute-done | bytes 20512 | tf_op jit(solution)/shard_map/ppermute | solution.py:543
  84.9 3.6 %all-to-all-done.winds = bf16[896,8,128]{2,1,0:T(8,128)(2,1)S(1)} async-done(((bf16[896,8,128]{2,1,0:T(8,128)(2,1)}), bf16[896,8,128]{2,1,0:T(8,128)(2,1)S(1)}, u32[]{:S(2)}, u32[]{:S(2)}) %all-to-all-start) | async-done | bytes 1835040 | tf_op jit(solution)/shard_map/all_to_all | solution.py:557
  91.7 6.0 %all-gather.1 = bf16[28,40,128]{2,1,0:T(8,128)(2,1)S(1)} all-gather(bf16[7,40,128]{2,1,0:T(8,128)(2,1)S(1)} %get-tuple-element.47), channel_id=3, replica_groups=mesh['zl'=2,'y'=8,'c'=2,'x'=8,'zh'=4] {'zl','c'}, dimensions={0}, use_global_device_ids=true | all-gather | bytes 358400 | tf_op jit(solution)/shard_map/all_gather | solution.py:546
  99.1 7.8 %all-to-all-start.1 = ((bf16[8,7,40,128]{3,2,1,0:T(8,128)(2,1)}), bf16[8,7,40,128]{3,2,1,0:T(8,128)(2,1)}, u32[]{:S(2)}, u32[]{:S(2)}) async-start(bf16[8,7,40,128]{3,2,1,0:T(8,128)(2,1)} %shard_map.79), calls=%async_computation.1 | async-start | bytes 1146880 | tf_op jit(solution)/shard_map/all_to_all | solution.py:553
  106.9 3.8 %shard_map.78 = (f32[16,2,40,128]{3,2,1,0:T(8,128)S(1)}, f32[40,128]{1,0:T(8,128)S(1)}, f32[40,128]{1,0:T(8,128)S(1)}) custom-call(s32[1,128]{1,0:T(1,128)S(1)} %get-tuple-element.43.found, bf16[896,8,128]{2,1,0:T(8,128)(2,1)S(1)} %all-to-all-done.winds, f32[16,2,40,128]{3,2,1,0:T(8,128)S(1)} %get-tuple-element.40.adj, f32[9,40,128]{2,1,0:T(8,128)S(1)} %copy-done.3, ...), custom_call_target="tpu_custom_call" | custom-call | flops 1048576 | bytes 1048576 | tf_op jit(solution)/shard_map/pallas_call | solution.py:588
  110.7 3.2 %collective-permute-start.7 = (f32[40,128]{1,0:T(8,128)S(1)}, f32[40,128]{1,0:T(8,128)S(1)}, u32[]{:S(2)}, u32[]{:S(2)}) collective-permute-start(f32[40,128]{1,0:T(8,128)S(1)} %get-tuple-element.48), channel_id=1, source_target_pairs={{0,1},{1,2},{2,3},{3,4},{4,5},{5,6},{6,7},{7,8},{8,9},{9,10},{10,1... | collective-permute-start | bytes 61448 | tf_op jit(solution)/shard_map/ppermute | solution.py:543
  114.0 6.8 %collective-permute-start.8 = (f32[40,128]{1,0:T(8,128)S(1)}, f32[40,128]{1,0:T(8,128)S(1)}, u32[]{:S(2)}, u32[]{:S(2)}) collective-permute-start(f32[40,128]{1,0:T(8,128)S(1)} %get-tuple-element.49), channel_id=1, source_target_pairs={{1,0},{2,1},{3,2},{4,3},{5,4},{6,5},{7,6},{8,7},{9,8},{10,9},{11,1... | collective-permute-start | bytes 61448 | tf_op jit(solution)/shard_map/ppermute | solution.py:543
  122.2 2.4 %all-to-all-done.1.edge = bf16[8,7,40,128]{3,2,1,0:T(8,128)(2,1)} async-done(((bf16[8,7,40,128]{3,2,1,0:T(8,128)(2,1)}), bf16[8,7,40,128]{3,2,1,0:T(8,128)(2,1)}, u32[]{:S(2)}, u32[]{:S(2)}) %all-to-all-start.1) | async-done | bytes 573472 | tf_op jit(solution)/shard_map/all_to_all | solution.py:553
  126.1 5.6 %all-gather.2 = bf16[20,40,128]{2,1,0:T(8,128)(2,1)S(1)} all-gather(bf16[5,40,128]{2,1,0:T(8,128)(2,1)S(1)} %get-tuple-element.52), channel_id=4, replica_groups=mesh['zl'=2,'y'=8,'c'=2,'x'=8,'zh'=4] {'zl','c'}, dimensions={0}, use_global_device_ids=true | all-gather | bytes 256000 | tf_op jit(solution)/shard_map/all_gather | solution.py:546
  133.1 4.9 %all-to-all-start.2 = ((bf16[8,5,40,128]{3,2,1,0:T(8,128)(2,1)}), bf16[8,5,40,128]{3,2,1,0:T(8,128)(2,1)S(1)}, u32[]{:S(2)}, u32[]{:S(2)}) async-start(bf16[8,5,40,128]{3,2,1,0:T(8,128)(2,1)} %shard_map.82), calls=%async_computation.2 | async-start | bytes 819200 | tf_op jit(solution)/shard_map/all_to_all | solution.py:553
  139.1 3.8 %shard_map.81 = (f32[16,2,40,128]{3,2,1,0:T(8,128)S(1)}, f32[40,128]{1,0:T(8,128)S(1)}, f32[40,128]{1,0:T(8,128)S(1)}) custom-call(s32[1,128]{1,0:T(1,128)S(1)} %get-tuple-element.43.found, bf16[896,8,128]{2,1,0:T(8,128)(2,1)S(1)} %all-to-all-done.winds, f32[16,2,40,128]{3,2,1,0:T(8,128)S(1)} %copy-done.1, f32[6,40,128]{2,1,0:T(8,128)S(1)} %get-tuple-element.50.ends, ...), custom_call_target="tpu_custom_call" | custom-call | flops 1048576 | bytes 1048576 | tf_op jit(solution)/shard_map/pallas_call | solution.py:588
  142.8 3.2 %collective-permute-start.9 = (f32[40,128]{1,0:T(8,128)S(1)}, f32[40,128]{1,0:T(8,128)S(1)}, u32[]{:S(2)}, u32[]{:S(2)}) collective-permute-start(f32[40,128]{1,0:T(8,128)S(1)} %get-tuple-element.53), channel_id=1, source_target_pairs={{0,1},{1,2},{2,3},{3,4},{4,5},{5,6},{6,7},{7,8},{8,9},{9,10},{10,1... | collective-permute-start | bytes 61448 | tf_op jit(solution)/shard_map/ppermute | solution.py:543
  146.1 7.3 %collective-permute-start.10 = (f32[40,128]{1,0:T(8,128)S(1)}, f32[40,128]{1,0:T(8,128)S(1)}, u32[]{:S(2)}, u32[]{:S(2)}) collective-permute-start(f32[40,128]{1,0:T(8,128)S(1)} %get-tuple-element.54), channel_id=1, source_target_pairs={{1,0},{2,1},{3,2},{4,3},{5,4},{6,5},{7,6},{8,7},{9,8},{10,9},{11,1... | collective-permute-start | bytes 61448 | tf_op jit(solution)/shard_map/ppermute | solution.py:543
  (38 shorter events, 20.3 us)
Async XLA Ops:
  1.3 1.1 copy-start.4
  3.5 14.3 %collective-permute-start = (bf16[4,40,128]{2,1,0:T(8,128)(2,1)S(1)}, bf16[4,40,128]{2,1,0:T(8,128)(2,1)S(1)}, u32[]{:S(2)}, u32[]{:S(2)}) collective-permute-start(bf16[4,40,128]{2,1,0:T(8,128)(2,1)S(1)} %get-tuple-element.30), channel_id=1, source_target_pairs={{0,512},{512,0},{1,513},{513,1},{2,514},{514,2},{3,515},{515,3},{4... | collective-permute-start | bytes 122888 | tf_op jit(solution)/shard_map/ppermute | solution.py:555
  17.9 70.6 %all-to-all-start = ((bf16[896,8,128]{2,1,0:T(8,128)(2,1)}), bf16[896,8,128]{2,1,0:T(8,128)(2,1)S(1)}, u32[]{:S(2)}, u32[]{:S(2)}) async-start(bf16[896,8,128]{2,1,0:T(8,128)(2,1)} %shard_map.74), calls=%async_computation | async-start | bytes 3670016 | tf_op jit(solution)/shard_map/all_to_all | solution.py:557
  41.0 44.0 %copy-start.5 = (bf16[12,40,128]{2,1,0:T(8,128)(2,1)}, bf16[12,40,128]{2,1,0:T(8,128)(2,1)S(1)}, u32[]{:S(2)}) copy-start(bf16[12,40,128]{2,1,0:T(8,128)(2,1)S(1)} %get-tuple-element.32.own) | copy-start | bytes 368644
  41.0 21.3 %collective-permute-start.1 = (bf16[12,40,128]{2,1,0:T(8,128)(2,1)S(1)}, bf16[12,40,128]{2,1,0:T(8,128)(2,1)S(1)}, u32[]{:S(2)}, u32[]{:S(2)}) collective-permute-start(bf16[12,40,128]{2,1,0:T(8,128)(2,1)S(1)} %get-tuple-element.33), channel_id=1, source_target_pairs={{0,64},{32,480},{64,128},{96,32},{128,192},{160,96},{192,256},{224... | collective-permute-start | bytes 368648 | tf_op jit(solution)/shard_map/ppermute | solution.py:571
  44.6 23.5 %collective-permute-start.2 = (bf16[12,40,128]{2,1,0:T(8,128)(2,1)S(1)}, bf16[12,40,128]{2,1,0:T(8,128)(2,1)S(1)}, u32[]{:S(2)}, u32[]{:S(2)}) collective-permute-start(bf16[12,40,128]{2,1,0:T(8,128)(2,1)S(1)} %get-tuple-element.34), channel_id=1, source_target_pairs={{0,128},{32,416},{64,192},{96,480},{128,256},{160,32},{192,320},{2... | collective-permute-start | bytes 368648 | tf_op jit(solution)/shard_map/ppermute | solution.py:571
  50.5 17.5 %collective-permute-start.3 = (bf16[12,40,128]{2,1,0:T(8,128)(2,1)S(1)}, bf16[12,40,128]{2,1,0:T(8,128)(2,1)S(1)}, u32[]{:S(2)}, u32[]{:S(2)}) collective-permute-start(bf16[12,40,128]{2,1,0:T(8,128)(2,1)S(1)} %get-tuple-element.35), channel_id=1, source_target_pairs={{0,192},{32,352},{64,256},{96,416},{128,320},{160,480},{192,384},{... | collective-permute-start | bytes 368648 | tf_op jit(solution)/shard_map/ppermute | solution.py:571
  53.7 14.4 %collective-permute-start.4 = (bf16[12,40,128]{2,1,0:T(8,128)(2,1)S(1)}, bf16[12,40,128]{2,1,0:T(8,128)(2,1)S(1)}, u32[]{:S(2)}, u32[]{:S(2)}) collective-permute-start(bf16[12,40,128]{2,1,0:T(8,128)(2,1)S(1)} %get-tuple-element.36), channel_id=1, source_target_pairs={{0,256},{64,320},{128,384},{192,448},{256,0},{320,64},{384,128},{4... | collective-permute-start | bytes 368648 | tf_op jit(solution)/shard_map/ppermute | solution.py:571
  57.9 27.0 %collective-permute-start.5 = (f32[40,128]{1,0:T(8,128)}, f32[40,128]{1,0:T(8,128)S(1)}, u32[]{:S(2)}, u32[]{:S(2)}) collective-permute-start(f32[40,128]{1,0:T(8,128)} %get-tuple-element.41), channel_id=1, source_target_pairs={{0,1},{1,2},{2,3},{3,4},{4,5},{5,6},{6,7},{7,8},{8,9},{9,10},{10,1... | collective-permute-start | bytes 61448 | tf_op jit(solution)/shard_map/ppermute | solution.py:543
  62.2 22.7 %collective-permute-start.6 = (f32[40,128]{1,0:T(8,128)S(1)}, f32[40,128]{1,0:T(8,128)S(1)}, u32[]{:S(2)}, u32[]{:S(2)}) collective-permute-start(f32[40,128]{1,0:T(8,128)S(1)} %get-tuple-element.42), channel_id=1, source_target_pairs={{1,0},{2,1},{3,2},{4,3},{5,4},{6,5},{7,6},{8,7},{9,8},{10,9},{11,1... | collective-permute-start | bytes 61448 | tf_op jit(solution)/shard_map/ppermute | solution.py:543
  88.5 0.9 copy-start.6
  91.0 0.7 copy-start.2
  91.7 15.3 %copy-start.3 = (f32[9,40,128]{2,1,0:T(8,128)S(1)}, f32[9,40,128]{2,1,0:T(8,128)}, u32[]{:S(2)}) copy-start(f32[9,40,128]{2,1,0:T(8,128)} %copy-done.2) | copy-start | bytes 552964
  99.1 25.5 %all-to-all-start.1 = ((bf16[8,7,40,128]{3,2,1,0:T(8,128)(2,1)}), bf16[8,7,40,128]{3,2,1,0:T(8,128)(2,1)}, u32[]{:S(2)}, u32[]{:S(2)}) async-start(bf16[8,7,40,128]{3,2,1,0:T(8,128)(2,1)} %shard_map.79), calls=%async_computation.1 | async-start | bytes 1146880 | tf_op jit(solution)/shard_map/all_to_all | solution.py:553
  110.7 22.4 %copy-start = (f32[16,2,40,128]{3,2,1,0:T(8,128)}, f32[16,2,40,128]{3,2,1,0:T(8,128)S(1)}, u32[]{:S(2)}) copy-start(f32[16,2,40,128]{3,2,1,0:T(8,128)S(1)} %get-tuple-element.46.adj) | copy-start | bytes 1966084
  110.7 10.1 %collective-permute-start.7 = (f32[40,128]{1,0:T(8,128)S(1)}, f32[40,128]{1,0:T(8,128)S(1)}, u32[]{:S(2)}, u32[]{:S(2)}) collective-permute-start(f32[40,128]{1,0:T(8,128)S(1)} %get-tuple-element.48), channel_id=1, source_target_pairs={{0,1},{1,2},{2,3},{3,4},{4,5},{5,6},{6,7},{7,8},{8,9},{9,10},{10,1... | collective-permute-start | bytes 61448 | tf_op jit(solution)/shard_map/ppermute | solution.py:543
  114.0 8.3 %collective-permute-start.8 = (f32[40,128]{1,0:T(8,128)S(1)}, f32[40,128]{1,0:T(8,128)S(1)}, u32[]{:S(2)}, u32[]{:S(2)}) collective-permute-start(f32[40,128]{1,0:T(8,128)S(1)} %get-tuple-element.49), channel_id=1, source_target_pairs={{1,0},{2,1},{3,2},{4,3},{5,4},{6,5},{7,6},{8,7},{9,8},{10,9},{11,1... | collective-permute-start | bytes 61448 | tf_op jit(solution)/shard_map/ppermute | solution.py:543
  133.1 23.2 %all-to-all-start.2 = ((bf16[8,5,40,128]{3,2,1,0:T(8,128)(2,1)}), bf16[8,5,40,128]{3,2,1,0:T(8,128)(2,1)S(1)}, u32[]{:S(2)}, u32[]{:S(2)}) async-start(bf16[8,5,40,128]{3,2,1,0:T(8,128)(2,1)} %shard_map.82), calls=%async_computation.2 | async-start | bytes 819200 | tf_op jit(solution)/shard_map/all_to_all | solution.py:553
  138.0 1.1 copy-start.1
  142.8 10.5 %collective-permute-start.9 = (f32[40,128]{1,0:T(8,128)S(1)}, f32[40,128]{1,0:T(8,128)S(1)}, u32[]{:S(2)}, u32[]{:S(2)}) collective-permute-start(f32[40,128]{1,0:T(8,128)S(1)} %get-tuple-element.53), channel_id=1, source_target_pairs={{0,1},{1,2},{2,3},{3,4},{4,5},{5,6},{6,7},{7,8},{8,9},{9,10},{10,1... | collective-permute-start | bytes 61448 | tf_op jit(solution)/shard_map/ppermute | solution.py:543
  146.1 8.8 %collective-permute-start.10 = (f32[40,128]{1,0:T(8,128)S(1)}, f32[40,128]{1,0:T(8,128)S(1)}, u32[]{:S(2)}, u32[]{:S(2)}) collective-permute-start(f32[40,128]{1,0:T(8,128)S(1)} %get-tuple-element.54), channel_id=1, source_target_pairs={{1,0},{2,1},{3,2},{4,3},{5,4},{6,5},{7,6},{8,7},{9,8},{10,9},{11,1... | collective-permute-start | bytes 61448 | tf_op jit(solution)/shard_map/ppermute | solution.py:543

commit v7 on v6

--- a/solution.py
+++ b/solution.py
@@ -16,7 +16,7 @@
 LABEL, LABEL_EAST = 64, 65
 CHUNKS = 4
 HALF = 64
-MATCH, TURN = 40, 41
+MATCH, TURN = 96, 97
 EDGE_COLUMN = 32
 INTERPRET = False
 
@@ -143,11 +143,25 @@
         copy.wait()
 
 
-def edges_kernel(levels, row_count, match, turn, adj, turned, item, last_out, head_out):
+class Columns:
+    def __init__(self, width):
+        self.pair = lax.shift_right_logical(lanes(PAD, width), 1)
+        self.held = jnp.zeros((PAD, width), F32)
+
+    def add(self, q, v):
+        self.held = jnp.where(self.pair == q, pltpu.roll(v, 2 * q + 1, 1), self.held)
+
+
+def joined(from_west, from_east):
+    shape = from_west.shape
+    even = (lanes(*shape) & 1) == 0
+    return jnp.where(even, pltpu.roll(from_east[...], shape[1] - 1, 1), pltpu.roll(from_west[...], 1, 1))
+
+
+def edges_kernel(levels, row_count, match, turn, adj, turned, item, sides):
     width = adj.shape[1]
     lane = lanes(PAD, width)
-    last = jnp.zeros((PAD, width), F32)
-    head = jnp.zeros((PAD, width), F32)
+    columns = Columns(width)
     for r in range(row_count):
         for f in range(2):
             for l0 in range(0, levels, 8):
@@ -155,9 +169,7 @@
                 turned[r, f, l0 : l0 + n, :] = adj[pl.ds((f * levels + l0) * row_count + r, n, stride=row_count), :]
             turned[r, f, levels:PAD, :] = jnp.zeros((PAD - levels, width), F32)
             v = turned[r, f]
-            q = r * 2 + f
-            last = jnp.where(lane == q, spread(v, width - 1, v.shape), last)
-            head = jnp.where(lane == q, spread(v, 0, v.shape), head)
+            columns.add(r * 2 + f, v)
             if r == 0:
                 item[f] = v.astype(BF16)
             if r == row_count - 1:
@@ -166,9 +178,8 @@
                     v = jnp.where(level == levels, match[0, 0].astype(F32), v)
                     v = jnp.where(level == levels + 1, turn[0, 0].astype(F32), v)
                 item[2 + f] = v.astype(BF16)
-    for out, v in ((last_out, last), (head_out, head)):
-        v = jnp.where(lane == MATCH, match[0, 0].astype(F32), v)
-        out[...] = jnp.where(lane == TURN, turn[0, 0].astype(F32), v)
+    v = jnp.where(lane == MATCH, match[0, 0].astype(F32), columns.held)
+    sides[...] = jnp.where(lane == TURN, turn[0, 0].astype(F32), v)
 
 
 def tail(tile, levels):
@@ -291,7 +302,7 @@
     return jnp.concatenate([main, rest], axis=0)
 
 
-def advance(step, rows, levels, winds, found, east_wind, row, upper, lower, south_end, from_west, from_east, put):
+def advance(step, rows, levels, winds, found, east_wind, row, upper, lower, south_end, halo, put):
     row_count, width = ROWS, winds.shape[2]
     lane = lanes(PAD, width)
     base = step * row_count
@@ -315,8 +326,9 @@
         for f in range(2):
             q = r * 2 + f
             a = row(r, f)
-            west = jnp.where(lane == 0, spread(from_west, q, a.shape), pltpu.roll(a, 1, 1))
-            east = jnp.where(lane == width - 1, spread(from_east, q, a.shape), pltpu.roll(a, width - 1, 1))
+            beside = pltpu.roll(halo, width - 1 - 2 * q, 1)
+            west = jnp.where(lane == 0, beside, pltpu.roll(a, 1, 1))
+            east = jnp.where(lane == width - 1, beside, pltpu.roll(a, width - 1, 1))
             v = a + cw * (a - west)
             v = v + ce * (east - a)
             v = v + cn * (a - (row(r - 1, f) if r > 0 else upper[f]))
@@ -325,31 +337,8 @@
             put(r, f, v)
 
 
-class Columns:
-    def __init__(self, width):
-        self.lane = lanes(PAD, width)
-        self.last = self.head = jnp.zeros((PAD, width), F32)
-
-    def add(self, r, f, v):
-        here = self.lane == r * 2 + f
-        self.last = jnp.where(here, spread(v, v.shape[1] - 1, v.shape), self.last)
-        self.head = jnp.where(here, spread(v, 0, v.shape), self.head)
-
-    def write(self, last_out, head_out):
-        last_out[...] = self.last
-        head_out[...] = self.head
-
-
-def first_kernel(
-    step, levels, sizes, tiles,
-    code, inverse, where, winds, adj, own, edge, from_west, from_east,
-    item, kept, found_out, east_wind,
-    found, sem, extras,
-):
-    end, width = adj.shape[0] - 1, adj.shape[3]
+def prepare_kernel(sizes, code, inverse, where, own, edge, ends):
     mates = sizes[0] * sizes[2]
-    find_slots(levels, tiles, CAPACITY, winds, found_out, found, sem, extras)
-    east_wind[...] = extras[0:PAD, :]
     north, north_mate, turn_north, south, _, turn_south = neighbours(sizes, code, inverse, where)
     y, c, ny = where[0, 1], where[0, 2], sizes[1]
     half = ny // 2
@@ -360,8 +349,21 @@
         both = own[pl.ds(row, 2)].astype(F32), edge[i, pl.ds(row, 2)].astype(F32)
         return jnp.where(d == 0, *both).astype(BF16)
 
-    upper = oriented(arrived(north, 2 * north_mate), turn_north)
-    lower = oriented(arrived(south, 2 * (mates + c)), turn_south)
+    ends[0:2] = oriented(arrived(north, 2 * north_mate), turn_north)
+    ends[2:4] = oriented(arrived(south, 2 * (mates + c)), turn_south)
+
+
+def first_kernel(
+    step, levels, tiles,
+    winds, adj, ends, from_west, from_east,
+    item, kept, found_out, east_wind,
+    found, sem, extras,
+):
+    end, width = adj.shape[0] - 1, adj.shape[3]
+    find_slots(levels, tiles, CAPACITY, winds, found_out, found, sem, extras)
+    east_wind[...] = extras[0:PAD, :]
+    halo = joined(from_west, from_east)
+    upper = (ends[0], ends[1])
 
     def put(r, f, v):
         item[f if r == 0 else 4 + f] = v.astype(BF16)
@@ -370,12 +372,12 @@
     def row(r, f):
         return adj[r, f]
 
-    advance(step, (0, end), levels, winds, found, east_wind, row, upper, None, None, from_west, from_east, put)
+    advance(step, (0, end), levels, winds, found, east_wind, row, upper, None, None, halo, put)
     edge_wind = wind(levels, winds, found, step * ROWS, 1)
     item[2] = edge_wind.astype(BF16)
     item[3] = wind(levels, winds, found, (step - 1) * ROWS, 1).astype(BF16)
     for f in range(2):
-        kept[f] = lower[f] - adj[end, f]
+        kept[f] = ends[2 + f] - adj[end, f]
         kept[2 + f] = adj[0, f].astype(BF16).astype(F32) - upper[f]
     kept[4] = edge_wind
 
@@ -393,7 +395,7 @@
 
 
 def inner_kernel(
-    step, levels, opening, found, winds, adj, ends, from_west, from_east, east_wind, out, last_out, head_out
+    step, levels, opening, found, winds, adj, ends, from_west, from_east, east_wind, out, sides
 ):
     row_count, width = adj.shape[0], adj.shape[3]
     columns = Columns(width)
@@ -401,23 +403,20 @@
 
     def put(r, f, v):
         out[r, f] = v
-        columns.add(r, f, v)
+        columns.add(2 * r + f, v)
 
     def row(r, f):
         return ends[f] if r == row_count - 1 and not opening else adj[r, f]
 
     rows = range(1, row_count - 1)
-    advance(step, rows, levels, winds, found, east_wind, row, None, None, None, from_west, from_east, put)
+    advance(step, rows, levels, winds, found, east_wind, row, None, None, None, joined(from_west, from_east), put)
     for f in range(2):
         put(0, f, ends[first_at + f])
         put(row_count - 1, f, ends[last_at + f])
     if opening:
         for f in range(2):
-            v = ends[f]
-            here = columns.lane == EDGE_COLUMN + f
-            columns.last = jnp.where(here, spread(v, width - 1, v.shape), columns.last)
-            columns.head = jnp.where(here, spread(v, 0, v.shape), columns.head)
-    columns.write(last_out, head_out)
+            columns.add(EDGE_COLUMN + f, ends[f])
+    sides[...] = columns.held
 
 
 def middle_kernel(
@@ -447,7 +446,8 @@
         cs = COURANT * jnp.maximum(corner, 0.0)
         mended = columns
         for f in range(2):
-            mended = jnp.where(lane == 2 * end + f, columns + cs * spread(columns, EDGE_COLUMN + f, shape), mended)
+            change = cs * spread(columns, 2 * (EDGE_COLUMN + f) + i, shape)
+            mended = jnp.where(lane == 2 * (2 * end + f) + i, columns + change, mended)
         sides.append(mended)
 
     def put(r, f, v):
@@ -457,28 +457,15 @@
     def row(r, f):
         return final[f] if r == end else adj[r, f]
 
-    advance(step, (0, end), levels, winds, found, east_wind, row, northern, lower, lower[3], *sides, put)
+    advance(step, (0, end), levels, winds, found, east_wind, row, northern, lower, lower[3], joined(*sides), put)
     both[0] = final[0]
     both[1] = final[1]
     item[2] = wind(levels, winds, found, (step - 1) * ROWS, 1).astype(BF16)
 
 
-def late_kernel(step, levels, found, winds, adj, from_west, from_east, east_wind, out):
-    rows = range(1, adj.shape[0] - 1)
-
-    def put(r, f, v):
-        out[r - 1, f] = v
-
-    def row(r, f):
-        return adj[r, f]
-
-    advance(step, rows, levels, winds, found, east_wind, row, None, None, None, from_west, from_east, put)
-
-
 def last_kernel(
-    step, levels, sizes, code, inverse, where, found, winds, adj, edge, from_west, from_east, east_wind, inner, out
+    step, levels, sizes, code, inverse, where, found, winds, adj, edge, from_west, from_east, east_wind, out
 ):
-    end = adj.shape[0] - 1
     north, _, turn_north, south, _, turn_south = neighbours(sizes, code, inverse, where)
     upper = oriented(edge[north, 3:5], turn_north)
     lower = oriented(edge[south, 0:3], turn_south)
@@ -491,10 +478,8 @@
     def row(r, f):
         return adj[r, f]
 
-    for r in range(1, end):
-        for f in range(2):
-            put(r, f, inner[r - 1, f])
-    advance(step, (0, end), levels, winds, found, east_wind, row, upper, lower, lower[2], from_west, from_east, put)
+    halo = joined(from_west, from_east)
+    advance(step, range(ROWS), levels, winds, found, east_wind, row, upper, lower, lower[2], halo, put)
 
 
 def shards(sizes, tile_sizes, adjoint_end, stored_rows, stored_owner, stored_unit, stored_valid, edge_match, edge_turn):
@@ -528,11 +513,11 @@
         61 << 20,
     )(stored_owner, stored_unit, stored_valid, stored_rows[0])
 
-    turned, item, *sides = call(
+    turned, item, sides = call(
         functools.partial(edges_kernel, levels, row_count),
-        (sds((row_count, 2, PAD, width), F32), sds((4, PAD, width), BF16), side, side),
+        (sds((row_count, 2, PAD, width), F32), sds((4, PAD, width), BF16), side),
         [SM, SM, VM],
-        (VM,) * 4,
+        (VM,) * 3,
     )(edge_match, edge_turn, adjoint_end.reshape(2 * levels * row_count, width))
 
     planes, mates = sizes[1], sizes[0] * sizes[2]
@@ -540,7 +525,7 @@
     def to_sides(sides):
         ahead = [(i, (i + 1) % tiles) for i in range(tiles)]
         back = [((i + 1) % tiles, i) for i in range(tiles)]
-        return lax.ppermute(sides[0], tile, ahead), lax.ppermute(sides[1], tile, back)
+        return lax.ppermute(sides, tile, ahead), lax.ppermute(sides, tile, back)
 
     def exchange(item, north_from, rows):
         gathered = lax.all_gather(item, group, axis=0, tiled=False)
@@ -575,23 +560,26 @@
         functools.partial(code_kernel, sizes, levels), (table, table), [SM, VM, VM], (VM, VM)
     )(where, own, edge)
 
+    ends = call(
+        functools.partial(prepare_kernel, sizes), sds((4, PAD, width), F32), [SM, SM, SM, VM, VM], VM
+    )(code, inverse, where, own, edge)
+
     item, kept, found, east_wind = call(
-        functools.partial(first_kernel, STEPS - 1, levels, sizes, tiles),
+        functools.partial(first_kernel, STEPS - 1, levels, tiles),
         (sds((7, PAD, width), BF16), sds((9, PAD, width), F32), table, side),
-        [SM, SM, SM] + [VM] * 6,
+        [VM] * 5,
         (VM,) * 4,
         [pltpu.SMEM((1, width), jnp.int32), pltpu.SemaphoreType.DMA, pltpu.VMEM((width, width), F32)],
-    )(code, inverse, where, winds, turned, own, edge, from_west, from_east)
+    )(winds, turned, ends, from_west, from_east)
     edge = exchange(item, 4, 6)
 
     def inner(step, opening, adj, ends):
-        adj, *sides = call(
+        return call(
             functools.partial(inner_kernel, step, levels, opening),
-            (sds(turned.shape, F32), side, side),
+            (sds(turned.shape, F32), side),
             [SM] + [VM] * 6,
-            (VM,) * 3,
+            (VM,) * 2,
         )(found, winds, adj, ends, from_west, from_east, east_wind)
-        return adj, sides
 
     adj, sides = inner(STEPS - 1, True, turned, kept)
     from_west, from_east = to_sides(sides)
@@ -605,18 +593,12 @@
     adj, sides = inner(STEPS - 2, False, adj, both)
 
     from_west, from_east = to_sides(sides)
-    late = call(
-        functools.partial(late_kernel, STEPS - 3, levels),
-        sds((row_count - 2,) + turned.shape[1:], F32),
-        [SM] + [VM] * 5,
-        VM,
-    )(found, winds, adj, from_west, from_east, east_wind)
     out = call(
         functools.partial(last_kernel, STEPS - 3, levels, sizes),
         sds((2 * levels * row_count, width), F32),
-        [SM] * 4 + [VM] * 7,
+        [SM] * 4 + [VM] * 6,
         VM,
-    )(code, inverse, where, found, winds, adj, edge, from_west, from_east, east_wind, late)
+    )(code, inverse, where, found, winds, adj, edge, from_west, from_east, east_wind)
     return out.reshape(adjoint_end.shape)
 
 

time: 159 us -> 161 us (1.013)
  waiting for transfers between devices: 22.6 us -> 28.9 us
  Pallas kernels: 25.2 us -> 22 us
    ppermute x6, waiting for transfers between devices: 16.6 us -> 22.3 us  [to_sides(): return (lax.ppermute(sides, tile, ahead), lax.ppermute(sides, tile, back))]
    pallas_call x2, Pallas kernels: 7.53 us -> 5.9 us  [inner(): call(functools.partial(inner_kernel, step, levels, opening), (sds(turned....]
    unnamed x15 -> x7, local copies, waits for them, and re-layouts: 6.79 us -> 6.08 us
  transfers between devices with their start and end apart: 14 -> 14, of which waited for: 5 -> 5; matrix products, arithmetic and copies ran while one was open for 2% -> 2% of each run, Pallas kernels for 10% -> 9%
where the time goes in v7:
time: 161 us; the launch traced here: 160 us
  starting transfers between devices  85.3 us (53%)
  waiting for transfers between devices  28.9 us (18%)
  Pallas kernels  22 us (14%)
  blocking collectives  15.9 us (10%)
  local copies, waits for them, and re-layouts  6.08 us (4%)
    ppermute x6, starting transfers between devices, to_sides(): return (lax.ppermute(sides, tile, ahead), lax.ppermute(sides, tile, back))  29.8 us
    ppermute x6, waiting for transfers between devices, to_sides(): return (lax.ppermute(sides, tile, ahead), lax.ppermute(sides, tile, back))  22.3 us
    all_to_all x1, starting transfers between devices, shards(): winds = lax.all_to_all(payload, tile, 0, 0, tiled=True)  20.4 us
    ppermute x4, starting transfers between devices, shards(): moved.append(lax.ppermute(part, ('y', 'c'), route))  16.9 us
    all_to_all x2, starting transfers between devices, exchange(): return lax.all_to_all(chosen, 'y', 0, 0, tiled=True)  12.9 us
    all_gather x2, blocking collectives, exchange(): gathered = lax.all_gather(item, group, axis=0, tiled=False)  11.5 us
    pallas_call x1, Pallas kernels, shards(): call(functools.partial(pack_kernel, levels, tiles, (STEPS - 1) * row_coun...  6.09 us
    unnamed x7, local copies, waits for them, and re-layouts  6.08 us
  transfers between devices with their start and end apart: 14, of which 5 were waited for; matrix products, arithmetic and copies ran while one was open for 2% of the time, Pallas kernels for 9%

profile of v7, /device:TPU:24, one launch (start us, length us, event | category | flops | bytes accessed | tf_op | source)
XLA Modules:
  0.0 159.9 jit_solution(14748712960842013554)
XLA Ops:
  2.7 5.2 %collective-permute-start = (bf16[4,40,128]{2,1,0:T(8,128)(2,1)S(1)}, bf16[4,40,128]{2,1,0:T(8,128)(2,1)S(1)}, u32[]{:S(2)}, u32[]{:S(2)}) collective-permute-start(bf16[4,40,128]{2,1,0:T(8,128)(2,1)S(1)} %get-tuple-element.27), channel_id=1, source_target_pairs={{0,512},{512,0},{1,513},{513,1},{2,514},{514,2},{3,515},{515,3},{4... | collective-permute-start | bytes 122888 | tf_op jit(solution)/shard_map/ppermute | solution.py:540
  7.9 3.1 %copy.11 = bf16[1,96,2,36,128]{4,3,2,1,0:T(8,128)(2,1)} copy(bf16[1,96,2,36,128]{4,2,3,1,0:T(2,128)(2,1)} %param.8) | data formatting | bytes 3538944 | tf_op args[1]
  11.0 6.1 %shard_map.74 = bf16[896,8,128]{2,1,0:T(8,128)(2,1)} custom-call(s32[1,96]{1,0:T(1,128)} %owner.1, s32[1,96]{1,0:T(1,128)} %unit.1, s32[1,96]{1,0:T(1,128)} %valid.1, bf16[96,2,36,128]{3,2,1,0:T(8,128)(2,1)} %bitcast.24), custom_call_target="tpu_custom_call" | custom-call | flops 1048576 | bytes 1048576 | tf_op jit(solution)/shard_map/pallas_call | solution.py:496
  17.1 20.4 %all-to-all-start = ((bf16[896,8,128]{2,1,0:T(8,128)(2,1)}), bf16[896,8,128]{2,1,0:T(8,128)(2,1)S(1)}, u32[]{:S(2)}, u32[]{:S(2)}) async-start(bf16[896,8,128]{2,1,0:T(8,128)(2,1)} %shard_map.74), calls=%async_computation | async-start | bytes 3670016 | tf_op jit(solution)/shard_map/all_to_all | solution.py:542
  40.2 4.7 %collective-permute-start.2 = (bf16[12,40,128]{2,1,0:T(8,128)(2,1)S(1)}, bf16[12,40,128]{2,1,0:T(8,128)(2,1)S(1)}, u32[]{:S(2)}, u32[]{:S(2)}) collective-permute-start(bf16[12,40,128]{2,1,0:T(8,128)(2,1)S(1)} %get-tuple-element.31), channel_id=1, source_target_pairs={{0,128},{32,416},{64,192},{96,480},{128,256},{160,32},{192,320},{2... | collective-permute-start | bytes 368648 | tf_op jit(solution)/shard_map/ppermute | solution.py:556
  44.9 5.3 %collective-permute-start.3 = (bf16[12,40,128]{2,1,0:T(8,128)(2,1)S(1)}, bf16[12,40,128]{2,1,0:T(8,128)(2,1)S(1)}, u32[]{:S(2)}, u32[]{:S(2)}) collective-permute-start(bf16[12,40,128]{2,1,0:T(8,128)(2,1)S(1)} %get-tuple-element.32), channel_id=1, source_target_pairs={{0,192},{32,352},{64,256},{96,416},{128,320},{160,480},{192,384},{... | collective-permute-start | bytes 368648 | tf_op jit(solution)/shard_map/ppermute | solution.py:556
  50.2 3.4 %collective-permute-start.4 = (bf16[12,40,128]{2,1,0:T(8,128)(2,1)S(1)}, bf16[12,40,128]{2,1,0:T(8,128)(2,1)S(1)}, u32[]{:S(2)}, u32[]{:S(2)}) collective-permute-start(bf16[12,40,128]{2,1,0:T(8,128)(2,1)S(1)} %get-tuple-element.33), channel_id=1, source_target_pairs={{0,256},{64,320},{128,384},{192,448},{256,0},{320,64},{384,128},{4... | collective-permute-start | bytes 368648 | tf_op jit(solution)/shard_map/ppermute | solution.py:556
  53.5 3.6 %collective-permute-start.1 = (bf16[12,40,128]{2,1,0:T(8,128)(2,1)S(1)}, bf16[12,40,128]{2,1,0:T(8,128)(2,1)S(1)}, u32[]{:S(2)}, u32[]{:S(2)}) collective-permute-start(bf16[12,40,128]{2,1,0:T(8,128)(2,1)S(1)} %get-tuple-element.30), channel_id=1, source_target_pairs={{0,64},{32,480},{64,128},{96,32},{128,192},{160,96},{192,256},{224... | collective-permute-start | bytes 368648 | tf_op jit(solution)/shard_map/ppermute | solution.py:556
  57.2 4.3 %collective-permute-start.5 = (f32[40,128]{1,0:T(8,128)S(1)}, f32[40,128]{1,0:T(8,128)S(1)}, u32[]{:S(2)}, u32[]{:S(2)}) collective-permute-start(f32[40,128]{1,0:T(8,128)S(1)} %get-tuple-element.38), channel_id=1, source_target_pairs={{0,1},{1,2},{2,3},{3,4},{4,5},{5,6},{6,7},{7,8},{8,9},{9,10},{10,1... | collective-permute-start | bytes 61448 | tf_op jit(solution)/shard_map/ppermute | solution.py:528
  61.4 5.8 %collective-permute-start.6 = (f32[40,128]{1,0:T(8,128)S(1)}, f32[40,128]{1,0:T(8,128)S(1)}, u32[]{:S(2)}, u32[]{:S(2)}) collective-permute-start(f32[40,128]{1,0:T(8,128)S(1)} %get-tuple-element.38), channel_id=1, source_target_pairs={{1,0},{2,1},{3,2},{4,3},{5,4},{6,5},{7,6},{8,7},{9,8},{10,9},{11,1... | collective-permute-start | bytes 61448 | tf_op jit(solution)/shard_map/ppermute | solution.py:528
  67.3 2.5 %all_gather.23.edge = bf16[8,12,40,128]{3,2,1,0:T(8,128)(2,1)S(1)} all-gather(bf16[4,12,40,128]{3,2,1,0:T(8,128)(2,1)S(1)} %pad_maximum_fusion), channel_id=1, replica_groups=mesh['zl'=2,'y'=8,'c'=2,'x'=8,'zh'=4] {'c'}, dimensions={0}, use_global_device_ids=true | all-gather | bytes 1474560 | tf_op jit(solution)/shard_map/all_gather | solution.py:557
  71.2 12.9 %collective-permute-done.5.from_west = f32[40,128]{1,0:T(8,128)S(1)} collective-permute-done((f32[40,128]{1,0:T(8,128)S(1)}, f32[40,128]{1,0:T(8,128)S(1)}, u32[]{:S(2)}, u32[]{:S(2)}) %collective-permute-start.5) | collective-permute-done | bytes 20512 | tf_op jit(solution)/shard_map/ppermute | solution.py:528
  84.1 3.4 %all-to-all-done.winds = bf16[896,8,128]{2,1,0:T(8,128)(2,1)S(1)} async-done(((bf16[896,8,128]{2,1,0:T(8,128)(2,1)}), bf16[896,8,128]{2,1,0:T(8,128)(2,1)S(1)}, u32[]{:S(2)}, u32[]{:S(2)}) %all-to-all-start) | async-done | bytes 1835040 | tf_op jit(solution)/shard_map/all_to_all | solution.py:542
  88.5 5.9 %all-gather.1 = bf16[28,40,128]{2,1,0:T(8,128)(2,1)S(1)} all-gather(bf16[7,40,128]{2,1,0:T(8,128)(2,1)S(1)} %get-tuple-element.43), channel_id=3, replica_groups=mesh['zl'=2,'y'=8,'c'=2,'x'=8,'zh'=4] {'zl','c'}, dimensions={0}, use_global_device_ids=true | all-gather | bytes 358400 | tf_op jit(solution)/shard_map/all_gather | solution.py:531
  95.9 8.1 %all-to-all-start.1 = ((bf16[8,7,40,128]{3,2,1,0:T(8,128)(2,1)}), bf16[8,7,40,128]{3,2,1,0:T(8,128)(2,1)}, u32[]{:S(2)}, u32[]{:S(2)}) async-start(bf16[8,7,40,128]{3,2,1,0:T(8,128)(2,1)} %shard_map.80), calls=%async_computation.1 | async-start | bytes 1146880 | tf_op jit(solution)/shard_map/all_to_all | solution.py:538
  103.9 3.0 %shard_map.79 = (f32[16,2,40,128]{3,2,1,0:T(8,128)S(1)}, f32[40,128]{1,0:T(8,128)S(1)}) custom-call(s32[1,128]{1,0:T(1,128)S(1)} %get-tuple-element.39.found, bf16[896,8,128]{2,1,0:T(8,128)(2,1)S(1)} %all-to-all-done.winds, f32[16,2,40,128]{3,2,1,0:T(8,128)S(1)} %get-tuple-element.37.adj, f32[9,40,128]{2,1,0:T(8,128)S(1)} %get-tuple-element.40.ends.kept, ...), custom_call_target="tpu_custom_call" | custom-call | flops 1048576 | bytes 1048576 | tf_op jit(solution)/shard_map/pallas_call | solution.py:577
  106.9 3.2 %collective-permute-start.7 = (f32[40,128]{1,0:T(8,128)S(1)}, f32[40,128]{1,0:T(8,128)S(1)}, u32[]{:S(2)}, u32[]{:S(2)}) collective-permute-start(f32[40,128]{1,0:T(8,128)S(1)} %get-tuple-element.44), channel_id=1, source_target_pairs={{0,1},{1,2},{2,3},{3,4},{4,5},{5,6},{6,7},{7,8},{8,9},{9,10},{10,1... | collective-permute-start | bytes 61448 | tf_op jit(solution)/shard_map/ppermute | solution.py:528
  110.1 6.9 %collective-permute-start.8 = (f32[40,128]{1,0:T(8,128)S(1)}, f32[40,128]{1,0:T(8,128)S(1)}, u32[]{:S(2)}, u32[]{:S(2)}) collective-permute-start(f32[40,128]{1,0:T(8,128)S(1)} %get-tuple-element.44), channel_id=1, source_target_pairs={{1,0},{2,1},{3,2},{4,3},{5,4},{6,5},{7,6},{8,7},{9,8},{10,9},{11,1... | collective-permute-start | bytes 61448 | tf_op jit(solution)/shard_map/ppermute | solution.py:528
  118.4 3.2 %all-to-all-done.1.edge = bf16[8,7,40,128]{3,2,1,0:T(8,128)(2,1)} async-done(((bf16[8,7,40,128]{3,2,1,0:T(8,128)(2,1)}), bf16[8,7,40,128]{3,2,1,0:T(8,128)(2,1)}, u32[]{:S(2)}, u32[]{:S(2)}) %all-to-all-start.1) | async-done | bytes 573472 | tf_op jit(solution)/shard_map/all_to_all | solution.py:538
  123.1 5.6 %all-gather.2 = bf16[20,40,128]{2,1,0:T(8,128)(2,1)S(1)} all-gather(bf16[5,40,128]{2,1,0:T(8,128)(2,1)S(1)} %get-tuple-element.47), channel_id=4, replica_groups=mesh['zl'=2,'y'=8,'c'=2,'x'=8,'zh'=4] {'zl','c'}, dimensions={0}, use_global_device_ids=true | all-gather | bytes 256000 | tf_op jit(solution)/shard_map/all_gather | solution.py:531
  130.2 4.9 %all-to-all-start.2 = ((bf16[8,5,40,128]{3,2,1,0:T(8,128)(2,1)}), bf16[8,5,40,128]{3,2,1,0:T(8,128)(2,1)S(1)}, u32[]{:S(2)}, u32[]{:S(2)}) async-start(bf16[8,5,40,128]{3,2,1,0:T(8,128)(2,1)} %shard_map.83), calls=%async_computation.2 | async-start | bytes 819200 | tf_op jit(solution)/shard_map/all_to_all | solution.py:538
  135.1 2.9 %shard_map.82 = (f32[16,2,40,128]{3,2,1,0:T(8,128)S(1)}, f32[40,128]{1,0:T(8,128)S(1)}) custom-call(s32[1,128]{1,0:T(1,128)S(1)} %get-tuple-element.39.found, bf16[896,8,128]{2,1,0:T(8,128)(2,1)S(1)} %all-to-all-done.winds, f32[16,2,40,128]{3,2,1,0:T(8,128)S(1)} %get-tuple-element.42.adj, f32[6,40,128]{2,1,0:T(8,128)S(1)} %get-tuple-element.45.ends, ...), custom_call_target="tpu_custom_call" | custom-call | flops 1048576 | bytes 1048576 | tf_op jit(solution)/shard_map/pallas_call | solution.py:577
  138.9 7.8 %collective-permute-start.10 = (f32[40,128]{1,0:T(8,128)S(1)}, f32[40,128]{1,0:T(8,128)S(1)}, u32[]{:S(2)}, u32[]{:S(2)}) collective-permute-start(f32[40,128]{1,0:T(8,128)S(1)} %get-tuple-element.48), channel_id=1, source_target_pairs={{1,0},{2,1},{3,2},{4,3},{5,4},{6,5},{7,6},{8,7},{9,8},{10,9},{11,1... | collective-permute-start | bytes 61448 | tf_op jit(solution)/shard_map/ppermute | solution.py:528
  148.6 8.0 %collective-permute-done.9.from_west = f32[40,128]{1,0:T(8,128)S(1)} collective-permute-done((f32[40,128]{1,0:T(8,128)S(1)}, f32[40,128]{1,0:T(8,128)S(1)}, u32[]{:S(2)}, u32[]{:S(2)}) %collective-permute-start.9) | collective-permute-done | bytes 20512 | tf_op jit(solution)/shard_map/ppermute | solution.py:528
  (30 shorter events, 18.4 us)
Async XLA Ops:
  1.3 1.1 copy-start.2
  2.7 14.4 %collective-permute-start = (bf16[4,40,128]{2,1,0:T(8,128)(2,1)S(1)}, bf16[4,40,128]{2,1,0:T(8,128)(2,1)S(1)}, u32[]{:S(2)}, u32[]{:S(2)}) collective-permute-start(bf16[4,40,128]{2,1,0:T(8,128)(2,1)S(1)} %get-tuple-element.27), channel_id=1, source_target_pairs={{0,512},{512,0},{1,513},{513,1},{2,514},{514,2},{3,515},{515,3},{4... | collective-permute-start | bytes 122888 | tf_op jit(solution)/shard_map/ppermute | solution.py:540
  17.1 70.4 %all-to-all-start = ((bf16[896,8,128]{2,1,0:T(8,128)(2,1)}), bf16[896,8,128]{2,1,0:T(8,128)(2,1)S(1)}, u32[]{:S(2)}, u32[]{:S(2)}) async-start(bf16[896,8,128]{2,1,0:T(8,128)(2,1)} %shard_map.74), calls=%async_computation | async-start | bytes 3670016 | tf_op jit(solution)/shard_map/all_to_all | solution.py:542
  40.2 21.3 %collective-permute-start.2 = (bf16[12,40,128]{2,1,0:T(8,128)(2,1)S(1)}, bf16[12,40,128]{2,1,0:T(8,128)(2,1)S(1)}, u32[]{:S(2)}, u32[]{:S(2)}) collective-permute-start(bf16[12,40,128]{2,1,0:T(8,128)(2,1)S(1)} %get-tuple-element.31), channel_id=1, source_target_pairs={{0,128},{32,416},{64,192},{96,480},{128,256},{160,32},{192,320},{2... | collective-permute-start | bytes 368648 | tf_op jit(solution)/shard_map/ppermute | solution.py:556
  44.9 22.3 %collective-permute-start.3 = (bf16[12,40,128]{2,1,0:T(8,128)(2,1)S(1)}, bf16[12,40,128]{2,1,0:T(8,128)(2,1)S(1)}, u32[]{:S(2)}, u32[]{:S(2)}) collective-permute-start(bf16[12,40,128]{2,1,0:T(8,128)(2,1)S(1)} %get-tuple-element.32), channel_id=1, source_target_pairs={{0,192},{32,352},{64,256},{96,416},{128,320},{160,480},{192,384},{... | collective-permute-start | bytes 368648 | tf_op jit(solution)/shard_map/ppermute | solution.py:556
  50.2 17.1 %collective-permute-start.4 = (bf16[12,40,128]{2,1,0:T(8,128)(2,1)S(1)}, bf16[12,40,128]{2,1,0:T(8,128)(2,1)S(1)}, u32[]{:S(2)}, u32[]{:S(2)}) collective-permute-start(bf16[12,40,128]{2,1,0:T(8,128)(2,1)S(1)} %get-tuple-element.33), channel_id=1, source_target_pairs={{0,256},{64,320},{128,384},{192,448},{256,0},{320,64},{384,128},{4... | collective-permute-start | bytes 368648 | tf_op jit(solution)/shard_map/ppermute | solution.py:556
  53.5 13.7 %collective-permute-start.1 = (bf16[12,40,128]{2,1,0:T(8,128)(2,1)S(1)}, bf16[12,40,128]{2,1,0:T(8,128)(2,1)S(1)}, u32[]{:S(2)}, u32[]{:S(2)}) collective-permute-start(bf16[12,40,128]{2,1,0:T(8,128)(2,1)S(1)} %get-tuple-element.30), channel_id=1, source_target_pairs={{0,64},{32,480},{64,128},{96,32},{128,192},{160,96},{192,256},{224... | collective-permute-start | bytes 368648 | tf_op jit(solution)/shard_map/ppermute | solution.py:556
  57.2 26.9 %collective-permute-start.5 = (f32[40,128]{1,0:T(8,128)S(1)}, f32[40,128]{1,0:T(8,128)S(1)}, u32[]{:S(2)}, u32[]{:S(2)}) collective-permute-start(f32[40,128]{1,0:T(8,128)S(1)} %get-tuple-element.38), channel_id=1, source_target_pairs={{0,1},{1,2},{2,3},{3,4},{4,5},{5,6},{6,7},{7,8},{8,9},{9,10},{10,1... | collective-permute-start | bytes 61448 | tf_op jit(solution)/shard_map/ppermute | solution.py:528
  61.4 22.6 %collective-permute-start.6 = (f32[40,128]{1,0:T(8,128)S(1)}, f32[40,128]{1,0:T(8,128)S(1)}, u32[]{:S(2)}, u32[]{:S(2)}) collective-permute-start(f32[40,128]{1,0:T(8,128)S(1)} %get-tuple-element.38), channel_id=1, source_target_pairs={{1,0},{2,1},{3,2},{4,3},{5,4},{6,5},{7,6},{8,7},{9,8},{10,9},{11,1... | collective-permute-start | bytes 61448 | tf_op jit(solution)/shard_map/ppermute | solution.py:528
  95.9 25.8 %all-to-all-start.1 = ((bf16[8,7,40,128]{3,2,1,0:T(8,128)(2,1)}), bf16[8,7,40,128]{3,2,1,0:T(8,128)(2,1)}, u32[]{:S(2)}, u32[]{:S(2)}) async-start(bf16[8,7,40,128]{3,2,1,0:T(8,128)(2,1)} %shard_map.80), calls=%async_computation.1 | async-start | bytes 1146880 | tf_op jit(solution)/shard_map/all_to_all | solution.py:538
  106.9 10.1 %collective-permute-start.7 = (f32[40,128]{1,0:T(8,128)S(1)}, f32[40,128]{1,0:T(8,128)S(1)}, u32[]{:S(2)}, u32[]{:S(2)}) collective-permute-start(f32[40,128]{1,0:T(8,128)S(1)} %get-tuple-element.44), channel_id=1, source_target_pairs={{0,1},{1,2},{2,3},{3,4},{4,5},{5,6},{6,7},{7,8},{8,9},{9,10},{10,1... | collective-permute-start | bytes 61448 | tf_op jit(solution)/shard_map/ppermute | solution.py:528
  110.1 8.3 %collective-permute-start.8 = (f32[40,128]{1,0:T(8,128)S(1)}, f32[40,128]{1,0:T(8,128)S(1)}, u32[]{:S(2)}, u32[]{:S(2)}) collective-permute-start(f32[40,128]{1,0:T(8,128)S(1)} %get-tuple-element.44), channel_id=1, source_target_pairs={{1,0},{2,1},{3,2},{4,3},{5,4},{6,5},{7,6},{8,7},{9,8},{10,9},{11,1... | collective-permute-start | bytes 61448 | tf_op jit(solution)/shard_map/ppermute | solution.py:528
  130.2 26.4 %all-to-all-start.2 = ((bf16[8,5,40,128]{3,2,1,0:T(8,128)(2,1)}), bf16[8,5,40,128]{3,2,1,0:T(8,128)(2,1)S(1)}, u32[]{:S(2)}, u32[]{:S(2)}) async-start(bf16[8,5,40,128]{3,2,1,0:T(8,128)(2,1)} %shard_map.83), calls=%async_computation.2 | async-start | bytes 819200 | tf_op jit(solution)/shard_map/all_to_all | solution.py:538
  138.0 0.9 copy-start
  138.9 9.7 %collective-permute-start.10 = (f32[40,128]{1,0:T(8,128)S(1)}, f32[40,128]{1,0:T(8,128)S(1)}, u32[]{:S(2)}, u32[]{:S(2)}) collective-permute-start(f32[40,128]{1,0:T(8,128)S(1)} %get-tuple-element.48), channel_id=1, source_target_pairs={{1,0},{2,1},{3,2},{4,3},{5,4},{6,5},{7,6},{8,7},{9,8},{10,9},{11,1... | collective-permute-start | bytes 61448 | tf_op jit(solution)/shard_map/ppermute | solution.py:528
  146.6 9.9 %collective-permute-start.9 = (f32[40,128]{1,0:T(8,128)S(1)}, f32[40,128]{1,0:T(8,128)S(1)}, u32[]{:S(2)}, u32[]{:S(2)}) collective-permute-start(f32[40,128]{1,0:T(8,128)S(1)} %get-tuple-element.48), channel_id=1, source_target_pairs={{0,1},{1,2},{2,3},{3,4},{4,5},{5,6},{6,7},{7,8},{8,9},{9,10},{10,1... | collective-permute-start | bytes 61448 | tf_op jit(solution)/shard_map/ppermute | solution.py:528
  156.5 1.1 copy-start.1

commit v8 on v7

--- a/solution.py
+++ b/solution.py
@@ -464,7 +464,7 @@
 
 
 def last_kernel(
-    step, levels, sizes, code, inverse, where, found, winds, adj, edge, from_west, from_east, east_wind, out
+    step, levels, sizes, code, inverse, where, found, winds, adj, edge, from_east, from_west, east_wind, out
 ):
     north, _, turn_north, south, _, turn_south = neighbours(sizes, code, inverse, where)
     upper = oriented(edge[north, 3:5], turn_north)
@@ -598,7 +598,7 @@
         sds((2 * levels * row_count, width), F32),
         [SM] * 4 + [VM] * 6,
         VM,
-    )(code, inverse, where, found, winds, adj, edge, from_west, from_east, east_wind)
+    )(code, inverse, where, found, winds, adj, edge, from_east, from_west, east_wind)
     return out.reshape(adjoint_end.shape)
 
 

time: 161 us -> 155 us (0.963)
  the two profiles are of different devices: /device:TPU:24 before, /device:TPU:9 now
where the time goes in v8:
time: 155 us; the launch traced here: 154 us
  starting transfers between devices  76.8 us (50%)
  waiting for transfers between devices  24.5 us (16%)
  blocking collectives  23 us (15%)
  Pallas kernels  22 us (14%)
  local copies, waits for them, and re-layouts  6.08 us (4%)
  between operations  1.56 us (1%)
    ppermute x6, starting transfers between devices, to_sides(): return (lax.ppermute(sides, tile, ahead), lax.ppermute(sides, tile, back))  28.5 us
    all_to_all x1, starting transfers between devices, shards(): winds = lax.all_to_all(payload, tile, 0, 0, tiled=True)  19.8 us
    ppermute x6, waiting for transfers between devices, to_sides(): return (lax.ppermute(sides, tile, ahead), lax.ppermute(sides, tile, back))  14.4 us
    ppermute x4, starting transfers between devices, shards(): moved.append(lax.ppermute(part, ('y', 'c'), route))  12.7 us
    all_gather x2, blocking collectives, exchange(): gathered = lax.all_gather(item, group, axis=0, tiled=False)  12.6 us
    all_to_all x2, starting transfers between devices, exchange(): return lax.all_to_all(chosen, 'y', 0, 0, tiled=True)  10.9 us
    all_gather x1, blocking collectives, shards(): edge = lax.all_gather(jnp.stack(moved), 'c', axis=0, tiled=True)  7.31 us
    all_to_all x2, waiting for transfers between devices, exchange(): return lax.all_to_all(chosen, 'y', 0, 0, tiled=True)  7.05 us
  transfers between devices with their start and end apart: 14, of which 7 were waited for; matrix products, arithmetic and copies ran while one was open for 2% of the time, Pallas kernels for 9%

profile of v8, /device:TPU:9, one launch (start us, length us, event | category | flops | bytes accessed | tf_op | source)
XLA Modules:
  0.0 154.1 jit_solution(9957390391918997218)
XLA Ops:
  2.7 4.9 %collective-permute-start = (bf16[4,40,128]{2,1,0:T(8,128)(2,1)S(1)}, bf16[4,40,128]{2,1,0:T(8,128)(2,1)S(1)}, u32[]{:S(2)}, u32[]{:S(2)}) collective-permute-start(bf16[4,40,128]{2,1,0:T(8,128)(2,1)S(1)} %get-tuple-element.27), channel_id=1, source_target_pairs={{0,512},{512,0},{1,513},{513,1},{2,514},{514,2},{3,515},{515,3},{4... | collective-permute-start | bytes 122888 | tf_op jit(solution)/shard_map/ppermute | solution.py:540
  7.6 3.1 %copy.11 = bf16[1,96,2,36,128]{4,3,2,1,0:T(8,128)(2,1)} copy(bf16[1,96,2,36,128]{4,2,3,1,0:T(2,128)(2,1)} %param.8) | data formatting | bytes 3538944 | tf_op args[1]
  10.7 6.1 %shard_map.74 = bf16[896,8,128]{2,1,0:T(8,128)(2,1)} custom-call(s32[1,96]{1,0:T(1,128)} %owner.1, s32[1,96]{1,0:T(1,128)} %unit.1, s32[1,96]{1,0:T(1,128)} %valid.1, bf16[96,2,36,128]{3,2,1,0:T(8,128)(2,1)} %bitcast.24), custom_call_target="tpu_custom_call" | custom-call | flops 1048576 | bytes 1048576 | tf_op jit(solution)/shard_map/pallas_call | solution.py:496
  16.8 19.8 %all-to-all-start = ((bf16[896,8,128]{2,1,0:T(8,128)(2,1)}), bf16[896,8,128]{2,1,0:T(8,128)(2,1)S(1)}, u32[]{:S(2)}, u32[]{:S(2)}) async-start(bf16[896,8,128]{2,1,0:T(8,128)(2,1)} %shard_map.74), calls=%async_computation | async-start | bytes 3670016 | tf_op jit(solution)/shard_map/all_to_all | solution.py:542
  36.8 3.1 %all-gather = bf16[4,4,40,128]{3,2,1,0:T(8,128)(2,1)S(1)} all-gather(bf16[2,4,40,128]{3,2,1,0:T(8,128)(2,1)S(1)} %pad_maximum_fusion.1), channel_id=2, replica_groups=mesh['zl'=2,'y'=8,'c'=2,'x'=8,'zh'=4] {'c'}, dimensions={0}, use_global_device_ids=true | all-gather | bytes 245760 | tf_op jit(solution)/shard_map/all_gather | solution.py:544
  40.5 6.6 %collective-permute-start.2 = (bf16[12,40,128]{2,1,0:T(8,128)(2,1)S(1)}, bf16[12,40,128]{2,1,0:T(8,128)(2,1)S(1)}, u32[]{:S(2)}, u32[]{:S(2)}) collective-permute-start(bf16[12,40,128]{2,1,0:T(8,128)(2,1)S(1)} %get-tuple-element.31), channel_id=1, source_target_pairs={{0,128},{32,416},{64,192},{96,480},{128,256},{160,32},{192,320},{2... | collective-permute-start | bytes 368648 | tf_op jit(solution)/shard_map/ppermute | solution.py:556
  47.1 3.3 %collective-permute-start.3 = (bf16[12,40,128]{2,1,0:T(8,128)(2,1)S(1)}, bf16[12,40,128]{2,1,0:T(8,128)(2,1)S(1)}, u32[]{:S(2)}, u32[]{:S(2)}) collective-permute-start(bf16[12,40,128]{2,1,0:T(8,128)(2,1)S(1)} %get-tuple-element.32), channel_id=1, source_target_pairs={{0,192},{32,352},{64,256},{96,416},{128,320},{160,480},{192,384},{... | collective-permute-start | bytes 368648 | tf_op jit(solution)/shard_map/ppermute | solution.py:556
  53.2 4.0 %collective-permute-start.5 = (f32[40,128]{1,0:T(8,128)S(1)}, f32[40,128]{1,0:T(8,128)S(1)}, u32[]{:S(2)}, u32[]{:S(2)}) collective-permute-start(f32[40,128]{1,0:T(8,128)S(1)} %get-tuple-element.38), channel_id=1, source_target_pairs={{0,1},{1,2},{2,3},{3,4},{4,5},{5,6},{6,7},{7,8},{8,9},{9,10},{10,1... | collective-permute-start | bytes 61448 | tf_op jit(solution)/shard_map/ppermute | solution.py:528
  57.2 5.5 %collective-permute-start.6 = (f32[40,128]{1,0:T(8,128)S(1)}, f32[40,128]{1,0:T(8,128)S(1)}, u32[]{:S(2)}, u32[]{:S(2)}) collective-permute-start(f32[40,128]{1,0:T(8,128)S(1)} %get-tuple-element.38), channel_id=1, source_target_pairs={{1,0},{2,1},{3,2},{4,3},{5,4},{6,5},{7,6},{8,7},{9,8},{10,9},{11,1... | collective-permute-start | bytes 61448 | tf_op jit(solution)/shard_map/ppermute | solution.py:528
  62.8 7.3 %all_gather.23.edge = bf16[8,12,40,128]{3,2,1,0:T(8,128)(2,1)S(1)} all-gather(bf16[4,12,40,128]{3,2,1,0:T(8,128)(2,1)S(1)} %pad_maximum_fusion), channel_id=1, replica_groups=mesh['zl'=2,'y'=8,'c'=2,'x'=8,'zh'=4] {'c'}, dimensions={0}, use_global_device_ids=true | all-gather | bytes 1474560 | tf_op jit(solution)/shard_map/all_gather | solution.py:557
  71.5 10.2 %collective-permute-done.5.from_west = f32[40,128]{1,0:T(8,128)S(1)} collective-permute-done((f32[40,128]{1,0:T(8,128)S(1)}, f32[40,128]{1,0:T(8,128)S(1)}, u32[]{:S(2)}, u32[]{:S(2)}) %collective-permute-start.5) | collective-permute-done | bytes 20512 | tf_op jit(solution)/shard_map/ppermute | solution.py:528
  81.7 2.5 %collective-permute-done.6.from_east = f32[40,128]{1,0:T(8,128)S(1)} collective-permute-done((f32[40,128]{1,0:T(8,128)S(1)}, f32[40,128]{1,0:T(8,128)S(1)}, u32[]{:S(2)}, u32[]{:S(2)}) %collective-permute-start.6) | collective-permute-done | bytes 20512 | tf_op jit(solution)/shard_map/ppermute | solution.py:528
  84.1 3.1 %all-to-all-done.winds = bf16[896,8,128]{2,1,0:T(8,128)(2,1)S(1)} async-done(((bf16[896,8,128]{2,1,0:T(8,128)(2,1)}), bf16[896,8,128]{2,1,0:T(8,128)(2,1)S(1)}, u32[]{:S(2)}, u32[]{:S(2)}) %all-to-all-start) | async-done | bytes 1835040 | tf_op jit(solution)/shard_map/all_to_all | solution.py:542
  88.2 6.7 %all-gather.1 = bf16[28,40,128]{2,1,0:T(8,128)(2,1)S(1)} all-gather(bf16[7,40,128]{2,1,0:T(8,128)(2,1)S(1)} %get-tuple-element.43), channel_id=3, replica_groups=mesh['zl'=2,'y'=8,'c'=2,'x'=8,'zh'=4] {'zl','c'}, dimensions={0}, use_global_device_ids=true | all-gather | bytes 358400 | tf_op jit(solution)/shard_map/all_gather | solution.py:531
  96.4 7.4 %all-to-all-start.1 = ((bf16[8,7,40,128]{3,2,1,0:T(8,128)(2,1)}), bf16[8,7,40,128]{3,2,1,0:T(8,128)(2,1)}, u32[]{:S(2)}, u32[]{:S(2)}) async-start(bf16[8,7,40,128]{3,2,1,0:T(8,128)(2,1)} %shard_map.80), calls=%async_computation.1 | async-start | bytes 1146880 | tf_op jit(solution)/shard_map/all_to_all | solution.py:538
  103.8 3.0 %shard_map.79 = (f32[16,2,40,128]{3,2,1,0:T(8,128)S(1)}, f32[40,128]{1,0:T(8,128)S(1)}) custom-call(s32[1,128]{1,0:T(1,128)S(1)} %get-tuple-element.39.found, bf16[896,8,128]{2,1,0:T(8,128)(2,1)S(1)} %all-to-all-done.winds, f32[16,2,40,128]{3,2,1,0:T(8,128)S(1)} %get-tuple-element.37.adj, f32[9,40,128]{2,1,0:T(8,128)S(1)} %get-tuple-element.40.ends.kept, ...), custom_call_target="tpu_custom_call" | custom-call | flops 1048576 | bytes 1048576 | tf_op jit(solution)/shard_map/pallas_call | solution.py:577
  106.8 2.9 %collective-permute-start.7 = (f32[40,128]{1,0:T(8,128)S(1)}, f32[40,128]{1,0:T(8,128)S(1)}, u32[]{:S(2)}, u32[]{:S(2)}) collective-permute-start(f32[40,128]{1,0:T(8,128)S(1)} %get-tuple-element.44), channel_id=1, source_target_pairs={{0,1},{1,2},{2,3},{3,4},{4,5},{5,6},{6,7},{7,8},{8,9},{9,10},{10,1... | collective-permute-start | bytes 61448 | tf_op jit(solution)/shard_map/ppermute | solution.py:528
  109.7 6.6 %collective-permute-start.8 = (f32[40,128]{1,0:T(8,128)S(1)}, f32[40,128]{1,0:T(8,128)S(1)}, u32[]{:S(2)}, u32[]{:S(2)}) collective-permute-start(f32[40,128]{1,0:T(8,128)S(1)} %get-tuple-element.44), channel_id=1, source_target_pairs={{1,0},{2,1},{3,2},{4,3},{5,4},{6,5},{7,6},{8,7},{9,8},{10,9},{11,1... | collective-permute-start | bytes 61448 | tf_op jit(solution)/shard_map/ppermute | solution.py:528
  117.2 5.8 %all-to-all-done.1.edge = bf16[8,7,40,128]{3,2,1,0:T(8,128)(2,1)} async-done(((bf16[8,7,40,128]{3,2,1,0:T(8,128)(2,1)}), bf16[8,7,40,128]{3,2,1,0:T(8,128)(2,1)}, u32[]{:S(2)}, u32[]{:S(2)}) %all-to-all-start.1) | async-done | bytes 573472 | tf_op jit(solution)/shard_map/all_to_all | solution.py:538
  124.5 5.9 %all-gather.2 = bf16[20,40,128]{2,1,0:T(8,128)(2,1)S(1)} all-gather(bf16[5,40,128]{2,1,0:T(8,128)(2,1)S(1)} %get-tuple-element.47), channel_id=4, replica_groups=mesh['zl'=2,'y'=8,'c'=2,'x'=8,'zh'=4] {'zl','c'}, dimensions={0}, use_global_device_ids=true | all-gather | bytes 256000 | tf_op jit(solution)/shard_map/all_gather | solution.py:531
  131.9 3.5 %all-to-all-start.2 = ((bf16[8,5,40,128]{3,2,1,0:T(8,128)(2,1)}), bf16[8,5,40,128]{3,2,1,0:T(8,128)(2,1)S(1)}, u32[]{:S(2)}, u32[]{:S(2)}) async-start(bf16[8,5,40,128]{3,2,1,0:T(8,128)(2,1)} %shard_map.83), calls=%async_computation.2 | async-start | bytes 819200 | tf_op jit(solution)/shard_map/all_to_all | solution.py:538
  135.3 2.9 %shard_map.82 = (f32[16,2,40,128]{3,2,1,0:T(8,128)S(1)}, f32[40,128]{1,0:T(8,128)S(1)}) custom-call(s32[1,128]{1,0:T(1,128)S(1)} %get-tuple-element.39.found, bf16[896,8,128]{2,1,0:T(8,128)(2,1)S(1)} %all-to-all-done.winds, f32[16,2,40,128]{3,2,1,0:T(8,128)S(1)} %get-tuple-element.42.adj, f32[6,40,128]{2,1,0:T(8,128)S(1)} %get-tuple-element.45.ends, ...), custom_call_target="tpu_custom_call" | custom-call | flops 1048576 | bytes 1048576 | tf_op jit(solution)/shard_map/pallas_call | solution.py:577
  139.1 2.9 %collective-permute-start.10 = (f32[40,128]{1,0:T(8,128)S(1)}, f32[40,128]{1,0:T(8,128)S(1)}, u32[]{:S(2)}, u32[]{:S(2)}) collective-permute-start(f32[40,128]{1,0:T(8,128)S(1)} %get-tuple-element.48), channel_id=1, source_target_pairs={{0,1},{1,2},{2,3},{3,4},{4,5},{5,6},{6,7},{7,8},{8,9},{9,10},{10,1... | collective-permute-start | bytes 61448 | tf_op jit(solution)/shard_map/ppermute | solution.py:528
  142.1 6.6 %collective-permute-start.9 = (f32[40,128]{1,0:T(8,128)S(1)}, f32[40,128]{1,0:T(8,128)S(1)}, u32[]{:S(2)}, u32[]{:S(2)}) collective-permute-start(f32[40,128]{1,0:T(8,128)S(1)} %get-tuple-element.48), channel_id=1, source_target_pairs={{1,0},{2,1},{3,2},{4,3},{5,4},{6,5},{7,6},{8,7},{9,8},{10,9},{11,1... | collective-permute-start | bytes 61448 | tf_op jit(solution)/shard_map/ppermute | solution.py:528
  (30 shorter events, 18.9 us)
Async XLA Ops:
  1.3 1.1 copy-start.2
  2.7 14.1 %collective-permute-start = (bf16[4,40,128]{2,1,0:T(8,128)(2,1)S(1)}, bf16[4,40,128]{2,1,0:T(8,128)(2,1)S(1)}, u32[]{:S(2)}, u32[]{:S(2)}) collective-permute-start(bf16[4,40,128]{2,1,0:T(8,128)(2,1)S(1)} %get-tuple-element.27), channel_id=1, source_target_pairs={{0,512},{512,0},{1,513},{513,1},{2,514},{514,2},{3,515},{515,3},{4... | collective-permute-start | bytes 122888 | tf_op jit(solution)/shard_map/ppermute | solution.py:540
  16.8 70.4 %all-to-all-start = ((bf16[896,8,128]{2,1,0:T(8,128)(2,1)}), bf16[896,8,128]{2,1,0:T(8,128)(2,1)S(1)}, u32[]{:S(2)}, u32[]{:S(2)}) async-start(bf16[896,8,128]{2,1,0:T(8,128)(2,1)} %shard_map.74), calls=%async_computation | async-start | bytes 3670016 | tf_op jit(solution)/shard_map/all_to_all | solution.py:542
  40.5 16.7 %collective-permute-start.2 = (bf16[12,40,128]{2,1,0:T(8,128)(2,1)S(1)}, bf16[12,40,128]{2,1,0:T(8,128)(2,1)S(1)}, u32[]{:S(2)}, u32[]{:S(2)}) collective-permute-start(bf16[12,40,128]{2,1,0:T(8,128)(2,1)S(1)} %get-tuple-element.31), channel_id=1, source_target_pairs={{0,128},{32,416},{64,192},{96,480},{128,256},{160,32},{192,320},{2... | collective-permute-start | bytes 368648 | tf_op jit(solution)/shard_map/ppermute | solution.py:556
  47.1 15.7 %collective-permute-start.3 = (bf16[12,40,128]{2,1,0:T(8,128)(2,1)S(1)}, bf16[12,40,128]{2,1,0:T(8,128)(2,1)S(1)}, u32[]{:S(2)}, u32[]{:S(2)}) collective-permute-start(bf16[12,40,128]{2,1,0:T(8,128)(2,1)S(1)} %get-tuple-element.32), channel_id=1, source_target_pairs={{0,192},{32,352},{64,256},{96,416},{128,320},{160,480},{192,384},{... | collective-permute-start | bytes 368648 | tf_op jit(solution)/shard_map/ppermute | solution.py:556
  50.4 12.4 %collective-permute-start.4 = (bf16[12,40,128]{2,1,0:T(8,128)(2,1)S(1)}, bf16[12,40,128]{2,1,0:T(8,128)(2,1)S(1)}, u32[]{:S(2)}, u32[]{:S(2)}) collective-permute-start(bf16[12,40,128]{2,1,0:T(8,128)(2,1)S(1)} %get-tuple-element.33), channel_id=1, source_target_pairs={{0,256},{64,320},{128,384},{192,448},{256,0},{320,64},{384,128},{4... | collective-permute-start | bytes 368648 | tf_op jit(solution)/shard_map/ppermute | solution.py:556
  51.1 11.7 %collective-permute-start.1 = (bf16[12,40,128]{2,1,0:T(8,128)(2,1)S(1)}, bf16[12,40,128]{2,1,0:T(8,128)(2,1)S(1)}, u32[]{:S(2)}, u32[]{:S(2)}) collective-permute-start(bf16[12,40,128]{2,1,0:T(8,128)(2,1)S(1)} %get-tuple-element.30), channel_id=1, source_target_pairs={{0,64},{32,480},{64,128},{96,32},{128,192},{160,96},{192,256},{224... | collective-permute-start | bytes 368648 | tf_op jit(solution)/shard_map/ppermute | solution.py:556
  53.2 28.4 %collective-permute-start.5 = (f32[40,128]{1,0:T(8,128)S(1)}, f32[40,128]{1,0:T(8,128)S(1)}, u32[]{:S(2)}, u32[]{:S(2)}) collective-permute-start(f32[40,128]{1,0:T(8,128)S(1)} %get-tuple-element.38), channel_id=1, source_target_pairs={{0,1},{1,2},{2,3},{3,4},{4,5},{5,6},{6,7},{7,8},{8,9},{9,10},{10,1... | collective-permute-start | bytes 61448 | tf_op jit(solution)/shard_map/ppermute | solution.py:528
  57.2 26.9 %collective-permute-start.6 = (f32[40,128]{1,0:T(8,128)S(1)}, f32[40,128]{1,0:T(8,128)S(1)}, u32[]{:S(2)}, u32[]{:S(2)}) collective-permute-start(f32[40,128]{1,0:T(8,128)S(1)} %get-tuple-element.38), channel_id=1, source_target_pairs={{1,0},{2,1},{3,2},{4,3},{5,4},{6,5},{7,6},{8,7},{9,8},{10,9},{11,1... | collective-permute-start | bytes 61448 | tf_op jit(solution)/shard_map/ppermute | solution.py:528
  96.4 26.6 %all-to-all-start.1 = ((bf16[8,7,40,128]{3,2,1,0:T(8,128)(2,1)}), bf16[8,7,40,128]{3,2,1,0:T(8,128)(2,1)}, u32[]{:S(2)}, u32[]{:S(2)}) async-start(bf16[8,7,40,128]{3,2,1,0:T(8,128)(2,1)} %shard_map.80), calls=%async_computation.1 | async-start | bytes 1146880 | tf_op jit(solution)/shard_map/all_to_all | solution.py:538
  106.8 9.5 %collective-permute-start.7 = (f32[40,128]{1,0:T(8,128)S(1)}, f32[40,128]{1,0:T(8,128)S(1)}, u32[]{:S(2)}, u32[]{:S(2)}) collective-permute-start(f32[40,128]{1,0:T(8,128)S(1)} %get-tuple-element.44), channel_id=1, source_target_pairs={{0,1},{1,2},{2,3},{3,4},{4,5},{5,6},{6,7},{7,8},{8,9},{9,10},{10,1... | collective-permute-start | bytes 61448 | tf_op jit(solution)/shard_map/ppermute | solution.py:528
  109.7 7.5 %collective-permute-start.8 = (f32[40,128]{1,0:T(8,128)S(1)}, f32[40,128]{1,0:T(8,128)S(1)}, u32[]{:S(2)}, u32[]{:S(2)}) collective-permute-start(f32[40,128]{1,0:T(8,128)S(1)} %get-tuple-element.44), channel_id=1, source_target_pairs={{1,0},{2,1},{3,2},{4,3},{5,4},{6,5},{7,6},{8,7},{9,8},{10,9},{11,1... | collective-permute-start | bytes 61448 | tf_op jit(solution)/shard_map/ppermute | solution.py:528
  131.9 18.9 %all-to-all-start.2 = ((bf16[8,5,40,128]{3,2,1,0:T(8,128)(2,1)}), bf16[8,5,40,128]{3,2,1,0:T(8,128)(2,1)S(1)}, u32[]{:S(2)}, u32[]{:S(2)}) async-start(bf16[8,5,40,128]{3,2,1,0:T(8,128)(2,1)} %shard_map.83), calls=%async_computation.2 | async-start | bytes 819200 | tf_op jit(solution)/shard_map/all_to_all | solution.py:538
  138.3 0.9 copy-start
  139.1 9.5 %collective-permute-start.10 = (f32[40,128]{1,0:T(8,128)S(1)}, f32[40,128]{1,0:T(8,128)S(1)}, u32[]{:S(2)}, u32[]{:S(2)}) collective-permute-start(f32[40,128]{1,0:T(8,128)S(1)} %get-tuple-element.48), channel_id=1, source_target_pairs={{0,1},{1,2},{2,3},{3,4},{4,5},{5,6},{6,7},{7,8},{8,9},{9,10},{10,1... | collective-permute-start | bytes 61448 | tf_op jit(solution)/shard_map/ppermute | solution.py:528
  142.1 7.5 %collective-permute-start.9 = (f32[40,128]{1,0:T(8,128)S(1)}, f32[40,128]{1,0:T(8,128)S(1)}, u32[]{:S(2)}, u32[]{:S(2)}) collective-permute-start(f32[40,128]{1,0:T(8,128)S(1)} %get-tuple-element.48), channel_id=1, source_target_pairs={{1,0},{2,1},{3,2},{4,3},{5,4},{6,5},{7,6},{8,7},{9,8},{10,9},{11,1... | collective-permute-start | bytes 61448 | tf_op jit(solution)/shard_map/ppermute | solution.py:528
  150.8 1.1 copy-start.1

commit v9 on v8

--- a/solution.py
+++ b/solution.py
@@ -14,7 +14,7 @@
 COURANT = 0.2
 PAD = 40
 LABEL, LABEL_EAST = 64, 65
-CHUNKS = 4
+CHUNKS = 8
 HALF = 64
 MATCH, TURN = 96, 97
 EDGE_COLUMN = 32
@@ -135,7 +135,7 @@
     chunk = tiles // CHUNKS
     copies = []
     for i in range(CHUNKS):
-        lax.fori_loop(i * chunk, (i + 1) * chunk, fill, 0, unroll=2)
+        lax.fori_loop(i * chunk, (i + 1) * chunk, fill, 0, unroll=4)
         span = pl.ds(i * chunk * block, chunk * block)
         copies.append(pltpu.make_async_copy(out.at[span], sent.at[span], sem_out.at[i]))
         copies[-1].start()

time: 155 us -> 155 us (level)
  no operation moved by 1% of the time
where the time goes in v9:
time: 155 us; the launch traced here: 154 us
  starting transfers between devices  76.7 us (49%)
  waiting for transfers between devices  24.6 us (16%)
  blocking collectives  23 us (15%)
  Pallas kernels  21.4 us (14%)
  local copies, waits for them, and re-layouts  6.08 us (4%)
  between operations  1.56 us (1%)
    ppermute x6, starting transfers between devices, to_sides(): return (lax.ppermute(sides, tile, ahead), lax.ppermute(sides, tile, back))  28.5 us
    all_to_all x1, starting transfers between devices, shards(): winds = lax.all_to_all(payload, tile, 0, 0, tiled=True)  19.8 us
    ppermute x6, waiting for transfers between devices, to_sides(): return (lax.ppermute(sides, tile, ahead), lax.ppermute(sides, tile, back))  14.5 us
    ppermute x4, starting transfers between devices, shards(): moved.append(lax.ppermute(part, ('y', 'c'), route))  12.7 us
    all_gather x2, blocking collectives, exchange(): gathered = lax.all_gather(item, group, axis=0, tiled=False)  12.6 us
    all_to_all x2, starting transfers between devices, exchange(): return lax.all_to_all(chosen, 'y', 0, 0, tiled=True)  10.8 us
    all_gather x1, blocking collectives, shards(): edge = lax.all_gather(jnp.stack(moved), 'c', axis=0, tiled=True)  7.31 us
    all_to_all x2, waiting for transfers between devices, exchange(): return lax.all_to_all(chosen, 'y', 0, 0, tiled=True)  7.05 us
  transfers between devices with their start and end apart: 14, of which 7 were waited for; matrix products, arithmetic and copies ran while one was open for 2% of the time, Pallas kernels for 9%

profile of v9, /device:TPU:9, one launch (start us, length us, event | category | flops | bytes accessed | tf_op | source)
XLA Modules:
  0.0 153.5 jit_solution(3871188077852064733)
XLA Ops:
  2.7 4.9 %collective-permute-start = (bf16[4,40,128]{2,1,0:T(8,128)(2,1)S(1)}, bf16[4,40,128]{2,1,0:T(8,128)(2,1)S(1)}, u32[]{:S(2)}, u32[]{:S(2)}) collective-permute-start(bf16[4,40,128]{2,1,0:T(8,128)(2,1)S(1)} %get-tuple-element.27), channel_id=1, source_target_pairs={{0,512},{512,0},{1,513},{513,1},{2,514},{514,2},{3,515},{515,3},{4... | collective-permute-start | bytes 122888 | tf_op jit(solution)/shard_map/ppermute | solution.py:540
  7.6 3.1 %copy.11 = bf16[1,96,2,36,128]{4,3,2,1,0:T(8,128)(2,1)} copy(bf16[1,96,2,36,128]{4,2,3,1,0:T(2,128)(2,1)} %param.8) | data formatting | bytes 3538944 | tf_op args[1]
  10.7 5.5 %shard_map.74 = bf16[896,8,128]{2,1,0:T(8,128)(2,1)} custom-call(s32[1,96]{1,0:T(1,128)} %owner.1, s32[1,96]{1,0:T(1,128)} %unit.1, s32[1,96]{1,0:T(1,128)} %valid.1, bf16[96,2,36,128]{3,2,1,0:T(8,128)(2,1)} %bitcast.24), custom_call_target="tpu_custom_call" | custom-call | flops 1048576 | bytes 1048576 | tf_op jit(solution)/shard_map/pallas_call | solution.py:496
  16.2 19.8 %all-to-all-start = ((bf16[896,8,128]{2,1,0:T(8,128)(2,1)}), bf16[896,8,128]{2,1,0:T(8,128)(2,1)S(1)}, u32[]{:S(2)}, u32[]{:S(2)}) async-start(bf16[896,8,128]{2,1,0:T(8,128)(2,1)} %shard_map.74), calls=%async_computation | async-start | bytes 3670016 | tf_op jit(solution)/shard_map/all_to_all | solution.py:542
  36.2 3.1 %all-gather = bf16[4,4,40,128]{3,2,1,0:T(8,128)(2,1)S(1)} all-gather(bf16[2,4,40,128]{3,2,1,0:T(8,128)(2,1)S(1)} %pad_maximum_fusion.1), channel_id=2, replica_groups=mesh['zl'=2,'y'=8,'c'=2,'x'=8,'zh'=4] {'c'}, dimensions={0}, use_global_device_ids=true | all-gather | bytes 245760 | tf_op jit(solution)/shard_map/all_gather | solution.py:544
  39.9 6.6 %collective-permute-start.2 = (bf16[12,40,128]{2,1,0:T(8,128)(2,1)S(1)}, bf16[12,40,128]{2,1,0:T(8,128)(2,1)S(1)}, u32[]{:S(2)}, u32[]{:S(2)}) collective-permute-start(bf16[12,40,128]{2,1,0:T(8,128)(2,1)S(1)} %get-tuple-element.31), channel_id=1, source_target_pairs={{0,128},{32,416},{64,192},{96,480},{128,256},{160,32},{192,320},{2... | collective-permute-start | bytes 368648 | tf_op jit(solution)/shard_map/ppermute | solution.py:556
  46.5 3.3 %collective-permute-start.3 = (bf16[12,40,128]{2,1,0:T(8,128)(2,1)S(1)}, bf16[12,40,128]{2,1,0:T(8,128)(2,1)S(1)}, u32[]{:S(2)}, u32[]{:S(2)}) collective-permute-start(bf16[12,40,128]{2,1,0:T(8,128)(2,1)S(1)} %get-tuple-element.32), channel_id=1, source_target_pairs={{0,192},{32,352},{64,256},{96,416},{128,320},{160,480},{192,384},{... | collective-permute-start | bytes 368648 | tf_op jit(solution)/shard_map/ppermute | solution.py:556
  52.6 4.0 %collective-permute-start.5 = (f32[40,128]{1,0:T(8,128)S(1)}, f32[40,128]{1,0:T(8,128)S(1)}, u32[]{:S(2)}, u32[]{:S(2)}) collective-permute-start(f32[40,128]{1,0:T(8,128)S(1)} %get-tuple-element.38), channel_id=1, source_target_pairs={{0,1},{1,2},{2,3},{3,4},{4,5},{5,6},{6,7},{7,8},{8,9},{9,10},{10,1... | collective-permute-start | bytes 61448 | tf_op jit(solution)/shard_map/ppermute | solution.py:528
  56.6 5.5 %collective-permute-start.6 = (f32[40,128]{1,0:T(8,128)S(1)}, f32[40,128]{1,0:T(8,128)S(1)}, u32[]{:S(2)}, u32[]{:S(2)}) collective-permute-start(f32[40,128]{1,0:T(8,128)S(1)} %get-tuple-element.38), channel_id=1, source_target_pairs={{1,0},{2,1},{3,2},{4,3},{5,4},{6,5},{7,6},{8,7},{9,8},{10,9},{11,1... | collective-permute-start | bytes 61448 | tf_op jit(solution)/shard_map/ppermute | solution.py:528
  62.3 7.3 %all_gather.23.edge = bf16[8,12,40,128]{3,2,1,0:T(8,128)(2,1)S(1)} all-gather(bf16[4,12,40,128]{3,2,1,0:T(8,128)(2,1)S(1)} %pad_maximum_fusion), channel_id=1, replica_groups=mesh['zl'=2,'y'=8,'c'=2,'x'=8,'zh'=4] {'c'}, dimensions={0}, use_global_device_ids=true | all-gather | bytes 1474560 | tf_op jit(solution)/shard_map/all_gather | solution.py:557
  70.9 10.3 %collective-permute-done.5.from_west = f32[40,128]{1,0:T(8,128)S(1)} collective-permute-done((f32[40,128]{1,0:T(8,128)S(1)}, f32[40,128]{1,0:T(8,128)S(1)}, u32[]{:S(2)}, u32[]{:S(2)}) %collective-permute-start.5) | collective-permute-done | bytes 20512 | tf_op jit(solution)/shard_map/ppermute | solution.py:528
  81.2 2.4 %collective-permute-done.6.from_east = f32[40,128]{1,0:T(8,128)S(1)} collective-permute-done((f32[40,128]{1,0:T(8,128)S(1)}, f32[40,128]{1,0:T(8,128)S(1)}, u32[]{:S(2)}, u32[]{:S(2)}) %collective-permute-start.6) | collective-permute-done | bytes 20512 | tf_op jit(solution)/shard_map/ppermute | solution.py:528
  83.6 3.1 %all-to-all-done.winds = bf16[896,8,128]{2,1,0:T(8,128)(2,1)S(1)} async-done(((bf16[896,8,128]{2,1,0:T(8,128)(2,1)}), bf16[896,8,128]{2,1,0:T(8,128)(2,1)S(1)}, u32[]{:S(2)}, u32[]{:S(2)}) %all-to-all-start) | async-done | bytes 1835040 | tf_op jit(solution)/shard_map/all_to_all | solution.py:542
  87.7 6.7 %all-gather.1 = bf16[28,40,128]{2,1,0:T(8,128)(2,1)S(1)} all-gather(bf16[7,40,128]{2,1,0:T(8,128)(2,1)S(1)} %get-tuple-element.43), channel_id=3, replica_groups=mesh['zl'=2,'y'=8,'c'=2,'x'=8,'zh'=4] {'zl','c'}, dimensions={0}, use_global_device_ids=true | all-gather | bytes 358400 | tf_op jit(solution)/shard_map/all_gather | solution.py:531
  95.9 7.3 %all-to-all-start.1 = ((bf16[8,7,40,128]{3,2,1,0:T(8,128)(2,1)}), bf16[8,7,40,128]{3,2,1,0:T(8,128)(2,1)}, u32[]{:S(2)}, u32[]{:S(2)}) async-start(bf16[8,7,40,128]{3,2,1,0:T(8,128)(2,1)} %shard_map.80), calls=%async_computation.1 | async-start | bytes 1146880 | tf_op jit(solution)/shard_map/all_to_all | solution.py:538
  103.2 3.0 %shard_map.79 = (f32[16,2,40,128]{3,2,1,0:T(8,128)S(1)}, f32[40,128]{1,0:T(8,128)S(1)}) custom-call(s32[1,128]{1,0:T(1,128)S(1)} %get-tuple-element.39.found, bf16[896,8,128]{2,1,0:T(8,128)(2,1)S(1)} %all-to-all-done.winds, f32[16,2,40,128]{3,2,1,0:T(8,128)S(1)} %get-tuple-element.37.adj, f32[9,40,128]{2,1,0:T(8,128)S(1)} %get-tuple-element.40.ends.kept, ...), custom_call_target="tpu_custom_call" | custom-call | flops 1048576 | bytes 1048576 | tf_op jit(solution)/shard_map/pallas_call | solution.py:577
  106.2 3.1 %collective-permute-start.7 = (f32[40,128]{1,0:T(8,128)S(1)}, f32[40,128]{1,0:T(8,128)S(1)}, u32[]{:S(2)}, u32[]{:S(2)}) collective-permute-start(f32[40,128]{1,0:T(8,128)S(1)} %get-tuple-element.44), channel_id=1, source_target_pairs={{0,1},{1,2},{2,3},{3,4},{4,5},{5,6},{6,7},{7,8},{8,9},{9,10},{10,1... | collective-permute-start | bytes 61448 | tf_op jit(solution)/shard_map/ppermute | solution.py:528
  109.3 6.4 %collective-permute-start.8 = (f32[40,128]{1,0:T(8,128)S(1)}, f32[40,128]{1,0:T(8,128)S(1)}, u32[]{:S(2)}, u32[]{:S(2)}) collective-permute-start(f32[40,128]{1,0:T(8,128)S(1)} %get-tuple-element.44), channel_id=1, source_target_pairs={{1,0},{2,1},{3,2},{4,3},{5,4},{6,5},{7,6},{8,7},{9,8},{10,9},{11,1... | collective-permute-start | bytes 61448 | tf_op jit(solution)/shard_map/ppermute | solution.py:528
  116.6 5.8 %all-to-all-done.1.edge = bf16[8,7,40,128]{3,2,1,0:T(8,128)(2,1)} async-done(((bf16[8,7,40,128]{3,2,1,0:T(8,128)(2,1)}), bf16[8,7,40,128]{3,2,1,0:T(8,128)(2,1)}, u32[]{:S(2)}, u32[]{:S(2)}) %all-to-all-start.1) | async-done | bytes 573472 | tf_op jit(solution)/shard_map/all_to_all | solution.py:538
  123.9 5.9 %all-gather.2 = bf16[20,40,128]{2,1,0:T(8,128)(2,1)S(1)} all-gather(bf16[5,40,128]{2,1,0:T(8,128)(2,1)S(1)} %get-tuple-element.47), channel_id=4, replica_groups=mesh['zl'=2,'y'=8,'c'=2,'x'=8,'zh'=4] {'zl','c'}, dimensions={0}, use_global_device_ids=true | all-gather | bytes 256000 | tf_op jit(solution)/shard_map/all_gather | solution.py:531
  131.3 3.5 %all-to-all-start.2 = ((bf16[8,5,40,128]{3,2,1,0:T(8,128)(2,1)}), bf16[8,5,40,128]{3,2,1,0:T(8,128)(2,1)S(1)}, u32[]{:S(2)}, u32[]{:S(2)}) async-start(bf16[8,5,40,128]{3,2,1,0:T(8,128)(2,1)} %shard_map.83), calls=%async_computation.2 | async-start | bytes 819200 | tf_op jit(solution)/shard_map/all_to_all | solution.py:538
  134.7 2.9 %shard_map.82 = (f32[16,2,40,128]{3,2,1,0:T(8,128)S(1)}, f32[40,128]{1,0:T(8,128)S(1)}) custom-call(s32[1,128]{1,0:T(1,128)S(1)} %get-tuple-element.39.found, bf16[896,8,128]{2,1,0:T(8,128)(2,1)S(1)} %all-to-all-done.winds, f32[16,2,40,128]{3,2,1,0:T(8,128)S(1)} %get-tuple-element.42.adj, f32[6,40,128]{2,1,0:T(8,128)S(1)} %get-tuple-element.45.ends, ...), custom_call_target="tpu_custom_call" | custom-call | flops 1048576 | bytes 1048576 | tf_op jit(solution)/shard_map/pallas_call | solution.py:577
  138.5 3.1 %collective-permute-start.10 = (f32[40,128]{1,0:T(8,128)S(1)}, f32[40,128]{1,0:T(8,128)S(1)}, u32[]{:S(2)}, u32[]{:S(2)}) collective-permute-start(f32[40,128]{1,0:T(8,128)S(1)} %get-tuple-element.48), channel_id=1, source_target_pairs={{0,1},{1,2},{2,3},{3,4},{4,5},{5,6},{6,7},{7,8},{8,9},{9,10},{10,1... | collective-permute-start | bytes 61448 | tf_op jit(solution)/shard_map/ppermute | solution.py:528
  141.7 6.4 %collective-permute-start.9 = (f32[40,128]{1,0:T(8,128)S(1)}, f32[40,128]{1,0:T(8,128)S(1)}, u32[]{:S(2)}, u32[]{:S(2)}) collective-permute-start(f32[40,128]{1,0:T(8,128)S(1)} %get-tuple-element.48), channel_id=1, source_target_pairs={{1,0},{2,1},{3,2},{4,3},{5,4},{6,5},{7,6},{8,7},{9,8},{10,9},{11,1... | collective-permute-start | bytes 61448 | tf_op jit(solution)/shard_map/ppermute | solution.py:528
  (30 shorter events, 18.9 us)
Async XLA Ops:
  1.3 1.1 copy-start.2
  2.7 13.5 %collective-permute-start = (bf16[4,40,128]{2,1,0:T(8,128)(2,1)S(1)}, bf16[4,40,128]{2,1,0:T(8,128)(2,1)S(1)}, u32[]{:S(2)}, u32[]{:S(2)}) collective-permute-start(bf16[4,40,128]{2,1,0:T(8,128)(2,1)S(1)} %get-tuple-element.27), channel_id=1, source_target_pairs={{0,512},{512,0},{1,513},{513,1},{2,514},{514,2},{3,515},{515,3},{4... | collective-permute-start | bytes 122888 | tf_op jit(solution)/shard_map/ppermute | solution.py:540
  16.2 70.5 %all-to-all-start = ((bf16[896,8,128]{2,1,0:T(8,128)(2,1)}), bf16[896,8,128]{2,1,0:T(8,128)(2,1)S(1)}, u32[]{:S(2)}, u32[]{:S(2)}) async-start(bf16[896,8,128]{2,1,0:T(8,128)(2,1)} %shard_map.74), calls=%async_computation | async-start | bytes 3670016 | tf_op jit(solution)/shard_map/all_to_all | solution.py:542
  39.9 16.7 %collective-permute-start.2 = (bf16[12,40,128]{2,1,0:T(8,128)(2,1)S(1)}, bf16[12,40,128]{2,1,0:T(8,128)(2,1)S(1)}, u32[]{:S(2)}, u32[]{:S(2)}) collective-permute-start(bf16[12,40,128]{2,1,0:T(8,128)(2,1)S(1)} %get-tuple-element.31), channel_id=1, source_target_pairs={{0,128},{32,416},{64,192},{96,480},{128,256},{160,32},{192,320},{2... | collective-permute-start | bytes 368648 | tf_op jit(solution)/shard_map/ppermute | solution.py:556
  46.5 15.7 %collective-permute-start.3 = (bf16[12,40,128]{2,1,0:T(8,128)(2,1)S(1)}, bf16[12,40,128]{2,1,0:T(8,128)(2,1)S(1)}, u32[]{:S(2)}, u32[]{:S(2)}) collective-permute-start(bf16[12,40,128]{2,1,0:T(8,128)(2,1)S(1)} %get-tuple-element.32), channel_id=1, source_target_pairs={{0,192},{32,352},{64,256},{96,416},{128,320},{160,480},{192,384},{... | collective-permute-start | bytes 368648 | tf_op jit(solution)/shard_map/ppermute | solution.py:556
  49.8 12.4 %collective-permute-start.4 = (bf16[12,40,128]{2,1,0:T(8,128)(2,1)S(1)}, bf16[12,40,128]{2,1,0:T(8,128)(2,1)S(1)}, u32[]{:S(2)}, u32[]{:S(2)}) collective-permute-start(bf16[12,40,128]{2,1,0:T(8,128)(2,1)S(1)} %get-tuple-element.33), channel_id=1, source_target_pairs={{0,256},{64,320},{128,384},{192,448},{256,0},{320,64},{384,128},{4... | collective-permute-start | bytes 368648 | tf_op jit(solution)/shard_map/ppermute | solution.py:556
  50.5 11.7 %collective-permute-start.1 = (bf16[12,40,128]{2,1,0:T(8,128)(2,1)S(1)}, bf16[12,40,128]{2,1,0:T(8,128)(2,1)S(1)}, u32[]{:S(2)}, u32[]{:S(2)}) collective-permute-start(bf16[12,40,128]{2,1,0:T(8,128)(2,1)S(1)} %get-tuple-element.30), channel_id=1, source_target_pairs={{0,64},{32,480},{64,128},{96,32},{128,192},{160,96},{192,256},{224... | collective-permute-start | bytes 368648 | tf_op jit(solution)/shard_map/ppermute | solution.py:556
  52.6 28.5 %collective-permute-start.5 = (f32[40,128]{1,0:T(8,128)S(1)}, f32[40,128]{1,0:T(8,128)S(1)}, u32[]{:S(2)}, u32[]{:S(2)}) collective-permute-start(f32[40,128]{1,0:T(8,128)S(1)} %get-tuple-element.38), channel_id=1, source_target_pairs={{0,1},{1,2},{2,3},{3,4},{4,5},{5,6},{6,7},{7,8},{8,9},{9,10},{10,1... | collective-permute-start | bytes 61448 | tf_op jit(solution)/shard_map/ppermute | solution.py:528
  56.6 27.0 %collective-permute-start.6 = (f32[40,128]{1,0:T(8,128)S(1)}, f32[40,128]{1,0:T(8,128)S(1)}, u32[]{:S(2)}, u32[]{:S(2)}) collective-permute-start(f32[40,128]{1,0:T(8,128)S(1)} %get-tuple-element.38), channel_id=1, source_target_pairs={{1,0},{2,1},{3,2},{4,3},{5,4},{6,5},{7,6},{8,7},{9,8},{10,9},{11,1... | collective-permute-start | bytes 61448 | tf_op jit(solution)/shard_map/ppermute | solution.py:528
  95.9 26.5 %all-to-all-start.1 = ((bf16[8,7,40,128]{3,2,1,0:T(8,128)(2,1)}), bf16[8,7,40,128]{3,2,1,0:T(8,128)(2,1)}, u32[]{:S(2)}, u32[]{:S(2)}) async-start(bf16[8,7,40,128]{3,2,1,0:T(8,128)(2,1)} %shard_map.80), calls=%async_computation.1 | async-start | bytes 1146880 | tf_op jit(solution)/shard_map/all_to_all | solution.py:538
  106.2 9.5 %collective-permute-start.7 = (f32[40,128]{1,0:T(8,128)S(1)}, f32[40,128]{1,0:T(8,128)S(1)}, u32[]{:S(2)}, u32[]{:S(2)}) collective-permute-start(f32[40,128]{1,0:T(8,128)S(1)} %get-tuple-element.44), channel_id=1, source_target_pairs={{0,1},{1,2},{2,3},{3,4},{4,5},{5,6},{6,7},{7,8},{8,9},{9,10},{10,1... | collective-permute-start | bytes 61448 | tf_op jit(solution)/shard_map/ppermute | solution.py:528
  109.3 7.3 %collective-permute-start.8 = (f32[40,128]{1,0:T(8,128)S(1)}, f32[40,128]{1,0:T(8,128)S(1)}, u32[]{:S(2)}, u32[]{:S(2)}) collective-permute-start(f32[40,128]{1,0:T(8,128)S(1)} %get-tuple-element.44), channel_id=1, source_target_pairs={{1,0},{2,1},{3,2},{4,3},{5,4},{6,5},{7,6},{8,7},{9,8},{10,9},{11,1... | collective-permute-start | bytes 61448 | tf_op jit(solution)/shard_map/ppermute | solution.py:528
  131.3 18.9 %all-to-all-start.2 = ((bf16[8,5,40,128]{3,2,1,0:T(8,128)(2,1)}), bf16[8,5,40,128]{3,2,1,0:T(8,128)(2,1)S(1)}, u32[]{:S(2)}, u32[]{:S(2)}) async-start(bf16[8,5,40,128]{3,2,1,0:T(8,128)(2,1)} %shard_map.83), calls=%async_computation.2 | async-start | bytes 819200 | tf_op jit(solution)/shard_map/all_to_all | solution.py:538
  137.7 0.9 copy-start
  138.5 9.5 %collective-permute-start.10 = (f32[40,128]{1,0:T(8,128)S(1)}, f32[40,128]{1,0:T(8,128)S(1)}, u32[]{:S(2)}, u32[]{:S(2)}) collective-permute-start(f32[40,128]{1,0:T(8,128)S(1)} %get-tuple-element.48), channel_id=1, source_target_pairs={{0,1},{1,2},{2,3},{3,4},{4,5},{5,6},{6,7},{7,8},{8,9},{9,10},{10,1... | collective-permute-start | bytes 61448 | tf_op jit(solution)/shard_map/ppermute | solution.py:528
  141.7 7.3 %collective-permute-start.9 = (f32[40,128]{1,0:T(8,128)S(1)}, f32[40,128]{1,0:T(8,128)S(1)}, u32[]{:S(2)}, u32[]{:S(2)}) collective-permute-start(f32[40,128]{1,0:T(8,128)S(1)} %get-tuple-element.48), channel_id=1, source_target_pairs={{1,0},{2,1},{3,2},{4,3},{5,4},{6,5},{7,6},{8,7},{9,8},{10,9},{11,1... | collective-permute-start | bytes 61448 | tf_op jit(solution)/shard_map/ppermute | solution.py:528
  150.2 1.1 copy-start.1
